TPU v7x, 32 devices: a whole 2x2x4 slice. The times are simulated.
32 devices in a mesh: fsdp: 8 (over z, y), ctx: 2 (over x), tp: 2 (over core).
Axes of the slice: x: 2, y: 2, z: 4, core: 2. Of those that a mesh axis runs over, the one named last changes fastest.
Arguments:
- tokens_in: bfloat16 [4096, 2048], P(('fsdp', 'ctx')), may hold values from -6 to 6
- doc_positions: int32 [4096], P(('fsdp', 'ctx')), may hold values from 0 to 383, as said below
- attn_gain: bfloat16 [2048], P('fsdp'), may hold values from 0.25 to 1.75
- query_weight: bfloat16 [2048, 2048], P('fsdp', 'tp'), may hold values from -1 to 1
- key_weight: bfloat16 [2048, 256], P('fsdp', 'tp'), may hold values from -1 to 1
- value_weight: bfloat16 [2048, 256], P('fsdp', 'tp'), may hold values from -0.125 to 0.125
- output_weight: bfloat16 [2048, 2048], P('fsdp', 'tp'), may hold values from -2 to 2
- mlp_gain: bfloat16 [2048], P('fsdp'), may hold values from 0.25 to 1.75
- gate_weight: bfloat16 [2048, 5632], P('fsdp', 'tp'), may hold values from -0.125 to 0.125
- up_weight: bfloat16 [2048, 5632], P('fsdp', 'tp'), may hold values from -0.125 to 0.125
- down_weight: bfloat16 [2048, 5632], P('fsdp', 'tp'), may hold values from -0.078125 to 0.078125
- cotangent: bfloat16 [4096, 2048], P(('fsdp', 'ctx')), may hold values from -6 to 6
Outputs:
- block_out: bfloat16 [4096, 2048], P(('fsdp', 'ctx'))
- grad_tokens: float32 [4096, 2048], P(('fsdp', 'ctx'))
- grad_attn_gain: float32 [2048], P('fsdp')
- grad_query: float32 [2048, 2048], P('fsdp', 'tp')
- grad_key: float32 [2048, 256], P('fsdp', 'tp')
- grad_value: float32 [2048, 256], P('fsdp', 'tp')
- grad_output: float32 [2048, 2048], P('fsdp', 'tp')
- grad_mlp_gain: float32 [2048], P('fsdp')
- grad_gate: float32 [2048, 5632], P('fsdp', 'tp')
- grad_up: float32 [2048, 5632], P('fsdp', 'tp')
- grad_down: float32 [2048, 5632], P('fsdp', 'tp')
Inputs may be any that keep to these rules, and one draw needn't show every extreme that they name: `doc_positions`: each sequence of 512 tokens is packed with documents and begins with a new one; a token's value is its offset within its document: 0 at a document's first token, rising by one along it. Documents hold 102 to 384 tokens, except that the last of a sequence may be cut short; some document holds exactly 384.
All inputs are finite; a program needn't handle non-finite values.
Results may differ from a plain program's by a relative error of at most 0.014.
The roundings to bfloat16 on the way count: a program that leaves them out, or rounds other values in their place, can miss the bound.
Values may be sent and summed in bfloat16 or wider, within the bound.
No kernel may reach another device: no remote copies, remote signals or barrier semaphores. Data moves between devices by JAX's collectives and lax.ppermute only.
A program may use at most 256 MiB of HBM per device.

v0:
```python
import functools

import jax
import jax.numpy as jnp
from jax import lax
from jax.experimental import pallas as pl
from jax.experimental.pallas import tpu as pltpu
from jax.sharding import PartitionSpec as P


HEADS = 32
KV_HEADS = 4
HEAD_DIM = 64

EPSILON = 1e-05
NEG_FILL = -1e30


F32 = jnp.float32
BF16 = jnp.bfloat16


def rotary_tables(positions):
    half_dim = HEAD_DIM // 2
    inverse = 1.0 / 10000.0 ** (jnp.arange(half_dim, dtype=F32) * (2.0 / HEAD_DIM))
    angles = positions.astype(F32)[:, None] * inverse[None, :]
    cosine_table = jnp.concatenate([jnp.cos(angles), jnp.cos(angles)], axis=-1)[:, None, :]
    sine_table = jnp.concatenate([jnp.sin(angles), jnp.sin(angles)], axis=-1)[:, None, :]
    return (cosine_table, sine_table)


def apply_rotary(values, cosine_table, sine_table):
    half_dim = values.shape[-1] // 2
    turned = jnp.concatenate([-values[..., half_dim:], values[..., :half_dim]], axis=-1)
    return values * cosine_table + turned * sine_table


def undo_rotary(gradient, cosine_table, sine_table):
    half_dim = gradient.shape[-1] // 2
    sined = gradient * sine_table
    return gradient * cosine_table + jnp.concatenate(
        [sined[..., half_dim:], -sined[..., :half_dim]], axis=-1
    )


def dot_nt(left, right):
    return lax.dot_general(left, right, (((1,), (1,)), ((), ())), preferred_element_type=F32)


def dot_tn(left, right):
    return lax.dot_general(left, right, (((0,), (0,)), ((), ())), preferred_element_type=F32)


def dot_nn(left, right):
    return jnp.dot(left, right, preferred_element_type=F32)


class Plane:
    def __init__(self, size):
        self.size = size
        self.far = size // 2

    def send(self, array, axis, pairs):
        return lax.ppermute(array, axis, pairs)

    def swap(self, array, step):
        pairs = [(i, i ^ step) for i in range(self.size)]
        return self.send(array, "fsdp", pairs)

    def swap_ctx(self, array):
        return self.send(array, "ctx", [(0, 1), (1, 0)])

    def swap_tp(self, array):
        return self.send(array, "tp", [(0, 1), (1, 0)])

    def sum_all(self, array):
        array = sum((self.swap(array, 2 * k) for k in range(1, self.far)), array)
        array = array + self.swap(array, 1)
        return array + self.swap_ctx(array)

    def gather_far(self, shard):
        far = [self.swap(shard, 2 * k) for k in range(1, self.far)]
        return [shard] + far

    def gather_near(self, blocks):
        out = []
        for block in blocks:
            out += [block, self.swap(block, 1)]
        return out

    def gather(self, shard):
        return self.gather_near(self.gather_far(shard))

    def exchange_near(self, blocks, low):
        here = low == 0
        kept = jnp.stack([jnp.where(here, a, b) for a, b in zip(blocks[0::2], blocks[1::2])])
        sent = jnp.stack([jnp.where(here, b, a) for a, b in zip(blocks[0::2], blocks[1::2])])
        return kept, self.swap(sent, 1)

    def exchange_far(self, kept, got, high):
        out = []
        for k in range(self.far):
            block = jnp.stack(
                [lax.dynamic_index_in_dim(b, high ^ k, 0, keepdims=False) for b in (kept, got)]
            )
            out.append(self.swap(block, 2 * k) if k else block)
        return out

    def reduce_near(self, chunk, wire=F32):
        chunk = chunk.reshape(self.far, 2, *chunk.shape[1:])
        sent = chunk[:, 1].astype(wire)
        return chunk[:, 0].astype(F32), self.swap(sent, 1)

    def reduce_far(self, sums, wire=F32):
        got = [self.swap(sums[k].astype(wire), 2 * k) for k in range(1, self.far)]
        return sum((g.astype(F32) for g in got), sums[0])


class Fences:
    def __init__(self, seed):
        self.value = seed

    def cut(self, *before):
        value, *before = lax.optimization_barrier((self.value, *before))
        self.value = value + 1
        return before[0] if len(before) == 1 else before

    def after(self, array):
        array, self.value = lax.optimization_barrier((array, self.value))
        return array


def place(blocks, index, size, axis):
    shape = list(blocks[0].shape)
    width = shape[axis]
    shape[axis] = width * size
    out = jnp.zeros(shape, blocks[0].dtype)
    for k, block in enumerate(blocks):
        out = lax.dynamic_update_slice_in_dim(out, block, (index ^ k) * width, axis)
    return out


def owned_kernel(far, count, half_hidden, place_ref, *refs):
    got, other = refs[:far], refs[far : 2 * far]
    outs, rows = refs[2 * far : 2 * far + count], refs[-1]
    high, low, ctx = place_ref[0], place_ref[1], place_ref[2]
    for i in range(count):
        for k in range(far):
            for r in range(2):
                owner = (high ^ k) * 2 + (low ^ r)
                first = pl.multiple_of((owner * 2 + ctx) * half_hidden, 8)
                second = pl.multiple_of((owner * 2 + 1 - ctx) * half_hidden, 8)
                rows[pl.ds(first, half_hidden), :] = got[k][r, i]
                rows[pl.ds(second, half_hidden), :] = other[k][r, i]
        for j in range(rows.shape[0] // 128):
            outs[i][:, j * 128 : (j + 1) * 128] = rows[j * 128 : (j + 1) * 128, :].T


WHOLE = pl.BlockSpec(memory_space=pltpu.VMEM)
SCALARS = pl.BlockSpec(memory_space=pltpu.SMEM)


def local_kernel(kernel, outs, scratch, *arrays):
    moved = sum(x.size * x.dtype.itemsize for x in (*arrays, *outs))
    return pl.pallas_call(
        kernel,
        out_shape=outs,
        in_specs=[SCALARS] + [WHOLE] * (len(arrays) - 1),
        out_specs=[WHOLE] * len(outs),
        scratch_shapes=scratch,
        compiler_params=pltpu.CompilerParams(vmem_limit_bytes=40 * 2**20),
        cost_estimate=pl.CostEstimate(flops=0, bytes_accessed=moved, transcendentals=0),
    )(*arrays)


def slab_of(where_ref, k, slab):
    return pl.ds(pl.multiple_of((where_ref[0] ^ k) * slab, 128), slab)


def project_in_kernel(slab, where_ref, tokens_ref, *refs):
    blocks, (lin_ref, normed_ref, gains_ref) = refs[:-3], refs[-3:]
    for k, block in enumerate(blocks):
        pair = block[slab : slab + 8, :slab].astype(F32)
        gains_ref[:, slab_of(where_ref, k, slab)] = pair
    tokens = tokens_ref[...].astype(F32)
    rms = lax.rsqrt(jnp.mean(tokens * tokens, axis=-1, keepdims=True) + EPSILON)
    normed_ref[...] = (tokens * rms * gains_ref[0:1, :]).astype(BF16)
    total = None
    for k, block in enumerate(blocks):
        part = dot_nn(normed_ref[:, slab_of(where_ref, k, slab)], block[:slab, :])
        total = part if total is None else total + part
    lin_ref[...] = total


def project_out_kernel(slab, where_ref, left_ref, *refs):
    blocks, out_ref = refs[:-1], refs[-1]
    for k, block in enumerate(blocks):
        out_ref[:, slab_of(where_ref, k, slab)] = dot_nt(left_ref[...], block[:slab, :])


def project_back_kernel(slab, where_ref, left_ref, *refs):
    blocks, out_ref = refs[:-1], refs[-1]
    total = None
    for k, block in enumerate(blocks):
        part = dot_nn(left_ref[:, slab_of(where_ref, k, slab)], block[:slab, :])
        total = part if total is None else total + part
    out_ref[...] = total.astype(out_ref.dtype)


def outer_kernel(half, where_ref, mine_ref, other_ref, *refs):
    blocks, out_ref = refs[:-1], refs[-1]
    here = pl.ds(pl.multiple_of(where_ref[1] * half, 16), half)
    there = pl.ds(pl.multiple_of((1 - where_ref[1]) * half, 16), half)
    total = None
    for k, block in enumerate(blocks):
        part = dot_tn(mine_ref[k], block[here, :]) + dot_tn(other_ref[k], block[there, :])
        total = part if total is None else total + part
    out_ref[...] = total


def owned(got, other, where):
    far = len(got)
    _, count, half_hidden, slab = got[0].shape
    total = far * 4 * half_hidden
    return local_kernel(
        functools.partial(owned_kernel, far, count, half_hidden),
        [jax.ShapeDtypeStruct((slab, total), F32)] * count,
        [pltpu.VMEM((total, slab), F32)],
        where,
        *got,
        *other,
    )


def layer(
    plane,
    tokens_in,
    doc_positions,
    attn_gain,
    query_weight,
    key_weight,
    value_weight,
    output_weight,
    mlp_gain,
    gate_weight,
    up_weight,
    down_weight,
    cotangent,
):
    nf = plane.size
    me = lax.axis_index("fsdp")
    high, low = me // 2, me % 2
    ctx = lax.axis_index("ctx")
    core = lax.axis_index("tp")
    rows, width = tokens_in.shape
    half_rows = rows // 2
    slab = query_weight.shape[0]
    query_columns = query_weight.shape[1]
    key_columns = key_weight.shape[1]
    hidden = gate_weight.shape[1] // nf
    half_hidden = hidden // 2
    local_groups = key_columns // HEAD_DIM
    group_size = HEADS // KV_HEADS
    group_width = group_size * HEAD_DIM
    score_scale = HEAD_DIM ** (-0.5)

    def my_half(array):
        return lax.dynamic_slice_in_dim(array, core * half_rows, half_rows, 0)

    def tp_order(mine, other):
        here = core == 0
        return jnp.where(here, mine, other), jnp.where(here, other, mine)

    def tp_sum(partial):
        return partial + plane.swap_tp(partial)

    def plane_rows(array):
        mine = jnp.concatenate(plane.gather(my_half(array)), axis=0)
        return jnp.concatenate([mine, plane.swap_tp(mine)], axis=0)

    def columns_near(array):
        mine = my_half(array)
        blocks = [mine[:, i * slab : (i + 1) * slab] for i in range(nf)]
        return plane.exchange_near(blocks, low)

    fences = Fences(doc_positions[0])

    gain_rows = jnp.zeros((8, query_columns + 2 * key_columns), BF16)
    gain_rows = gain_rows.at[0, :slab].set(attn_gain).at[1, :slab].set(mlp_gain)
    qkv_shard = jnp.concatenate(
        [jnp.concatenate([query_weight, key_weight, value_weight], axis=1), gain_rows], axis=0
    )
    qkv_blocks = plane.gather(qkv_shard)
    output_blocks = plane.gather(output_weight)
    cot_all = plane_rows(cotangent)

    mlp_shard = jnp.stack([gate_weight.T, up_weight.T, down_weight.T])
    mlp_halves = mlp_shard.reshape(3, nf, 2, half_hidden, slab)
    mlp_sent = jnp.where(ctx == 0, mlp_halves[:, :, 0], mlp_halves[:, :, 1])
    mlp_kept, mlp_got = plane.exchange_near([mlp_sent[:, i] for i in range(nf)], low)
    mlp_blocks = plane.exchange_far(mlp_kept, mlp_got, high)

    fences.cut()
    fences.cut()
    fences.cut()
    fences.cut()
    tokens = tokens_in.astype(F32)
    rms_one = lax.rsqrt(jnp.mean(tokens * tokens, axis=-1, keepdims=True) + EPSILON)
    scaled_one = tokens * rms_one
    where = jnp.stack([me, core]).astype(jnp.int32)
    qkv_lin, normed_one, gains = local_kernel(
        functools.partial(project_in_kernel, slab),
        [
            jax.ShapeDtypeStruct((rows, query_columns + 2 * key_columns), F32),
            jax.ShapeDtypeStruct((rows, width), BF16),
            jax.ShapeDtypeStruct((8, width), F32),
        ],
        [],
        where,
        tokens_in,
        *qkv_blocks,
    )
    gain_one, gain_two = gains[0:1], gains[1:2]

    def project_out(left, blocks):
        return local_kernel(
            functools.partial(project_out_kernel, slab),
            [jax.ShapeDtypeStruct((rows, width), F32)],
            [],
            where,
            left,
            *blocks,
        )[0]

    def outer(got, blocks):
        mine = jnp.concatenate(got)
        return local_kernel(
            functools.partial(outer_kernel, half_rows),
            [jax.ShapeDtypeStruct((slab, blocks[0].shape[1]), F32)],
            [],
            where,
            mine,
            plane.swap_tp(mine),
            *blocks,
        )[0]

    query_lin = qkv_lin[:, :query_columns]
    key_lin = qkv_lin[:, query_columns : query_columns + key_columns]
    value_lin = qkv_lin[:, query_columns + key_columns :]
    cosine_table, sine_table = rotary_tables(doc_positions)
    queries = (
        apply_rotary(query_lin.reshape(rows, -1, HEAD_DIM), cosine_table, sine_table)
        .astype(BF16)
        .reshape(rows, query_columns)
    )
    keys_low = (
        apply_rotary(key_lin.reshape(rows, -1, HEAD_DIM), cosine_table, sine_table)
        .astype(BF16)
        .reshape(rows, key_columns)
    )
    values_low = value_lin.astype(BF16)
    kv_mine = jnp.concatenate([keys_low, values_low], axis=1)
    kv_mine, queries = fences.cut(kv_mine, queries)
    kv_all = jnp.concatenate([kv_mine, plane.swap_ctx(kv_mine)], axis=0)
    key_all, value_all = kv_all[:, :key_columns], kv_all[:, key_columns:]
    places = jnp.arange(rows, dtype=jnp.int32)
    query_places = ctx * rows + places
    key_places = jnp.concatenate([ctx * rows + places, (1 - ctx) * rows + places])
    allowed = (key_places[None, :] <= query_places[:, None]) & (
        key_places[None, :] >= (query_places - doc_positions)[:, None]
    )

    def head_scores(query_group, key_head):
        raw_scores = (
            jnp.einsum("ngd,kd->gnk", query_group, key_head, preferred_element_type=F32)
            * score_scale
        )
        return jnp.where(allowed[None], raw_scores, NEG_FILL)

    attended_parts = []
    lse_parts = []
    for group_index in range(local_groups):
        query_group = queries[
            :, group_index * group_width : (group_index + 1) * group_width
        ].reshape(rows, group_size, HEAD_DIM)
        key_head = key_all[:, group_index * HEAD_DIM : (group_index + 1) * HEAD_DIM]
        value_head = value_all[:, group_index * HEAD_DIM : (group_index + 1) * HEAD_DIM]
        scores = head_scores(query_group, key_head)
        largest = jnp.max(scores, axis=-1, keepdims=True)
        exponent = jnp.exp(scores - largest)
        totals = jnp.sum(exponent, axis=-1, keepdims=True)
        probs_low = (exponent / totals).astype(BF16)
        attended_parts.append(
            jnp.einsum("gnk,kd->ngd", probs_low, value_head, preferred_element_type=F32).reshape(
                rows, group_width
            )
        )
        lse_parts.append(largest + jnp.log(totals))
    attended_low = jnp.concatenate(attended_parts, axis=1).astype(BF16)
    attended_low = fences.cut(attended_low)
    residual = tokens + tp_sum(project_out(attended_low, output_blocks))
    rms_two = lax.rsqrt(jnp.mean(residual * residual, axis=-1, keepdims=True) + EPSILON)
    scaled_two = residual * rms_two
    normed_two = (scaled_two * gain_two).astype(BF16)

    normed_all = plane_rows(normed_two)
    fences.cut()
    fences.cut()
    fences.cut()
    fences.cut()
    mlp_mine = place([b[r] for b in mlp_blocks for r in range(2)], me, nf, 2)
    mlp_all = jnp.concatenate([mlp_mine, plane.swap_ctx(mlp_mine)], axis=1)
    gate_t, up_t, down_t = mlp_all[0], mlp_all[1], mlp_all[2]
    attended_far = plane.gather_far(attended_low)
    normed_near = columns_near(normed_one)
    normed_got = plane.exchange_far(*normed_near, high)
    gate_lin = dot_nt(normed_all, gate_t)
    up_lin = dot_nt(normed_all, up_t)
    grad_act = dot_nt(cot_all, down_t)
    sigmoid = 1.0 / (1.0 + jnp.exp(-gate_lin))
    silu_value = gate_lin / (1.0 + jnp.exp(-gate_lin))
    act_low = (silu_value * up_lin).astype(BF16)
    grad_gate_lin = (grad_act * up_lin * sigmoid * (1.0 + gate_lin * (1.0 - sigmoid))).astype(BF16)
    grad_up_lin = (grad_act * silu_value).astype(BF16)

    def ctx_half(left, right):
        whole = dot_tn(left, right)
        return whole[:half_hidden], plane.swap_ctx(whole[half_hidden:])

    def owners_near(halves):
        blocks = [
            jnp.stack([h[:, i * slab : (i + 1) * slab] for h in halves]) for i in range(nf)
        ]
        return plane.exchange_near(blocks, low)

    def from_owners(got):
        other = [plane.swap_ctx(g) for g in got]
        where = jnp.stack([high, low, ctx]).astype(jnp.int32)
        return owned(got, other, where)

    def tp_part(terms, wire, columns):
        half = nf * half_rows
        mine, other = [
            sum(dot_nn(left[h * half : (h + 1) * half], right[:, columns]) for left, right in terms)
            for h in range(2)
        ]
        other = plane.swap_tp(other.astype(wire)).astype(F32)
        return plane.reduce_near((mine + other).reshape(nf, half_rows, -1), wire)

    def whole_rows(mine):
        one, two = tp_order(mine, plane.swap_tp(mine))
        return jnp.concatenate([one, two], axis=0)

    pieces = 4
    step = width // pieces
    near = []
    reduced = []

    def piece(i):
        near.append(
            tp_part(
                ((fences.after(grad_gate_lin), gate_t), (fences.after(grad_up_lin), up_t)),
                F32,
                slice(i * step, (i + 1) * step),
            )
        )

    def piece_far(i):
        reduced.append(plane.reduce_far(near[i][0] + near[i][1]))

    grad_gate_lin, grad_up_lin, act_low = fences.cut(grad_gate_lin, grad_up_lin, act_low)
    piece(0)
    piece(1)
    half_down = sum(ctx_half(fences.after(act_low), cot_all))
    fences.cut()
    piece_far(0)
    piece(2)
    half_gate = sum(ctx_half(fences.after(grad_gate_lin), normed_all))
    fences.cut()
    piece_far(1)
    piece(3)
    half_up = sum(ctx_half(fences.after(grad_up_lin), normed_all))
    fences.cut()
    piece_far(2)
    mlp_kept, mlp_odd = tp_part(((fences.after(act_low), down_t),), BF16, slice(None))
    down_near = owners_near([half_down])
    fences.cut()
    piece_far(3)
    gate_up_near = owners_near([half_gate, half_up])
    fences.cut()
    down_got = plane.exchange_far(*down_near, high)
    fences.cut()
    grad_normed_two = whole_rows(jnp.concatenate(reduced, axis=-1))
    fences.cut()
    grad_out = cotangent.astype(F32)
    scaled_grad_two = grad_normed_two * gain_two
    grad_residual = (
        grad_out
        + rms_two * scaled_grad_two
        - residual
        * (rms_two * rms_two * rms_two)
        * jnp.mean(scaled_grad_two * residual, axis=-1, keepdims=True)
    )
    grad_attn_low = grad_residual.astype(BF16)
    grad_attended = local_kernel(
        functools.partial(project_back_kernel, slab),
        [jax.ShapeDtypeStruct((rows, query_columns), BF16)],
        [],
        where,
        grad_attn_low,
        *output_blocks,
    )[0]
    grad_attn_near = columns_near(grad_attn_low)
    grad_attended = fences.cut(grad_attended)
    query_grads = []
    key_grads = []
    value_grads = []
    for group_index in range(local_groups):
        query_group = queries[
            :, group_index * group_width : (group_index + 1) * group_width
        ].reshape(rows, group_size, HEAD_DIM)
        key_head = key_all[:, group_index * HEAD_DIM : (group_index + 1) * HEAD_DIM]
        value_head = value_all[:, group_index * HEAD_DIM : (group_index + 1) * HEAD_DIM]
        probabilities = jnp.exp(head_scores(query_group, key_head) - lse_parts[group_index])
        probs_low = probabilities.astype(BF16)
        grad_group = grad_attended[
            :, group_index * group_width : (group_index + 1) * group_width
        ].reshape(rows, group_size, HEAD_DIM)
        grad_probs = jnp.einsum("ngd,kd->gnk", grad_group, value_head, preferred_element_type=F32)
        row_dot = jnp.sum(probabilities * grad_probs, axis=-1, keepdims=True)
        grad_scores = (probabilities * (grad_probs - row_dot)).astype(BF16)
        query_grads.append(
            jnp.einsum("gnk,kd->ngd", grad_scores, key_head, preferred_element_type=F32)
            * score_scale
        )
        key_grads.append(
            jnp.einsum("gnk,ngd->kd", grad_scores, query_group, preferred_element_type=F32)
            * score_scale
        )
        value_grads.append(
            jnp.einsum("gnk,ngd->kd", probs_low, grad_group, preferred_element_type=F32)
        )
    kv_grads = jnp.concatenate(key_grads + value_grads, axis=1)
    kv_grads, *query_grads = fences.cut(kv_grads, *query_grads)
    mlp_mine = plane.reduce_far(mlp_kept + mlp_odd.astype(F32), BF16)
    grad_attn_got = plane.exchange_far(*grad_attn_near, high)
    kv_grad_local = kv_grads[:rows] + plane.swap_ctx(kv_grads[rows:])
    key_grad_local, value_grad_local = kv_grad_local[:, :key_columns], kv_grad_local[:, key_columns:]
    grad_q_lin = (
        undo_rotary(jnp.concatenate(query_grads, axis=1), cosine_table, sine_table)
        .astype(BF16)
        .reshape(rows, query_columns)
    )
    grad_k_lin = (
        undo_rotary(key_grad_local.reshape(rows, -1, HEAD_DIM), cosine_table, sine_table)
        .astype(BF16)
        .reshape(rows, key_columns)
    )
    grad_qkv_lin = jnp.concatenate(
        [grad_q_lin, grad_k_lin, value_grad_local.astype(BF16)], axis=1
    )
    grad_qkv_all = plane.gather(grad_qkv_lin)
    fences.cut()
    gate_up_got = plane.exchange_far(*gate_up_near, high)
    attended_all = plane.gather_near(attended_far)
    grad_normed_one = tp_sum(project_out(fences.after(grad_qkv_lin), qkv_blocks))
    fences.cut()
    gain_sums = plane.sum_all(
        jnp.stack(
            [
                jnp.sum(grad_normed_one * scaled_one, axis=0),
                jnp.sum(grad_normed_two * scaled_two, axis=0),
            ]
        ),
    )
    fences.cut()
    grad_wo = outer(grad_attn_got, [fences.after(b) for b in attended_all])
    fences.cut()
    grad_qkv = outer(normed_got, [fences.after(b) for b in grad_qkv_all])
    fences.cut()
    fences.cut()
    fences.cut()
    scaled_grad_one = grad_normed_one * gain_one
    grad_tokens = (
        grad_residual
        + rms_one * scaled_grad_one
        - tokens
        * (rms_one * rms_one * rms_one)
        * jnp.mean(scaled_grad_one * tokens, axis=-1, keepdims=True)
    )

    output_grad = grad_wo + plane.swap_ctx(grad_wo)
    block_out = (fences.after(residual) + whole_rows(mlp_mine)).astype(BF16)
    grad_qkv = grad_qkv + plane.swap_ctx(grad_qkv)
    query_grad = grad_qkv[:, :query_columns]
    key_grad = grad_qkv[:, query_columns : query_columns + key_columns]
    value_grad = grad_qkv[:, query_columns + key_columns :]
    (down_grad,) = from_owners(down_got)
    gate_grad, up_grad = from_owners(gate_up_got)

    gain_sums = lax.dynamic_slice_in_dim(gain_sums, me * slab, slab, 1)
    gain_sums = jnp.where(fences.value > 0, gain_sums, 0.0)
    return (
        block_out,
        grad_tokens,
        gain_sums[0],
        query_grad,
        key_grad,
        value_grad,
        output_grad,
        gain_sums[1],
        gate_grad,
        up_grad,
        down_grad,
    )


def contract_last(left_array, right_array):
    return lax.dot_general(
        left_array, right_array, (((1,), (1,)), ((), ())), preferred_element_type=F32
    )


def contract_first(left_array, right_array):
    return lax.dot_general(
        left_array, right_array, (((0,), (0,)), ((), ())), preferred_element_type=F32
    )


def normed_fold(scaled, pieces):
    gain_float = pieces[0].astype(F32)
    normed = (scaled * gain_float[None, :]).astype(BF16)
    sums = tuple(
        (jnp.dot(normed, matrix, preferred_element_type=F32) for matrix in pieces[1:])
    )
    return sums + (normed, gain_float)


def row_fold(left_array, shard_piece):
    return jnp.dot(left_array, shard_piece, preferred_element_type=F32)


def column_fold(gradients_in, pieces):
    part_sum = contract_last(gradients_in[0], pieces[0])
    for grad_piece, weight_piece in zip(gradients_in[1:], pieces[1:]):
        part_sum = part_sum + contract_last(grad_piece, weight_piece)
    return part_sum


def column_map(left_array, shard_piece):
    return contract_last(left_array, shard_piece)


def tensor_total(partial_sum):
    return lax.psum(partial_sum, "tp")


def rows_body(
    tokens_in,
    doc_positions,
    attn_gain,
    query_weight,
    key_weight,
    value_weight,
    output_weight,
    mlp_gain,
    gate_weight,
    up_weight,
    down_weight,
    cotangent,
):
    local_rows = tokens_in.shape[0]
    query_columns = query_weight.shape[1]
    key_columns = key_weight.shape[1]
    local_groups = key_columns // HEAD_DIM
    group_size = HEADS // KV_HEADS
    group_width = group_size * HEAD_DIM
    score_scale = HEAD_DIM ** (-0.5)
    tokens = tokens_in.astype(F32)
    rms_one = lax.rsqrt(jnp.mean(tokens * tokens, axis=-1, keepdims=True) + EPSILON)
    scaled_one = tokens * rms_one
    query_lin, key_lin, value_lin, normed_one, gain_one = normed_fold(
        scaled_one,
        (
            lax.all_gather(attn_gain, "fsdp", axis=0, tiled=True),
            lax.all_gather(query_weight, "fsdp", axis=0, tiled=True),
            lax.all_gather(key_weight, "fsdp", axis=0, tiled=True),
            lax.all_gather(value_weight, "fsdp", axis=0, tiled=True),
        ),
    )
    cosine_table, sine_table = rotary_tables(doc_positions)
    queries = (
        apply_rotary(query_lin.reshape(local_rows, -1, HEAD_DIM), cosine_table, sine_table)
        .astype(BF16)
        .reshape(local_rows, query_columns)
    )
    keys_low = (
        apply_rotary(key_lin.reshape(local_rows, -1, HEAD_DIM), cosine_table, sine_table)
        .astype(BF16)
        .reshape(local_rows, key_columns)
    )
    values_low = value_lin.astype(BF16)
    key_all, value_all = (
        lax.all_gather(keys_low, "ctx", axis=0, tiled=True),
        lax.all_gather(values_low, "ctx", axis=0, tiled=True),
    )
    key_count = key_all.shape[0]
    query_places = lax.axis_index("ctx") * local_rows + jnp.arange(local_rows, dtype=jnp.int32)
    key_places = jnp.arange(key_count, dtype=jnp.int32)
    allowed = (key_places[None, :] <= query_places[:, None]) & (
        key_places[None, :] >= (query_places - doc_positions)[:, None]
    )

    def head_scores(query_group, key_head):
        raw_scores = (
            jnp.einsum("ngd,kd->gnk", query_group, key_head, preferred_element_type=F32)
            * score_scale
        )
        return jnp.where(allowed[None], raw_scores, NEG_FILL)

    attended_parts = []
    lse_parts = []
    for group_index in range(local_groups):
        query_group = queries[
            :, group_index * group_width : (group_index + 1) * group_width
        ].reshape(local_rows, group_size, HEAD_DIM)
        key_head = key_all[:, group_index * HEAD_DIM : (group_index + 1) * HEAD_DIM]
        value_head = value_all[:, group_index * HEAD_DIM : (group_index + 1) * HEAD_DIM]
        scores = head_scores(query_group, key_head)
        largest = jnp.max(scores, axis=-1, keepdims=True)
        exponent = jnp.exp(scores - largest)
        totals = jnp.sum(exponent, axis=-1, keepdims=True)
        probs_low = (exponent / totals).astype(BF16)
        attended_parts.append(
            jnp.einsum(
                "gnk,kd->ngd", probs_low, value_head, preferred_element_type=F32
            ).reshape(local_rows, group_width)
        )
        lse_parts.append(largest + jnp.log(totals))
    attended_low = jnp.concatenate(attended_parts, axis=1).astype(BF16)
    attn_branch = tensor_total(
        column_map(attended_low, lax.all_gather(output_weight, "fsdp", axis=0, tiled=True))
    )
    residual = tokens + attn_branch
    rms_two = lax.rsqrt(jnp.mean(residual * residual, axis=-1, keepdims=True) + EPSILON)
    scaled_two = residual * rms_two
    gate_lin, up_lin, normed_two, gain_two = normed_fold(
        scaled_two,
        (
            lax.all_gather(mlp_gain, "fsdp", axis=0, tiled=True),
            lax.all_gather(gate_weight, "fsdp", axis=0, tiled=True),
            lax.all_gather(up_weight, "fsdp", axis=0, tiled=True),
        ),
    )
    silu_value = gate_lin / (1.0 + jnp.exp(-gate_lin))
    act_low = (silu_value * up_lin).astype(BF16)
    mlp_branch = tensor_total(
        column_map(act_low, lax.all_gather(down_weight, "fsdp", axis=0, tiled=True))
    )
    block_out = (residual + mlp_branch).astype(BF16)
    grad_out = cotangent.astype(F32)
    grad_act = row_fold(cotangent, lax.all_gather(down_weight, "fsdp", axis=0, tiled=True))
    sigmoid = 1.0 / (1.0 + jnp.exp(-gate_lin))
    grad_gate_lin = (grad_act * up_lin * sigmoid * (1.0 + gate_lin * (1.0 - sigmoid))).astype(
        BF16
    )
    grad_up_lin = (grad_act * silu_value).astype(BF16)
    grad_normed_two = tensor_total(
        column_fold(
            (grad_gate_lin, grad_up_lin),
            (
                lax.all_gather(gate_weight, "fsdp", axis=0, tiled=True),
                lax.all_gather(up_weight, "fsdp", axis=0, tiled=True),
            ),
        )
    )
    scaled_grad_two = grad_normed_two * gain_two[None, :]
    grad_residual = (
        grad_out
        + rms_two * scaled_grad_two
        - residual
        * (rms_two * rms_two * rms_two)
        * jnp.mean(scaled_grad_two * residual, axis=-1, keepdims=True)
    )
    grad_attn_low = grad_residual.astype(BF16)
    grad_attended = row_fold(
        grad_attn_low, lax.all_gather(output_weight, "fsdp", axis=0, tiled=True)
    ).astype(BF16)
    query_grads = []
    key_grads = []
    value_grads = []
    for group_index in range(local_groups):
        query_group = queries[
            :, group_index * group_width : (group_index + 1) * group_width
        ].reshape(local_rows, group_size, HEAD_DIM)
        key_head = key_all[:, group_index * HEAD_DIM : (group_index + 1) * HEAD_DIM]
        value_head = value_all[:, group_index * HEAD_DIM : (group_index + 1) * HEAD_DIM]
        probabilities = jnp.exp(head_scores(query_group, key_head) - lse_parts[group_index])
        probs_low = probabilities.astype(BF16)
        grad_group = grad_attended[
            :, group_index * group_width : (group_index + 1) * group_width
        ].reshape(local_rows, group_size, HEAD_DIM)
        grad_probs = jnp.einsum(
            "ngd,kd->gnk", grad_group, value_head, preferred_element_type=F32
        )
        row_dot = jnp.sum(probabilities * grad_probs, axis=-1, keepdims=True)
        grad_scores = (probabilities * (grad_probs - row_dot)).astype(BF16)
        query_grads.append(
            jnp.einsum("gnk,kd->ngd", grad_scores, key_head, preferred_element_type=F32)
            * score_scale
        )
        key_grads.append(
            jnp.einsum("gnk,ngd->kd", grad_scores, query_group, preferred_element_type=F32)
            * score_scale
        )
        value_grads.append(
            jnp.einsum("gnk,ngd->kd", probs_low, grad_group, preferred_element_type=F32)
        )
    key_grad_local, value_grad_local = (
        lax.psum_scatter(
            jnp.concatenate(key_grads, axis=1), "ctx", scatter_dimension=0, tiled=True
        ),
        lax.psum_scatter(
            jnp.concatenate(value_grads, axis=1), "ctx", scatter_dimension=0, tiled=True
        ),
    )
    grad_q_lin = (
        undo_rotary(jnp.concatenate(query_grads, axis=1), cosine_table, sine_table)
        .astype(BF16)
        .reshape(local_rows, query_columns)
    )
    grad_k_lin = (
        undo_rotary(key_grad_local.reshape(local_rows, -1, HEAD_DIM), cosine_table, sine_table)
        .astype(BF16)
        .reshape(local_rows, key_columns)
    )
    grad_v_lin = value_grad_local.astype(BF16)
    grad_normed_one = tensor_total(
        column_fold(
            (grad_q_lin, grad_k_lin, grad_v_lin),
            (
                lax.all_gather(query_weight, "fsdp", axis=0, tiled=True),
                lax.all_gather(key_weight, "fsdp", axis=0, tiled=True),
                lax.all_gather(value_weight, "fsdp", axis=0, tiled=True),
            ),
        )
    )
    scaled_grad_one = grad_normed_one * gain_one[None, :]
    grad_tokens = (
        grad_residual
        + rms_one * scaled_grad_one
        - tokens
        * (rms_one * rms_one * rms_one)
        * jnp.mean(scaled_grad_one * tokens, axis=-1, keepdims=True)
    )
    owned = lax.psum_scatter(
        (
            jnp.sum(grad_normed_one * scaled_one, axis=0),
            contract_first(normed_one, grad_q_lin),
            contract_first(normed_one, grad_k_lin),
            contract_first(normed_one, grad_v_lin),
            contract_first(grad_attn_low, attended_low),
            jnp.sum(grad_normed_two * scaled_two, axis=0),
            contract_first(normed_two, grad_gate_lin),
            contract_first(normed_two, grad_up_lin),
            contract_first(cotangent, act_low),
        ),
        "fsdp",
        scatter_dimension=0,
        tiled=True,
    )
    (
        gain_one_grad,
        query_grad,
        key_grad,
        value_grad,
        output_grad,
        gain_two_grad,
        gate_grad,
        up_grad,
        down_grad,
    ) = owned
    summed = lax.psum(
        (
            gain_one_grad,
            query_grad,
            key_grad,
            value_grad,
            output_grad,
            gain_two_grad,
            gate_grad,
            up_grad,
            down_grad,
        ),
        "ctx",
    )
    return (
        block_out,
        grad_tokens,
        summed[0],
        summed[1],
        summed[2],
        summed[3],
        summed[4],
        summed[5],
        summed[6],
        summed[7],
        summed[8],
    )


def choose_body(size, *arrays):
    rows, width = arrays[0].shape
    if size * rows <= width:
        return layer(Plane(size), *arrays)
    return rows_body(*arrays)


def solution(mesh):
    rows = P(("fsdp", "ctx"), None)
    weight = P("fsdp", "tp")
    gain = P("fsdp")
    return jax.shard_map(
        functools.partial(choose_body, mesh.shape["fsdp"]),
        mesh=mesh,
        in_specs=(
            rows,
            P(("fsdp", "ctx")),
            gain,
            weight,
            weight,
            weight,
            weight,
            gain,
            weight,
            weight,
            weight,
            rows,
        ),
        out_specs=(rows, rows, gain, weight, weight, weight, weight, gain, weight, weight, weight),
        check_vma=False,
    )
```

profile of v0, /device:TPU:0, one launch (start us, length us, event | category | flops | bytes accessed | tf_op | source)
XLA Modules:
  0.0 1089.0 jit_solution(8931900254750419805)
XLA Ops:
  38.2 16.2 %collective-permute-done.3.refs_4_ = bf16[264,1280]{1,0:T(8,128)(2,1)S(1)} collective-permute-done((bf16[264,1280]{1,0:T(8,128)(2,1)S(1)}, bf16[264,1280]{1,0:T(8,128)(2,1)S(1)}, u32[]{:S(2)}, u32[]{:S(2)}) %collective-permute-start.3) | collective-permute-done | bytes 675872 | tf_op jit(solution)/shard_map/ppermute | solution.py:64
  67.7 12.3 %collective-permute-start.9 = (bf16[256,1024]{1,0:T(8,128)(2,1)}, bf16[256,1024]{1,0:T(8,128)(2,1)}, u32[]{:S(2)}, u32[]{:S(2)}) collective-permute-start(bf16[256,1024]{1,0:T(8,128)(2,1)} %refs_0_.3), channel_id=1, source_target_pairs={{0,8},{4,12},{8,0},{12,4},{16,24},{20,28},{24,16},{28,20},{1,9},{5... | collective-permute-start | bytes 1572872 | tf_op jit(solution)/shard_map/ppermute | solution.py:64
  83.4 11.5 %collective-permute-done.6.refs_7_ = bf16[264,1280]{1,0:T(8,128)(2,1)} collective-permute-done((bf16[264,1280]{1,0:T(8,128)(2,1)}, bf16[264,1280]{1,0:T(8,128)(2,1)}, u32[]{:S(2)}, u32[]{:S(2)}) %collective-permute-start.6) | collective-permute-done | bytes 675872 | tf_op jit(solution)/shard_map/ppermute | solution.py:64
  94.9 4.0 shard_map.203
  117.1 3.5 collective-permute-start.19
  126.2 14.7 %collective-permute-done.11.refs_4_ = bf16[256,1024]{1,0:T(8,128)(2,1)} collective-permute-done((bf16[256,1024]{1,0:T(8,128)(2,1)}, bf16[256,1024]{1,0:T(8,128)(2,1)}, u32[]{:S(2)}, u32[]{:S(2)}) %collective-permute-start.11) | collective-permute-done | bytes 524320 | tf_op jit(solution)/shard_map/ppermute | solution.py:64
  142.9 20.4 %collective-permute-done.19 = bf16[128,2048]{1,0:T(8,128)(2,1)} collective-permute-done((bf16[128,2048]{1,0:T(8,128)(2,1)}, bf16[128,2048]{1,0:T(8,128)(2,1)}, u32[]{:S(2)}, u32[]{:S(2)}) %collective-permute-start.19) | collective-permute-done | bytes 524320 | tf_op jit(solution)/shard_map/ppermute | solution.py:64
  172.0 6.4 collective-permute-done.14.refs_7_
  178.4 3.5 shard_map.204
  191.9 25.3 %collective-permute-done.22 = bf16[128,2048]{1,0:T(8,128)(2,1)S(1)} collective-permute-done((bf16[128,2048]{1,0:T(8,128)(2,1)}, bf16[128,2048]{1,0:T(8,128)(2,1)S(1)}, u32[]{:S(2)}, u32[]{:S(2)}) %collective-permute-start.22) | collective-permute-done | bytes 524320 | tf_op jit(solution)/shard_map/ppermute | solution.py:64
  228.3 15.5 %collective-permute-done.25 = bf16[2,3,176,256]{3,2,1,0:T(8,128)(2,1)S(1)} collective-permute-done((bf16[2,3,176,256]{3,2,1,0:T(8,128)(2,1)S(1)}, bf16[2,3,176,256]{3,2,1,0:T(8,128)(2,1)S(1)}, u32[]{:S(2)}, u32[]{:S(2)}) %collective-permute-start.25) | collective-permute-done | bytes 540704 | tf_op jit(solution)/shard_map/ppermute | solution.py:64
  251.9 8.1 collective-permute-done.30
  263.9 32.3 %collective-permute-done.32 = bf16[128,2048]{1,0:T(8,128)(2,1)S(1)} collective-permute-done((bf16[128,2048]{1,0:T(8,128)(2,1)S(1)}, bf16[128,2048]{1,0:T(8,128)(2,1)S(1)}, u32[]{:S(2)}, u32[]{:S(2)}) %collective-permute-start.32) | collective-permute-done | bytes 524320 | tf_op jit(solution)/shard_map/ppermute | solution.py:64
  301.9 3.5 collective-permute-done.33
  307.2 3.8 collective-permute-done.35
  318.5 5.9 collective-permute-done.85
  327.0 36.9 %collective-permute-done.28 = bf16[3,176,2048]{2,1,0:T(8,128)(2,1)} collective-permute-done((bf16[3,176,2048]{2,1,0:T(8,128)(2,1)}, bf16[3,176,2048]{2,1,0:T(8,128)(2,1)}, u32[]{:S(2)}, u32[]{:S(2)}) %collective-permute-start.28) | collective-permute-done | bytes 2162720 | tf_op jit(solution)/shard_map/ppermute | solution.py:64
  366.0 5.8 constant_dynamic-update-slice_fusion.10
  371.8 6.1 fusion.131
  384.0 6.1 multiply_convert_fusion
  409.5 5.6 fusion.148
  416.8 5.5 fusion.147
  422.3 5.8 fusion.149
  432.4 5.9 convolution_convert_fusion
  438.3 11.5 %collective-permute-done.98 = f32[176,2048]{1,0:T(8,128)S(1)} collective-permute-done((f32[176,2048]{1,0:T(8,128)S(1)}, f32[176,2048]{1,0:T(8,128)S(1)}, u32[]{:S(2)}, u32[]{:S(2)}) %collective-permute-start.98) | collective-permute-done | bytes 1441824 | tf_op jit(solution)/shard_map/ppermute | solution.py:64
  454.0 26.7 %collective-permute-done.107 = f32[176,2048]{1,0:T(8,128)S(1)} collective-permute-done((f32[176,2048]{1,0:T(8,128)}, f32[176,2048]{1,0:T(8,128)S(1)}, u32[]{:S(2)}, u32[]{:S(2)}) %collective-permute-start.107) | collective-permute-done | bytes 1441824 | tf_op jit(solution)/shard_map/ppermute | solution.py:64
  481.1 29.8 %collective-permute-done.97 = f32[176,2048]{1,0:T(8,128)S(1)} collective-permute-done((f32[176,2048]{1,0:T(8,128)S(1)}, f32[176,2048]{1,0:T(8,128)S(1)}, u32[]{:S(2)}, u32[]{:S(2)}) %collective-permute-start.97) | collective-permute-done | bytes 1441824 | tf_op jit(solution)/shard_map/ppermute | solution.py:64
  520.5 41.4 %collective-permute-done.108 = f32[4,1,176,256]{3,2,1,0:T(8,128)S(1)} collective-permute-done((f32[4,1,176,256]{3,2,1,0:T(8,128)S(1)}, f32[4,1,176,256]{3,2,1,0:T(8,128)S(1)}, u32[]{:S(2)}, u32[]{:S(2)}) %collective-permute-start.108) | collective-permute-done | bytes 720928 | tf_op jit(solution)/shard_map/ppermute | solution.py:64
  570.2 14.1 %collective-permute-done.53 = f32[4,128,512]{2,1,0:T(8,128)S(1)} collective-permute-done((f32[4,128,512]{2,1,0:T(8,128)S(1)}, f32[4,128,512]{2,1,0:T(8,128)S(1)}, u32[]{:S(2)}, u32[]{:S(2)}) %collective-permute-start.53) | collective-permute-done | bytes 1048608 | tf_op jit(solution)/shard_map/ppermute | solution.py:64
  587.2 19.7 %collective-permute-done.48 = f32[4,128,512]{2,1,0:T(8,128)S(1)} collective-permute-done((f32[4,128,512]{2,1,0:T(8,128)S(1)}, f32[4,128,512]{2,1,0:T(8,128)S(1)}, u32[]{:S(2)}, u32[]{:S(2)}) %collective-permute-start.48) | collective-permute-done | bytes 1048608 | tf_op jit(solution)/shard_map/ppermute | solution.py:64
  606.8 6.7 collective-permute-start.55
  613.8 15.5 %collective-permute-done.43 = f32[4,128,512]{2,1,0:T(8,128)S(1)} collective-permute-done((f32[4,128,512]{2,1,0:T(8,128)S(1)}, f32[4,128,512]{2,1,0:T(8,128)S(1)}, u32[]{:S(2)}, u32[]{:S(2)}) %collective-permute-start.43) | collective-permute-done | bytes 1048608 | tf_op jit(solution)/shard_map/ppermute | solution.py:64
  629.3 6.2 collective-permute-start.54
  635.7 15.6 %collective-permute-done.38 = f32[4,128,512]{2,1,0:T(8,128)S(1)} collective-permute-done((f32[4,128,512]{2,1,0:T(8,128)S(1)}, f32[4,128,512]{2,1,0:T(8,128)S(1)}, u32[]{:S(2)}, u32[]{:S(2)}) %collective-permute-start.38) | collective-permute-done | bytes 1048608 | tf_op jit(solution)/shard_map/ppermute | solution.py:64
  654.0 5.2 collective-permute-start.50
  661.5 13.5 %collective-permute-start.45 = (f32[128,512]{1,0:T(8,128)S(1)}, f32[128,512]{1,0:T(8,128)S(1)}, u32[]{:S(2)}, u32[]{:S(2)}) collective-permute-start(f32[128,512]{1,0:T(8,128)S(1)} %get-tuple-element.293), channel_id=1, source_target_pairs={{0,16},{4,20},{8,24},{12,28},{16,0},{20,4},{24,8},{28,12},{1,17},{... | collective-permute-start | bytes 786440 | tf_op jit(solution)/shard_map/ppermute | solution.py:64
  675.0 14.1 %collective-permute-done.50 = f32[128,512]{1,0:T(8,128)S(1)} collective-permute-done((f32[128,512]{1,0:T(8,128)S(1)}, f32[128,512]{1,0:T(8,128)S(1)}, u32[]{:S(2)}, u32[]{:S(2)}) %collective-permute-start.50) | collective-permute-done | bytes 262176 | tf_op jit(solution)/shard_map/ppermute | solution.py:64
  691.8 4.6 collective-permute-start.40
  696.3 15.3 %collective-permute-done.45 = f32[128,512]{1,0:T(8,128)S(1)} collective-permute-done((f32[128,512]{1,0:T(8,128)S(1)}, f32[128,512]{1,0:T(8,128)S(1)}, u32[]{:S(2)}, u32[]{:S(2)}) %collective-permute-start.45) | collective-permute-done | bytes 262176 | tf_op jit(solution)/shard_map/ppermute | solution.py:64
  714.4 4.4 collective-permute-start.68
  718.9 26.6 %collective-permute-done.40 = f32[128,512]{1,0:T(8,128)S(1)} collective-permute-done((f32[128,512]{1,0:T(8,128)S(1)}, f32[128,512]{1,0:T(8,128)S(1)}, u32[]{:S(2)}, u32[]{:S(2)}) %collective-permute-start.40) | collective-permute-done | bytes 262176 | tf_op jit(solution)/shard_map/ppermute | solution.py:64
  746.6 7.0 convert_add_fusion
  753.6 3.8 fusion.23
  815.9 4.5 collective-permute-done.109.refs_1_
  822.6 10.3 collective-permute-done.110.refs_2_
  833.0 7.2 collective-permute-start.101
  845.8 8.5 collective-permute-done.114.refs_6_
  858.9 28.3 %collective-permute-done.101.refs_2_ = f32[2,2,176,256]{3,2,1,0:T(8,128)S(1)} collective-permute-done((f32[2,2,176,256]{3,2,1,0:T(8,128)}, f32[2,2,176,256]{3,2,1,0:T(8,128)S(1)}, u32[]{:S(2)}, u32[]{:S(2)}) %collective-permute-start.101) | collective-permute-done | bytes 720928 | tf_op jit(solution)/shard_map/ppermute | solution.py:64
  893.0 5.8 collective-permute-done.91
  902.9 25.0 %collective-permute-start.63 = (bf16[256,1280]{1,0:T(8,128)(2,1)S(1)}, bf16[256,1280]{1,0:T(8,128)(2,1)}, u32[]{:S(2)}, u32[]{:S(2)}) collective-permute-start(bf16[256,1280]{1,0:T(8,128)(2,1)S(1)} %pad_maximum_fusion.16.left_ref.refs_0_), channel_id=1, source_target_pairs={{0,8},{4,12},{8,0},{12,4},{16,24},{20,28},{24,16},{28,20},{1,9},{5... | collective-permute-start | bytes 1966088 | tf_op jit(solution)/shard_map/ppermute | solution.py:64
  933.0 12.0 %collective-permute-done.92 = bf16[2,128,256]{2,1,0:T(8,128)(2,1)S(1)} collective-permute-done((bf16[2,128,256]{2,1,0:T(8,128)(2,1)S(1)}, bf16[2,128,256]{2,1,0:T(8,128)(2,1)S(1)}, u32[]{:S(2)}, u32[]{:S(2)}) %collective-permute-start.92) | collective-permute-done | bytes 131104 | tf_op jit(solution)/shard_map/ppermute | solution.py:64
  948.7 4.6 collective-permute-done.94
  958.9 3.6 shard_map.206
  962.5 15.2 %collective-permute-done.61.refs_4_ = bf16[256,1280]{1,0:T(8,128)(2,1)} collective-permute-done((bf16[256,1280]{1,0:T(8,128)(2,1)S(1)}, bf16[256,1280]{1,0:T(8,128)(2,1)}, u32[]{:S(2)}, u32[]{:S(2)}) %collective-permute-start.61) | collective-permute-done | bytes 655392 | tf_op jit(solution)/shard_map/ppermute | solution.py:64
  984.6 4.1 shard_map.210
  988.7 5.2 shard_map.209
  996.0 5.3 shard_map.208
  1001.3 9.4 collective-permute-done.62.refs_5_
  1011.3 5.5 shard_map.207
  1018.3 3.7 fusion.133
  1023.9 14.8 %collective-permute-start.76 = (bf16[128,2048]{1,0:T(8,128)(2,1)S(1)}, bf16[128,2048]{1,0:T(8,128)(2,1)S(1)}, u32[]{:S(2)}, u32[]{:S(2)}) collective-permute-start(bf16[128,2048]{1,0:T(8,128)(2,1)S(1)} %get-tuple-element.226), channel_id=1, source_target_pairs={{0,16},{4,20},{8,24},{12,28},{16,0},{20,4},{24,8},{28,12},{1,17},{... | collective-permute-start | bytes 1572872 | tf_op jit(solution)/shard_map/ppermute | solution.py:64
  1038.6 13.5 %collective-permute-start.75 = (bf16[128,2048]{1,0:T(8,128)(2,1)S(1)}, bf16[128,2048]{1,0:T(8,128)(2,1)S(1)}, u32[]{:S(2)}, u32[]{:S(2)}) collective-permute-start(bf16[128,2048]{1,0:T(8,128)(2,1)S(1)} %get-tuple-element.224), channel_id=1, source_target_pairs={{0,8},{4,12},{8,0},{12,4},{16,24},{20,28},{24,16},{28,20},{1,9},{5... | collective-permute-start | bytes 1572872 | tf_op jit(solution)/shard_map/ppermute | solution.py:64
  1060.4 11.1 %collective-permute-done.76 = bf16[128,2048]{1,0:T(8,128)(2,1)S(1)} collective-permute-done((bf16[128,2048]{1,0:T(8,128)(2,1)S(1)}, bf16[128,2048]{1,0:T(8,128)(2,1)S(1)}, u32[]{:S(2)}, u32[]{:S(2)}) %collective-permute-start.76) | collective-permute-done | bytes 524320 | tf_op jit(solution)/shard_map/ppermute | solution.py:64
  1079.8 3.6 fusion.19
  (611 shorter events, 338.0 us)
Async XLA Ops:
  6.5 48.0 %collective-permute-start.3 = (bf16[264,1280]{1,0:T(8,128)(2,1)S(1)}, bf16[264,1280]{1,0:T(8,128)(2,1)S(1)}, u32[]{:S(2)}, u32[]{:S(2)}) collective-permute-start(bf16[264,1280]{1,0:T(8,128)(2,1)S(1)} %pad_maximum_fusion.15.refs_0_), channel_id=1, source_target_pairs={{0,16},{4,20},{8,24},{12,28},{16,0},{20,4},{24,8},{28,12},{1,17},{... | collective-permute-start | bytes 2027528 | tf_op jit(solution)/shard_map/ppermute | solution.py:64
  9.1 46.9 %collective-permute-start.5 = (bf16[264,1280]{1,0:T(8,128)(2,1)S(1)}, bf16[264,1280]{1,0:T(8,128)(2,1)}, u32[]{:S(2)}, u32[]{:S(2)}) collective-permute-start(bf16[264,1280]{1,0:T(8,128)(2,1)S(1)} %pad_maximum_fusion.15.refs_0_), channel_id=1, source_target_pairs={{0,24},{4,28},{8,16},{12,20},{16,8},{20,12},{24,0},{28,4},{1,25},{... | collective-permute-start | bytes 2027528 | tf_op jit(solution)/shard_map/ppermute | solution.py:64
  13.0 51.0 %collective-permute-start.17 = (bf16[128,2048]{1,0:T(8,128)(2,1)}, bf16[128,2048]{1,0:T(8,128)(2,1)}, u32[]{:S(2)}, u32[]{:S(2)}) collective-permute-start(bf16[128,2048]{1,0:T(8,128)(2,1)} %get-tuple-element.204), channel_id=1, source_target_pairs={{0,8},{4,12},{8,0},{12,4},{16,24},{20,28},{24,16},{28,20},{1,9},{5... | collective-permute-start | bytes 1572872 | tf_op jit(solution)/shard_map/ppermute | solution.py:64
  33.2 34.5 %collective-permute-start = (bf16[264,1280]{1,0:T(8,128)(2,1)S(1)}, bf16[264,1280]{1,0:T(8,128)(2,1)}, u32[]{:S(2)}, u32[]{:S(2)}) collective-permute-start(bf16[264,1280]{1,0:T(8,128)(2,1)S(1)} %pad_maximum_fusion.15.refs_0_), channel_id=1, source_target_pairs={{0,4},{4,0},{8,12},{12,8},{16,20},{20,16},{24,28},{28,24},{1,5},{5... | collective-permute-start | bytes 2027528 | tf_op jit(solution)/shard_map/ppermute | solution.py:64
  36.3 43.7 %collective-permute-start.2 = (bf16[264,1280]{1,0:T(8,128)(2,1)S(1)}, bf16[264,1280]{1,0:T(8,128)(2,1)}, u32[]{:S(2)}, u32[]{:S(2)}) collective-permute-start(bf16[264,1280]{1,0:T(8,128)(2,1)S(1)} %collective-permute-done.1.refs_2_), channel_id=1, source_target_pairs={{0,4},{4,0},{8,12},{12,8},{16,20},{20,16},{24,28},{28,24},{1,5},{5... | collective-permute-start | bytes 2027528 | tf_op jit(solution)/shard_map/ppermute | solution.py:64
  56.0 38.9 %collective-permute-start.6 = (bf16[264,1280]{1,0:T(8,128)(2,1)}, bf16[264,1280]{1,0:T(8,128)(2,1)}, u32[]{:S(2)}, u32[]{:S(2)}) collective-permute-start(bf16[264,1280]{1,0:T(8,128)(2,1)} %collective-permute-done.5.refs_6_), channel_id=1, source_target_pairs={{0,4},{4,0},{8,12},{12,8},{16,20},{20,16},{24,28},{28,24},{1,5},{5... | collective-permute-start | bytes 2027528 | tf_op jit(solution)/shard_map/ppermute | solution.py:64
  64.0 61.6 %collective-permute-start.8 = (bf16[256,1024]{1,0:T(8,128)(2,1)}, bf16[256,1024]{1,0:T(8,128)(2,1)}, u32[]{:S(2)}, u32[]{:S(2)}) collective-permute-start(bf16[256,1024]{1,0:T(8,128)(2,1)} %refs_0_.3), channel_id=1, source_target_pairs={{0,4},{4,0},{8,12},{12,8},{16,20},{20,16},{24,28},{28,24},{1,5},{5... | collective-permute-start | bytes 1572872 | tf_op jit(solution)/shard_map/ppermute | solution.py:64
  67.7 58.2 %collective-permute-start.9 = (bf16[256,1024]{1,0:T(8,128)(2,1)}, bf16[256,1024]{1,0:T(8,128)(2,1)}, u32[]{:S(2)}, u32[]{:S(2)}) collective-permute-start(bf16[256,1024]{1,0:T(8,128)(2,1)} %refs_0_.3), channel_id=1, source_target_pairs={{0,8},{4,12},{8,0},{12,4},{16,24},{20,28},{24,16},{28,20},{1,9},{5... | collective-permute-start | bytes 1572872 | tf_op jit(solution)/shard_map/ppermute | solution.py:64
  79.9 61.0 %collective-permute-start.11 = (bf16[256,1024]{1,0:T(8,128)(2,1)}, bf16[256,1024]{1,0:T(8,128)(2,1)}, u32[]{:S(2)}, u32[]{:S(2)}) collective-permute-start(bf16[256,1024]{1,0:T(8,128)(2,1)} %refs_0_.3), channel_id=1, source_target_pairs={{0,16},{4,20},{8,24},{12,28},{16,0},{20,4},{24,8},{28,12},{1,17},{... | collective-permute-start | bytes 1572872 | tf_op jit(solution)/shard_map/ppermute | solution.py:64
  81.0 61.4 %collective-permute-start.13 = (bf16[256,1024]{1,0:T(8,128)(2,1)}, bf16[256,1024]{1,0:T(8,128)(2,1)}, u32[]{:S(2)}, u32[]{:S(2)}) collective-permute-start(bf16[256,1024]{1,0:T(8,128)(2,1)} %refs_0_.3), channel_id=1, source_target_pairs={{0,24},{4,28},{8,16},{12,20},{16,8},{20,12},{24,0},{28,4},{1,25},{... | collective-permute-start | bytes 1572872 | tf_op jit(solution)/shard_map/ppermute | solution.py:64
  117.1 46.3 %collective-permute-start.19 = (bf16[128,2048]{1,0:T(8,128)(2,1)}, bf16[128,2048]{1,0:T(8,128)(2,1)}, u32[]{:S(2)}, u32[]{:S(2)}) collective-permute-start(bf16[128,2048]{1,0:T(8,128)(2,1)} %get-tuple-element.204), channel_id=1, source_target_pairs={{0,16},{4,20},{8,24},{12,28},{16,0},{20,4},{24,8},{28,12},{1,17},{... | collective-permute-start | bytes 1572872 | tf_op jit(solution)/shard_map/ppermute | solution.py:64
  125.6 42.0 %collective-permute-start.21 = (bf16[128,2048]{1,0:T(8,128)(2,1)}, bf16[128,2048]{1,0:T(8,128)(2,1)S(1)}, u32[]{:S(2)}, u32[]{:S(2)}) collective-permute-start(bf16[128,2048]{1,0:T(8,128)(2,1)} %get-tuple-element.204), channel_id=1, source_target_pairs={{0,24},{4,28},{8,16},{12,20},{16,8},{20,12},{24,0},{28,4},{1,25},{... | collective-permute-start | bytes 1572872 | tf_op jit(solution)/shard_map/ppermute | solution.py:64
  125.9 56.1 %collective-permute-start.18 = (bf16[128,2048]{1,0:T(8,128)(2,1)}, bf16[128,2048]{1,0:T(8,128)(2,1)}, u32[]{:S(2)}, u32[]{:S(2)}) collective-permute-start(bf16[128,2048]{1,0:T(8,128)(2,1)} %collective-permute-done.17), channel_id=1, source_target_pairs={{0,4},{4,0},{8,12},{12,8},{16,20},{20,16},{24,28},{28,24},{1,5},{5... | collective-permute-start | bytes 1572872 | tf_op jit(solution)/shard_map/ppermute | solution.py:64
  169.9 48.4 %collective-permute-start.24 = (bf16[4,3,176,256]{3,2,1,0:T(8,128)(2,1)}, bf16[4,3,176,256]{3,2,1,0:T(8,128)(2,1)S(1)}, u32[]{:S(2)}, u32[]{:S(2)}) collective-permute-start(bf16[4,3,176,256]{3,2,1,0:T(8,128)(2,1)} %pad_maximum_fusion.6), channel_id=1, source_target_pairs={{0,4},{4,0},{8,12},{12,8},{16,20},{20,16},{24,28},{28,24},{1,5},{5... | collective-permute-start | bytes 3244040 | tf_op jit(solution)/shard_map/ppermute | solution.py:64
  171.5 45.7 %collective-permute-start.22 = (bf16[128,2048]{1,0:T(8,128)(2,1)}, bf16[128,2048]{1,0:T(8,128)(2,1)S(1)}, u32[]{:S(2)}, u32[]{:S(2)}) collective-permute-start(bf16[128,2048]{1,0:T(8,128)(2,1)} %copy-done.81), channel_id=1, source_target_pairs={{0,4},{4,0},{8,12},{12,8},{16,20},{20,16},{24,28},{28,24},{1,5},{5... | collective-permute-start | bytes 1572872 | tf_op jit(solution)/shard_map/ppermute | solution.py:64
  181.9 41.2 %collective-permute-start.15 = (f32[256,2048]{1,0:T(8,128)S(1)}, f32[256,2048]{1,0:T(8,128)S(1)}, u32[]{:S(2)}, u32[]{:S(2)}) collective-permute-start(f32[256,2048]{1,0:T(8,128)S(1)} %shard_map.204), channel_id=1, source_target_pairs={{0,1},{1,0},{2,3},{3,2},{4,5},{5,4},{6,7},{7,6},{8,9},{9,8},{10,11... | collective-permute-start | bytes 6291464 | tf_op jit(solution)/shard_map/ppermute | solution.py:64
  226.4 33.5 %collective-permute-start.30 = (bf16[128,2048]{1,0:T(8,128)(2,1)S(1)}, bf16[128,2048]{1,0:T(8,128)(2,1)S(1)}, u32[]{:S(2)}, u32[]{:S(2)}) collective-permute-start(bf16[128,2048]{1,0:T(8,128)(2,1)S(1)} %get-tuple-element.206), channel_id=1, source_target_pairs={{0,8},{4,12},{8,0},{12,4},{16,24},{20,28},{24,16},{28,20},{1,9},{5... | collective-permute-start | bytes 1572872 | tf_op jit(solution)/shard_map/ppermute | solution.py:64
  246.8 49.4 %collective-permute-start.32 = (bf16[128,2048]{1,0:T(8,128)(2,1)S(1)}, bf16[128,2048]{1,0:T(8,128)(2,1)S(1)}, u32[]{:S(2)}, u32[]{:S(2)}) collective-permute-start(bf16[128,2048]{1,0:T(8,128)(2,1)S(1)} %get-tuple-element.206), channel_id=1, source_target_pairs={{0,16},{4,20},{8,24},{12,28},{16,0},{20,4},{24,8},{28,12},{1,17},{... | collective-permute-start | bytes 1572872 | tf_op jit(solution)/shard_map/ppermute | solution.py:64
  248.0 48.6 %collective-permute-start.34 = (bf16[128,2048]{1,0:T(8,128)(2,1)S(1)}, bf16[128,2048]{1,0:T(8,128)(2,1)S(1)}, u32[]{:S(2)}, u32[]{:S(2)}) collective-permute-start(bf16[128,2048]{1,0:T(8,128)(2,1)S(1)} %get-tuple-element.206), channel_id=1, source_target_pairs={{0,24},{4,28},{8,16},{12,20},{16,8},{20,12},{24,0},{28,4},{1,25},{... | collective-permute-start | bytes 1572872 | tf_op jit(solution)/shard_map/ppermute | solution.py:64
  251.2 114.8 %collective-permute-start.23 = (bf16[1024,2048]{1,0:T(8,128)(2,1)}, bf16[1024,2048]{1,0:T(8,128)(2,1)}, u32[]{:S(2)}, u32[]{:S(2)}) collective-permute-start(bf16[1024,2048]{1,0:T(8,128)(2,1)} %get-tuple-element.320), channel_id=1, source_target_pairs={{0,1},{1,0},{2,3},{3,2},{4,5},{5,4},{6,7},{7,6},{8,9},{9,8},{10,11... | collective-permute-start | bytes 12582920 | tf_op jit(solution)/shard_map/ppermute | solution.py:64
  260.0 40.1 %collective-permute-start.31 = (bf16[128,2048]{1,0:T(8,128)(2,1)S(1)}, bf16[128,2048]{1,0:T(8,128)(2,1)S(1)}, u32[]{:S(2)}, u32[]{:S(2)}) collective-permute-start(bf16[128,2048]{1,0:T(8,128)(2,1)S(1)} %collective-permute-done.30), channel_id=1, source_target_pairs={{0,4},{4,0},{8,12},{12,8},{16,20},{20,16},{24,28},{28,24},{1,5},{5... | collective-permute-start | bytes 1572872 | tf_op jit(solution)/shard_map/ppermute | solution.py:64
  262.1 50.6 %collective-permute-start.27 = (bf16[2,3,176,256]{3,2,1,0:T(8,128)(2,1)S(1)}, bf16[2,3,176,256]{3,2,1,0:T(8,128)(2,1)S(1)}, u32[]{:S(2)}, u32[]{:S(2)}) collective-permute-start(bf16[2,3,176,256]{3,2,1,0:T(8,128)(2,1)S(1)} %pad_maximum_fusion.19), channel_id=1, source_target_pairs={{0,24},{4,28},{8,16},{12,20},{16,8},{20,12},{24,0},{28,4},{1,25},{... | collective-permute-start | bytes 1622024 | tf_op jit(solution)/shard_map/ppermute | solution.py:64
  312.0 66.0 %collective-permute-start.36 = (bf16[1024,2048]{1,0:T(8,128)(2,1)}, bf16[1024,2048]{1,0:T(8,128)(2,1)}, u32[]{:S(2)}, u32[]{:S(2)}) collective-permute-start(bf16[1024,2048]{1,0:T(8,128)(2,1)} %get-tuple-element.334), channel_id=1, source_target_pairs={{0,1},{1,0},{2,3},{3,2},{4,5},{5,4},{6,7},{7,6},{8,9},{9,8},{10,11... | collective-permute-start | bytes 12582920 | tf_op jit(solution)/shard_map/ppermute | solution.py:64
  315.6 48.3 %collective-permute-start.28 = (bf16[3,176,2048]{2,1,0:T(8,128)(2,1)}, bf16[3,176,2048]{2,1,0:T(8,128)(2,1)}, u32[]{:S(2)}, u32[]{:S(2)}) collective-permute-start(bf16[3,176,2048]{2,1,0:T(8,128)(2,1)} %fusion.106), channel_id=1, source_target_pairs={{0,2},{2,0},{1,3},{3,1},{4,6},{6,4},{5,7},{7,5},{8,10},{10,8},{9,1... | collective-permute-start | bytes 6488072 | tf_op jit(solution)/shard_map/ppermute | solution.py:64
  406.7 105.2 %collective-permute-start.52 = (f32[1024,512]{1,0:T(8,128)S(1)}, f32[1024,512]{1,0:T(8,128)S(1)}, u32[]{:S(2)}, u32[]{:S(2)}) collective-permute-start(f32[1024,512]{1,0:T(8,128)S(1)} %convolution_add_fusion), channel_id=1, source_target_pairs={{0,1},{1,0},{2,3},{3,2},{4,5},{5,4},{6,7},{7,6},{8,9},{9,8},{10,11... | collective-permute-start | bytes 6291464 | tf_op jit(solution)/shard_map/ppermute | solution.py:64
  408.1 106.1 %collective-permute-start.47 = (f32[1024,512]{1,0:T(8,128)S(1)}, f32[1024,512]{1,0:T(8,128)S(1)}, u32[]{:S(2)}, u32[]{:S(2)}) collective-permute-start(f32[1024,512]{1,0:T(8,128)S(1)} %convolution_add_fusion.1), channel_id=1, source_target_pairs={{0,1},{1,0},{2,3},{3,2},{4,5},{5,4},{6,7},{7,6},{8,9},{9,8},{10,11... | collective-permute-start | bytes 6291464 | tf_op jit(solution)/shard_map/ppermute | solution.py:64
  409.2 107.4 %collective-permute-start.42 = (f32[1024,512]{1,0:T(8,128)S(1)}, f32[1024,512]{1,0:T(8,128)S(1)}, u32[]{:S(2)}, u32[]{:S(2)}) collective-permute-start(f32[1024,512]{1,0:T(8,128)S(1)} %convolution_add_fusion.2), channel_id=1, source_target_pairs={{0,1},{1,0},{2,3},{3,2},{4,5},{5,4},{6,7},{7,6},{8,9},{9,8},{10,11... | collective-permute-start | bytes 6291464 | tf_op jit(solution)/shard_map/ppermute | solution.py:64
  415.2 34.5 %collective-permute-start.98 = (f32[176,2048]{1,0:T(8,128)S(1)}, f32[176,2048]{1,0:T(8,128)S(1)}, u32[]{:S(2)}, u32[]{:S(2)}) collective-permute-start(f32[176,2048]{1,0:T(8,128)S(1)} %slice.751), channel_id=1, source_target_pairs={{0,2},{2,0},{1,3},{3,1},{4,6},{6,4},{5,7},{7,5},{8,10},{10,8},{9,1... | collective-permute-start | bytes 4325384 | tf_op jit(solution)/shard_map/ppermute | solution.py:64
  429.5 51.1 %collective-permute-start.107 = (f32[176,2048]{1,0:T(8,128)}, f32[176,2048]{1,0:T(8,128)S(1)}, u32[]{:S(2)}, u32[]{:S(2)}) collective-permute-start(f32[176,2048]{1,0:T(8,128)} %slice.768), channel_id=1, source_target_pairs={{0,2},{2,0},{1,3},{3,1},{4,6},{6,4},{5,7},{7,5},{8,10},{10,8},{9,1... | collective-permute-start | bytes 4325384 | tf_op jit(solution)/shard_map/ppermute | solution.py:64
  450.9 60.0 %collective-permute-start.97 = (f32[176,2048]{1,0:T(8,128)S(1)}, f32[176,2048]{1,0:T(8,128)S(1)}, u32[]{:S(2)}, u32[]{:S(2)}) collective-permute-start(f32[176,2048]{1,0:T(8,128)S(1)} %slice.748), channel_id=1, source_target_pairs={{0,2},{2,0},{1,3},{3,1},{4,6},{6,4},{5,7},{7,5},{8,10},{10,8},{9,1... | collective-permute-start | bytes 4325384 | tf_op jit(solution)/shard_map/ppermute | solution.py:64
  480.7 38.3 %collective-permute-start.37 = (f32[1024,512]{1,0:T(8,128)S(1)}, f32[1024,512]{1,0:T(8,128)S(1)}, u32[]{:S(2)}, u32[]{:S(2)}) collective-permute-start(f32[1024,512]{1,0:T(8,128)S(1)} %convolution_add_fusion.3), channel_id=1, source_target_pairs={{0,1},{1,0},{2,3},{3,2},{4,5},{5,4},{6,7},{7,6},{8,9},{9,8},{10,11... | collective-permute-start | bytes 6291464 | tf_op jit(solution)/shard_map/ppermute | solution.py:64
  510.8 235.6 %collective-permute-start.73 = (bf16[1024,2048]{1,0:T(8,128)(2,1)}, bf16[1024,2048]{1,0:T(8,128)(2,1)S(1)}, u32[]{:S(2)}, u32[]{:S(2)}) collective-permute-start(bf16[1024,2048]{1,0:T(8,128)(2,1)} %convolution_convert_fusion), channel_id=1, source_target_pairs={{0,1},{1,0},{2,3},{3,2},{4,5},{5,4},{6,7},{7,6},{8,9},{9,8},{10,11... | collective-permute-start | bytes 12582920 | tf_op jit(solution)/shard_map/ppermute | solution.py:64
  511.9 52.8 %collective-permute-start.99 = (f32[4,2,176,256]{3,2,1,0:T(8,128)S(1)}, f32[4,2,176,256]{3,2,1,0:T(8,128)S(1)}, u32[]{:S(2)}, u32[]{:S(2)}) collective-permute-start(f32[4,2,176,256]{3,2,1,0:T(8,128)S(1)} %pad_maximum_fusion.4), channel_id=1, source_target_pairs={{0,4},{4,0},{8,12},{12,8},{16,20},{20,16},{24,28},{28,24},{1,5},{5... | collective-permute-start | bytes 4325384 | tf_op jit(solution)/shard_map/ppermute | solution.py:64
  514.2 47.7 %collective-permute-start.108 = (f32[4,1,176,256]{3,2,1,0:T(8,128)S(1)}, f32[4,1,176,256]{3,2,1,0:T(8,128)S(1)}, u32[]{:S(2)}, u32[]{:S(2)}) collective-permute-start(f32[4,1,176,256]{3,2,1,0:T(8,128)S(1)} %pad_maximum_fusion.14), channel_id=1, source_target_pairs={{0,4},{4,0},{8,12},{12,8},{16,20},{20,16},{24,28},{28,24},{1,5},{5... | collective-permute-start | bytes 2162696 | tf_op jit(solution)/shard_map/ppermute | solution.py:64
  516.6 67.8 %collective-permute-start.53 = (f32[4,128,512]{2,1,0:T(8,128)S(1)}, f32[4,128,512]{2,1,0:T(8,128)S(1)}, u32[]{:S(2)}, u32[]{:S(2)}) collective-permute-start(f32[4,128,512]{2,1,0:T(8,128)S(1)} %slice_bitcast_fusion.1), channel_id=1, source_target_pairs={{0,4},{4,0},{8,12},{12,8},{16,20},{20,16},{24,28},{28,24},{1,5},{5... | collective-permute-start | bytes 3145736 | tf_op jit(solution)/shard_map/ppermute | solution.py:64
  518.9 87.9 %collective-permute-start.48 = (f32[4,128,512]{2,1,0:T(8,128)S(1)}, f32[4,128,512]{2,1,0:T(8,128)S(1)}, u32[]{:S(2)}, u32[]{:S(2)}) collective-permute-start(f32[4,128,512]{2,1,0:T(8,128)S(1)} %slice_bitcast_fusion.3), channel_id=1, source_target_pairs={{0,4},{4,0},{8,12},{12,8},{16,20},{20,16},{24,28},{28,24},{1,5},{5... | collective-permute-start | bytes 3145736 | tf_op jit(solution)/shard_map/ppermute | solution.py:64
  561.9 67.4 %collective-permute-start.43 = (f32[4,128,512]{2,1,0:T(8,128)S(1)}, f32[4,128,512]{2,1,0:T(8,128)S(1)}, u32[]{:S(2)}, u32[]{:S(2)}) collective-permute-start(f32[4,128,512]{2,1,0:T(8,128)S(1)} %slice_bitcast_fusion.5), channel_id=1, source_target_pairs={{0,4},{4,0},{8,12},{12,8},{16,20},{20,16},{24,28},{28,24},{1,5},{5... | collective-permute-start | bytes 3145736 | tf_op jit(solution)/shard_map/ppermute | solution.py:64
  564.7 86.6 %collective-permute-start.38 = (f32[4,128,512]{2,1,0:T(8,128)S(1)}, f32[4,128,512]{2,1,0:T(8,128)S(1)}, u32[]{:S(2)}, u32[]{:S(2)}) collective-permute-start(f32[4,128,512]{2,1,0:T(8,128)S(1)} %slice_bitcast_fusion.7), channel_id=1, source_target_pairs={{0,4},{4,0},{8,12},{12,8},{16,20},{20,16},{24,28},{28,24},{1,5},{5... | collective-permute-start | bytes 3145736 | tf_op jit(solution)/shard_map/ppermute | solution.py:64
  584.6 69.3 %collective-permute-start.56 = (f32[128,512]{1,0:T(8,128)S(1)}, f32[128,512]{1,0:T(8,128)S(1)}, u32[]{:S(2)}, u32[]{:S(2)}) collective-permute-start(f32[128,512]{1,0:T(8,128)S(1)} %get-tuple-element.298), channel_id=1, source_target_pairs={{0,24},{4,28},{8,16},{12,20},{16,8},{20,12},{24,0},{28,4},{1,25},{... | collective-permute-start | bytes 786440 | tf_op jit(solution)/shard_map/ppermute | solution.py:64
  606.8 52.5 %collective-permute-start.55 = (f32[128,512]{1,0:T(8,128)S(1)}, f32[128,512]{1,0:T(8,128)S(1)}, u32[]{:S(2)}, u32[]{:S(2)}) collective-permute-start(f32[128,512]{1,0:T(8,128)S(1)} %get-tuple-element.299), channel_id=1, source_target_pairs={{0,16},{4,20},{8,24},{12,28},{16,0},{20,4},{24,8},{28,12},{1,17},{... | collective-permute-start | bytes 786440 | tf_op jit(solution)/shard_map/ppermute | solution.py:64
  654.0 35.2 %collective-permute-start.50 = (f32[128,512]{1,0:T(8,128)S(1)}, f32[128,512]{1,0:T(8,128)S(1)}, u32[]{:S(2)}, u32[]{:S(2)}) collective-permute-start(f32[128,512]{1,0:T(8,128)S(1)} %get-tuple-element.296), channel_id=1, source_target_pairs={{0,16},{4,20},{8,24},{12,28},{16,0},{20,4},{24,8},{28,12},{1,17},{... | collective-permute-start | bytes 786440 | tf_op jit(solution)/shard_map/ppermute | solution.py:64
  661.5 50.2 %collective-permute-start.45 = (f32[128,512]{1,0:T(8,128)S(1)}, f32[128,512]{1,0:T(8,128)S(1)}, u32[]{:S(2)}, u32[]{:S(2)}) collective-permute-start(f32[128,512]{1,0:T(8,128)S(1)} %get-tuple-element.293), channel_id=1, source_target_pairs={{0,16},{4,20},{8,24},{12,28},{16,0},{20,4},{24,8},{28,12},{1,17},{... | collective-permute-start | bytes 786440 | tf_op jit(solution)/shard_map/ppermute | solution.py:64
  691.8 53.6 %collective-permute-start.40 = (f32[128,512]{1,0:T(8,128)S(1)}, f32[128,512]{1,0:T(8,128)S(1)}, u32[]{:S(2)}, u32[]{:S(2)}) collective-permute-start(f32[128,512]{1,0:T(8,128)S(1)} %get-tuple-element.290), channel_id=1, source_target_pairs={{0,16},{4,20},{8,24},{12,28},{16,0},{20,4},{24,8},{28,12},{1,17},{... | collective-permute-start | bytes 786440 | tf_op jit(solution)/shard_map/ppermute | solution.py:64
  711.7 33.8 %collective-permute-start.39 = (f32[128,512]{1,0:T(8,128)S(1)}, f32[128,512]{1,0:T(8,128)S(1)}, u32[]{:S(2)}, u32[]{:S(2)}) collective-permute-start(f32[128,512]{1,0:T(8,128)S(1)} %get-tuple-element.288), channel_id=1, source_target_pairs={{0,8},{4,12},{8,0},{12,4},{16,24},{20,28},{24,16},{28,20},{1,9},{5... | collective-permute-start | bytes 786440 | tf_op jit(solution)/shard_map/ppermute | solution.py:64
  711.8 45.6 %collective-permute-start.66 = (bf16[256,1024]{1,0:T(8,128)(2,1)S(1)}, bf16[256,1024]{1,0:T(8,128)(2,1)}, u32[]{:S(2)}, u32[]{:S(2)}) collective-permute-start(bf16[256,1024]{1,0:T(8,128)(2,1)S(1)} %pad_maximum_fusion.20.left_ref.refs_0_), channel_id=1, source_target_pairs={{0,24},{4,28},{8,16},{12,20},{16,8},{20,12},{24,0},{28,4},{1,25},{... | collective-permute-start | bytes 1572872 | tf_op jit(solution)/shard_map/ppermute | solution.py:64
  714.4 74.5 %collective-permute-start.68 = (bf16[256,1024]{1,0:T(8,128)(2,1)S(1)}, bf16[256,1024]{1,0:T(8,128)(2,1)}, u32[]{:S(2)}, u32[]{:S(2)}) collective-permute-start(bf16[256,1024]{1,0:T(8,128)(2,1)S(1)} %pad_maximum_fusion.20.left_ref.refs_0_), channel_id=1, source_target_pairs={{0,16},{4,20},{8,24},{12,28},{16,0},{20,4},{24,8},{28,12},{1,17},{... | collective-permute-start | bytes 1572872 | tf_op jit(solution)/shard_map/ppermute | solution.py:64
  745.4 54.2 %collective-permute-start.70 = (bf16[256,1024]{1,0:T(8,128)(2,1)S(1)}, bf16[256,1024]{1,0:T(8,128)(2,1)}, u32[]{:S(2)}, u32[]{:S(2)}) collective-permute-start(bf16[256,1024]{1,0:T(8,128)(2,1)S(1)} %pad_maximum_fusion.20.left_ref.refs_0_), channel_id=1, source_target_pairs={{0,8},{4,12},{8,0},{12,4},{16,24},{20,28},{24,16},{28,20},{1,9},{5... | collective-permute-start | bytes 1572872 | tf_op jit(solution)/shard_map/ppermute | solution.py:64
  745.4 59.8 %collective-permute-start.72 = (bf16[256,1024]{1,0:T(8,128)(2,1)S(1)}, bf16[256,1024]{1,0:T(8,128)(2,1)}, u32[]{:S(2)}, u32[]{:S(2)}) collective-permute-start(bf16[256,1024]{1,0:T(8,128)(2,1)S(1)} %pad_maximum_fusion.20.left_ref.refs_0_), channel_id=1, source_target_pairs={{0,4},{4,0},{8,12},{12,8},{16,20},{20,16},{24,28},{28,24},{1,5},{5... | collective-permute-start | bytes 1572872 | tf_op jit(solution)/shard_map/ppermute | solution.py:64
  759.3 48.2 %collective-permute-start.67 = (bf16[256,1024]{1,0:T(8,128)(2,1)}, bf16[256,1024]{1,0:T(8,128)(2,1)}, u32[]{:S(2)}, u32[]{:S(2)}) collective-permute-start(bf16[256,1024]{1,0:T(8,128)(2,1)} %collective-permute-done.66.refs_6_), channel_id=1, source_target_pairs={{0,4},{4,0},{8,12},{12,8},{16,20},{20,16},{24,28},{28,24},{1,5},{5... | collective-permute-start | bytes 1572872 | tf_op jit(solution)/shard_map/ppermute | solution.py:64
  833.0 54.3 %collective-permute-start.101 = (f32[2,2,176,256]{3,2,1,0:T(8,128)}, f32[2,2,176,256]{3,2,1,0:T(8,128)S(1)}, u32[]{:S(2)}, u32[]{:S(2)}) collective-permute-start(f32[2,2,176,256]{3,2,1,0:T(8,128)} %pad_maximum_fusion.11), channel_id=1, source_target_pairs={{0,16},{4,20},{8,24},{12,28},{16,0},{20,4},{24,8},{28,12},{1,17},{... | collective-permute-start | bytes 2162696 | tf_op jit(solution)/shard_map/ppermute | solution.py:64
  840.2 48.5 %collective-permute-start.102 = (f32[2,2,176,256]{3,2,1,0:T(8,128)}, f32[2,2,176,256]{3,2,1,0:T(8,128)}, u32[]{:S(2)}, u32[]{:S(2)}) collective-permute-start(f32[2,2,176,256]{3,2,1,0:T(8,128)} %pad_maximum_fusion.12), channel_id=1, source_target_pairs={{0,24},{4,28},{8,16},{12,20},{16,8},{20,12},{24,0},{28,4},{1,25},{... | collective-permute-start | bytes 2162696 | tf_op jit(solution)/shard_map/ppermute | solution.py:64
  844.3 45.0 %collective-permute-start.115 = (f32[2,1,176,256]{3,2,1,0:T(8,128)}, f32[2,1,176,256]{3,2,1,0:T(8,128)S(1)}, u32[]{:S(2)}, u32[]{:S(2)}) collective-permute-start(f32[2,1,176,256]{3,2,1,0:T(8,128)} %collective-permute-done.111.refs_3_), channel_id=1, source_target_pairs={{0,2},{2,0},{1,3},{3,1},{4,6},{6,4},{5,7},{7,5},{8,10},{10,8},{9,1... | collective-permute-start | bytes 1081352 | tf_op jit(solution)/shard_map/ppermute | solution.py:64
  855.1 44.4 %collective-permute-start.103 = (f32[2,2,176,256]{3,2,1,0:T(8,128)}, f32[2,2,176,256]{3,2,1,0:T(8,128)}, u32[]{:S(2)}, u32[]{:S(2)}) collective-permute-start(f32[2,2,176,256]{3,2,1,0:T(8,128)} %pad_maximum_fusion.9.refs_0_), channel_id=1, source_target_pairs={{0,2},{2,0},{1,3},{3,1},{4,6},{6,4},{5,7},{7,5},{8,10},{10,8},{9,1... | collective-permute-start | bytes 2162696 | tf_op jit(solution)/shard_map/ppermute | solution.py:64
  858.3 44.5 %collective-permute-start.104 = (f32[2,2,176,256]{3,2,1,0:T(8,128)S(1)}, f32[2,2,176,256]{3,2,1,0:T(8,128)S(1)}, u32[]{:S(2)}, u32[]{:S(2)}) collective-permute-start(f32[2,2,176,256]{3,2,1,0:T(8,128)S(1)} %collective-permute-done.100.refs_1_), channel_id=1, source_target_pairs={{0,2},{2,0},{1,3},{3,1},{4,6},{6,4},{5,7},{7,5},{8,10},{10,8},{9,1... | collective-permute-start | bytes 2162696 | tf_op jit(solution)/shard_map/ppermute | solution.py:64
  887.3 40.6 %collective-permute-start.105 = (f32[2,2,176,256]{3,2,1,0:T(8,128)S(1)}, f32[2,2,176,256]{3,2,1,0:T(8,128)S(1)}, u32[]{:S(2)}, u32[]{:S(2)}) collective-permute-start(f32[2,2,176,256]{3,2,1,0:T(8,128)S(1)} %collective-permute-done.101.refs_2_), channel_id=1, source_target_pairs={{0,2},{2,0},{1,3},{3,1},{4,6},{6,4},{5,7},{7,5},{8,10},{10,8},{9,1... | collective-permute-start | bytes 2162696 | tf_op jit(solution)/shard_map/ppermute | solution.py:64
  888.7 41.0 %collective-permute-start.106 = (f32[2,2,176,256]{3,2,1,0:T(8,128)}, f32[2,2,176,256]{3,2,1,0:T(8,128)S(1)}, u32[]{:S(2)}, u32[]{:S(2)}) collective-permute-start(f32[2,2,176,256]{3,2,1,0:T(8,128)} %collective-permute-done.102.refs_3_), channel_id=1, source_target_pairs={{0,2},{2,0},{1,3},{3,1},{4,6},{6,4},{5,7},{7,5},{8,10},{10,8},{9,1... | collective-permute-start | bytes 2162696 | tf_op jit(solution)/shard_map/ppermute | solution.py:64
  898.9 119.5 %collective-permute-start.74 = (bf16[4,128,2048]{2,1,0:T(8,128)(2,1)}, bf16[4,128,2048]{2,1,0:T(8,128)(2,1)}, u32[]{:S(2)}, u32[]{:S(2)}) collective-permute-start(bf16[4,128,2048]{2,1,0:T(8,128)(2,1)} %fusion.23), channel_id=1, source_target_pairs={{0,4},{4,0},{8,12},{12,8},{16,20},{20,16},{24,28},{28,24},{1,5},{5... | collective-permute-start | bytes 6291464 | tf_op jit(solution)/shard_map/ppermute | solution.py:64
  899.5 56.4 %collective-permute-start.59 = (bf16[256,1280]{1,0:T(8,128)(2,1)S(1)}, bf16[256,1280]{1,0:T(8,128)(2,1)}, u32[]{:S(2)}, u32[]{:S(2)}) collective-permute-start(bf16[256,1280]{1,0:T(8,128)(2,1)S(1)} %pad_maximum_fusion.16.left_ref.refs_0_), channel_id=1, source_target_pairs={{0,24},{4,28},{8,16},{12,20},{16,8},{20,12},{24,0},{28,4},{1,25},{... | collective-permute-start | bytes 1966088 | tf_op jit(solution)/shard_map/ppermute | solution.py:64
  902.9 53.0 %collective-permute-start.63 = (bf16[256,1280]{1,0:T(8,128)(2,1)S(1)}, bf16[256,1280]{1,0:T(8,128)(2,1)}, u32[]{:S(2)}, u32[]{:S(2)}) collective-permute-start(bf16[256,1280]{1,0:T(8,128)(2,1)S(1)} %pad_maximum_fusion.16.left_ref.refs_0_), channel_id=1, source_target_pairs={{0,8},{4,12},{8,0},{12,4},{16,24},{20,28},{24,16},{28,20},{1,9},{5... | collective-permute-start | bytes 1966088 | tf_op jit(solution)/shard_map/ppermute | solution.py:64
  977.7 77.2 %collective-permute-start.79 = (f32[256,2048]{1,0:T(8,128)S(1)}, f32[256,2048]{1,0:T(8,128)}, u32[]{:S(2)}, u32[]{:S(2)}) collective-permute-start(f32[256,2048]{1,0:T(8,128)S(1)} %shard_map.206), channel_id=1, source_target_pairs={{0,1},{1,0},{2,3},{3,2},{4,5},{5,4},{6,7},{7,6},{8,9},{9,8},{10,11... | collective-permute-start | bytes 6291464 | tf_op jit(solution)/shard_map/ppermute | solution.py:64
  1016.8 67.2 %collective-permute-start.90 = (f32[256,1280]{1,0:T(8,128)S(1)}, f32[256,1280]{1,0:T(8,128)S(1)}, u32[]{:S(2)}, u32[]{:S(2)}) collective-permute-start(f32[256,1280]{1,0:T(8,128)S(1)} %shard_map.207), channel_id=1, source_target_pairs={{0,2},{2,0},{1,3},{3,1},{4,6},{6,4},{5,7},{7,5},{8,10},{10,8},{9,1... | collective-permute-start | bytes 3932168 | tf_op jit(solution)/shard_map/ppermute | solution.py:64
  1022.3 36.7 %collective-permute-start.77 = (bf16[128,2048]{1,0:T(8,128)(2,1)S(1)}, bf16[128,2048]{1,0:T(8,128)(2,1)S(1)}, u32[]{:S(2)}, u32[]{:S(2)}) collective-permute-start(bf16[128,2048]{1,0:T(8,128)(2,1)S(1)} %get-tuple-element.225), channel_id=1, source_target_pairs={{0,24},{4,28},{8,16},{12,20},{16,8},{20,12},{24,0},{28,4},{1,25},{... | collective-permute-start | bytes 1572872 | tf_op jit(solution)/shard_map/ppermute | solution.py:64
  1023.9 47.7 %collective-permute-start.76 = (bf16[128,2048]{1,0:T(8,128)(2,1)S(1)}, bf16[128,2048]{1,0:T(8,128)(2,1)S(1)}, u32[]{:S(2)}, u32[]{:S(2)}) collective-permute-start(bf16[128,2048]{1,0:T(8,128)(2,1)S(1)} %get-tuple-element.226), channel_id=1, source_target_pairs={{0,16},{4,20},{8,24},{12,28},{16,0},{20,4},{24,8},{28,12},{1,17},{... | collective-permute-start | bytes 1572872 | tf_op jit(solution)/shard_map/ppermute | solution.py:64
  1038.6 32.9 %collective-permute-start.75 = (bf16[128,2048]{1,0:T(8,128)(2,1)S(1)}, bf16[128,2048]{1,0:T(8,128)(2,1)S(1)}, u32[]{:S(2)}, u32[]{:S(2)}) collective-permute-start(bf16[128,2048]{1,0:T(8,128)(2,1)S(1)} %get-tuple-element.224), channel_id=1, source_target_pairs={{0,8},{4,12},{8,0},{12,4},{16,24},{20,28},{24,16},{28,20},{1,9},{5... | collective-permute-start | bytes 1572872 | tf_op jit(solution)/shard_map/ppermute | solution.py:64
  (146 other events, 3420.1 us)
where the time goes:
time: 1100 us; the launch traced here: 1090 us
  waiting for transfers between devices  560 us (51%)
  starting transfers between devices  230 us (21%)
  local copies, waits for them, and re-layouts  111 us (10%)
  matrix products  86.4 us (8%)
  other arithmetic  64.1 us (6%)
  Pallas kernels  34.1 us (3%)
    ppermute x116, waiting for transfers between devices, send(): return lax.ppermute(array, axis, pairs)  560 us
    ppermute x116, starting transfers between devices, send(): return lax.ppermute(array, axis, pairs)  230 us
    unnamed x212, local copies, waits for them, and re-layouts  55.1 us
    dot_general x18, matrix products, dot_nn(): return jnp.dot(left, right, preferred_element_type=F32)  36.3 us
    pallas_call x8, Pallas kernels, local_kernel(): pl.pallas_call(kernel, out_shape=outs, in_specs=[SCALARS] + [WHOLE] * (le...  34.1 us
  transfers between devices with their start and end apart: 116, of which 43 were waited for; matrix products, arithmetic and copies ran while one was open for 19% of the time, Pallas kernels for 3%

commit v1 on v0

--- a/solution.py
+++ b/solution.py
@@ -20,27 +20,28 @@
 BF16 = jnp.bfloat16
 
 
-def rotary_tables(positions):
+def pair_tables(positions):
     half_dim = HEAD_DIM // 2
     inverse = 1.0 / 10000.0 ** (jnp.arange(half_dim, dtype=F32) * (2.0 / HEAD_DIM))
     angles = positions.astype(F32)[:, None] * inverse[None, :]
-    cosine_table = jnp.concatenate([jnp.cos(angles), jnp.cos(angles)], axis=-1)[:, None, :]
-    sine_table = jnp.concatenate([jnp.sin(angles), jnp.sin(angles)], axis=-1)[:, None, :]
-    return (cosine_table, sine_table)
-
-
-def apply_rotary(values, cosine_table, sine_table):
-    half_dim = values.shape[-1] // 2
-    turned = jnp.concatenate([-values[..., half_dim:], values[..., :half_dim]], axis=-1)
-    return values * cosine_table + turned * sine_table
-
-
-def undo_rotary(gradient, cosine_table, sine_table):
-    half_dim = gradient.shape[-1] // 2
-    sined = gradient * sine_table
-    return gradient * cosine_table + jnp.concatenate(
-        [sined[..., half_dim:], -sined[..., :half_dim]], axis=-1
-    )
+    return jnp.tile(jnp.cos(angles), (1, 4)), jnp.tile(jnp.sin(angles), (1, 4))
+
+
+def first_half(shape):
+    return lax.broadcasted_iota(jnp.int32, shape, 1) % HEAD_DIM < HEAD_DIM // 2
+
+
+def rope_pair(values, cosine, sine):
+    span, half_dim = values.shape[1], HEAD_DIM // 2
+    ahead, behind = pltpu.roll(values, span - half_dim, 1), pltpu.roll(values, half_dim, 1)
+    return values * cosine + jnp.where(first_half(values.shape), -ahead, behind) * sine
+
+
+def unrope_pair(gradient, cosine, sine):
+    span, half_dim = gradient.shape[1], HEAD_DIM // 2
+    sined = gradient * sine
+    ahead, behind = pltpu.roll(sined, span - half_dim, 1), pltpu.roll(sined, half_dim, 1)
+    return gradient * cosine + jnp.where(first_half(sined.shape), ahead, -behind)
 
 
 def dot_nt(left, right):
@@ -74,9 +75,9 @@
         return self.send(array, "tp", [(0, 1), (1, 0)])
 
     def sum_all(self, array):
-        array = sum((self.swap(array, 2 * k) for k in range(1, self.far)), array)
         array = array + self.swap(array, 1)
-        return array + self.swap_ctx(array)
+        array = array + self.swap_ctx(array)
+        return sum((self.swap(array, 2 * k) for k in range(1, self.far)), array)
 
     def gather_far(self, shard):
         far = [self.swap(shard, 2 * k) for k in range(1, self.far)]
@@ -91,6 +92,20 @@
     def gather(self, shard):
         return self.gather_near(self.gather_far(shard))
 
+    def gather_shared(self, shard, ctx, rows):
+        first = shard.shape[0] - 2 * rows
+        mine = jnp.where(ctx == 0, shard[first : first + rows], shard[first + rows :])
+        blocks = self.gather(jnp.concatenate([shard[:first], mine]))
+        groups = [(1, 2), (3, 4, 6), (5, 7)] if self.size == 8 else [range(1, self.size)]
+        others = [None] * self.size
+        for g, members in enumerate(groups):
+            sent = jnp.stack([blocks[k][first:] for k in members])
+            got = self.swap_ctx(sent)
+            for j, k in enumerate(members):
+                others[k] = (g, j)
+            groups[g] = got
+        return shard, blocks[1:], groups, others[1:]
+
     def exchange_near(self, blocks, low):
         here = low == 0
         kept = jnp.stack([jnp.where(here, a, b) for a, b in zip(blocks[0::2], blocks[1::2])])
@@ -98,6 +113,7 @@
         return kept, self.swap(sent, 1)
 
     def exchange_far(self, kept, got, high):
+        kept, high = lax.optimization_barrier((kept, high))
         out = []
         for k in range(self.far):
             block = jnp.stack(
@@ -128,16 +144,6 @@
     def after(self, array):
         array, self.value = lax.optimization_barrier((array, self.value))
         return array
-
-
-def place(blocks, index, size, axis):
-    shape = list(blocks[0].shape)
-    width = shape[axis]
-    shape[axis] = width * size
-    out = jnp.zeros(shape, blocks[0].dtype)
-    for k, block in enumerate(blocks):
-        out = lax.dynamic_update_slice_in_dim(out, block, (index ^ k) * width, axis)
-    return out
 
 
 def owned_kernel(far, count, half_hidden, place_ref, *refs):
@@ -177,34 +183,197 @@
     return pl.ds(pl.multiple_of((where_ref[0] ^ k) * slab, 128), slab)
 
 
-def project_in_kernel(slab, where_ref, tokens_ref, *refs):
-    blocks, (lin_ref, normed_ref, gains_ref) = refs[:-3], refs[-3:]
-    for k, block in enumerate(blocks):
-        pair = block[slab : slab + 8, :slab].astype(F32)
-        gains_ref[:, slab_of(where_ref, k, slab)] = pair
+def assemble(where_ref, whole_ref, own, blocks, groups, others):
+    rows = groups[0].shape[1]
+    total = own.shape[0]
+    first = total - 2 * rows
+    here = pl.ds(pl.multiple_of(first + where_ref[2] * rows, 16), rows)
+    there = pl.ds(pl.multiple_of(first + (1 - where_ref[2]) * rows, 16), rows)
+    whole_ref[0] = own[...]
+    for k, (block, (g, j)) in enumerate(zip(blocks, others)):
+        whole_ref[k + 1, :first, :] = block[:first, :]
+        whole_ref[k + 1, here, :] = block[first:, :]
+        whole_ref[k + 1, there, :] = groups[g][j]
+
+
+def split_refs(refs, others, outs):
+    count = len(others)
+    inputs = refs[: len(refs) - outs]
+    return inputs[0], inputs[1 : 1 + count], inputs[1 + count :], refs[len(refs) - outs :]
+
+
+def project_in_kernel(slab, others, where_ref, tokens_ref, cosine_ref, sine_ref, *refs):
+    own, blocks, groups, outs = split_refs(refs, others, 5)
+    query_ref, kv_ref, normed_ref, gains_ref, whole_ref = outs
+    assemble(where_ref, whole_ref, own, blocks, groups, others)
+    count = len(others) + 1
+    for k in range(count):
+        gains_ref[:, slab_of(where_ref, k, slab)] = whole_ref[k, slab:, :slab].astype(F32)
     tokens = tokens_ref[...].astype(F32)
     rms = lax.rsqrt(jnp.mean(tokens * tokens, axis=-1, keepdims=True) + EPSILON)
     normed_ref[...] = (tokens * rms * gains_ref[0:1, :]).astype(BF16)
     total = None
-    for k, block in enumerate(blocks):
-        part = dot_nn(normed_ref[:, slab_of(where_ref, k, slab)], block[:slab, :])
+    for k in range(count):
+        part = dot_nn(normed_ref[:, slab_of(where_ref, k, slab)], whole_ref[k, :slab, :])
         total = part if total is None else total + part
-    lin_ref[...] = total
-
-
-def project_out_kernel(slab, where_ref, left_ref, *refs):
-    blocks, out_ref = refs[:-1], refs[-1]
-    for k, block in enumerate(blocks):
-        out_ref[:, slab_of(where_ref, k, slab)] = dot_nt(left_ref[...], block[:slab, :])
-
-
-def project_back_kernel(slab, where_ref, left_ref, *refs):
-    blocks, out_ref = refs[:-1], refs[-1]
+    cosine, sine = cosine_ref[...], sine_ref[...]
+    queries, keys = query_ref.shape[1], kv_ref.shape[1] // 2
+    for j in range(0, queries + 2 * keys, 128):
+        part = total[:, j : j + 128]
+        if j < queries + keys:
+            part = rope_pair(part, cosine, sine)
+        if j < queries:
+            query_ref[:, j : j + 128] = part.astype(BF16)
+        else:
+            kv_ref[:, j - queries : j - queries + 128] = part.astype(BF16)
+
+
+def project_gathered_kernel(slab, others, where_ref, left_ref, *refs):
+    own, blocks, groups, (out_ref, whole_ref) = split_refs(refs, others, 2)
+    assemble(where_ref, whole_ref, own, blocks, groups, others)
+    for k in range(len(others) + 1):
+        out_ref[:, slab_of(where_ref, k, slab)] = dot_nt(left_ref[...], whole_ref[k])
+
+
+def project_out_kernel(slab, where_ref, left_ref, whole_ref, out_ref):
+    for k in range(whole_ref.shape[0]):
+        out_ref[:, slab_of(where_ref, k, slab)] = dot_nt(left_ref[...], whole_ref[k, :slab, :])
+
+
+def project_back_kernel(slab, where_ref, left_ref, whole_ref, out_ref):
     total = None
-    for k, block in enumerate(blocks):
-        part = dot_nn(left_ref[:, slab_of(where_ref, k, slab)], block[:slab, :])
+    for k in range(whole_ref.shape[0]):
+        part = dot_nn(left_ref[:, slab_of(where_ref, k, slab)], whole_ref[k, :slab, :])
         total = part if total is None else total + part
     out_ref[...] = total.astype(out_ref.dtype)
+
+
+def allowed_pairs(ctx, positions):
+    count = positions.shape[1]
+    shape = (2 * count, count)
+    key = lax.broadcasted_iota(jnp.int32, shape, 0)
+    key = jnp.where(key < count, ctx * count + key, (1 - ctx) * count + key - count)
+    query = ctx * count + lax.broadcasted_iota(jnp.int32, shape, 1)
+    return (key <= query) & (key >= query - positions)
+
+
+def attend_kernel(where_ref, positions_ref, query_ref, kv_ref, out_ref, lse_ref):
+    keys = kv_ref.shape[1] // 2
+    groups = keys // HEAD_DIM
+    pairs = query_ref.shape[1] // 128 // groups
+    allowed = allowed_pairs(where_ref[2], positions_ref[...])
+    for g in range(groups):
+        key = kv_ref[:, g * HEAD_DIM : (g + 1) * HEAD_DIM]
+        value_t = kv_ref[:, keys + g * HEAD_DIM : keys + (g + 1) * HEAD_DIM].T
+
+        def step(i, carry, g=g, key=key, value_t=value_t):
+            at = g * pairs + i
+            columns = pl.ds(pl.multiple_of(at * 128, 128), 128)
+            query = query_ref[:, columns]
+            attended, sums = [], []
+            for h in range(2):
+                scores = dot_nt(key, query[:, h * HEAD_DIM : (h + 1) * HEAD_DIM])
+                scores = jnp.where(allowed, scores * HEAD_DIM ** (-0.5), NEG_FILL)
+                largest = jnp.max(scores, axis=0, keepdims=True)
+                exponent = jnp.exp(scores - largest)
+                totals = jnp.sum(exponent, axis=0, keepdims=True)
+                attended.append(dot_nn(value_t, (exponent / totals).astype(BF16)))
+                sums.append(largest + jnp.log(totals))
+            out_ref[:, columns] = jnp.concatenate(attended, axis=0).T.astype(BF16)
+            lse_ref[at] = jnp.concatenate(sums, axis=0)
+            return carry
+
+        lax.fori_loop(0, pairs, step, 0)
+
+
+def attend_back_kernel(
+    where_ref,
+    positions_ref,
+    query_ref,
+    kv_ref,
+    lse_ref,
+    grad_ref,
+    cosine_ref,
+    sine_ref,
+    grad_query_ref,
+    grad_kv_ref,
+):
+    keys = kv_ref.shape[1] // 2
+    groups = keys // HEAD_DIM
+    pairs = query_ref.shape[1] // 128 // groups
+    scale = HEAD_DIM ** (-0.5)
+    allowed = allowed_pairs(where_ref[2], positions_ref[...])
+    cosine, sine = cosine_ref[...], sine_ref[...]
+    grad_kv_ref[...] = jnp.zeros_like(grad_kv_ref)
+    for g in range(groups):
+        key_columns = slice(g * HEAD_DIM, (g + 1) * HEAD_DIM)
+        value_columns = slice(keys + g * HEAD_DIM, keys + (g + 1) * HEAD_DIM)
+        key, value = kv_ref[:, key_columns], kv_ref[:, value_columns]
+        key_t = key.T
+
+        def step(i, carry, g=g, key=key, value=value, key_t=key_t):
+            at = g * pairs + i
+            columns = pl.ds(pl.multiple_of(at * 128, 128), 128)
+            query, grad, lse = query_ref[:, columns], grad_ref[:, columns], lse_ref[at]
+            grad_query, grad_key, grad_value = [], 0.0, 0.0
+            for h in range(2):
+                head = slice(h * HEAD_DIM, (h + 1) * HEAD_DIM)
+                scores = jnp.where(allowed, dot_nt(key, query[:, head]) * scale, NEG_FILL)
+                probs = jnp.exp(scores - lse[h : h + 1])
+                grad_probs = dot_nt(value, grad[:, head])
+                row_dot = jnp.sum(probs * grad_probs, axis=0, keepdims=True)
+                grad_scores = (probs * (grad_probs - row_dot)).astype(BF16)
+                grad_query.append(dot_nn(key_t, grad_scores) * scale)
+                grad_key += dot_nn(grad_scores, query[:, head])
+                grad_value += dot_nn(probs.astype(BF16), grad[:, head])
+            turned = jnp.concatenate(grad_query, axis=0).T
+            grad_query_ref[:, columns] = unrope_pair(turned, cosine, sine).astype(BF16)
+            return carry[0] + grad_key, carry[1] + grad_value
+
+        zero = jnp.zeros((kv_ref.shape[0], HEAD_DIM), F32)
+        grad_key, grad_value = lax.fori_loop(0, pairs, step, (zero, zero))
+        grad_kv_ref[:, key_columns] = grad_key * scale
+        grad_kv_ref[:, value_columns] = grad_value
+
+
+def finish_kv_kernel(where_ref, grad_query_ref, mine_ref, other_ref, cosine_ref, sine_ref, out_ref):
+    queries, keys = grad_query_ref.shape[1], mine_ref.shape[1] // 2
+    out_ref[:, :queries] = grad_query_ref[...]
+    total = mine_ref[...] + other_ref[...]
+    for j in range(0, keys, 128):
+        turned = unrope_pair(total[:, j : j + 128], cosine_ref[...], sine_ref[...])
+        out_ref[:, queries + j : queries + j + 128] = turned.astype(BF16)
+    out_ref[:, queries + keys :] = total[:, keys:].astype(BF16)
+
+
+def hidden_kernel(hidden, slab, where_ref, *refs):
+    gate_up_ref, down_ref = refs[-2:]
+    far = (len(refs) - 2) // 2
+    padded, half = down_ref.shape[0], hidden // 2
+    places = ((gate_up_ref, 0), (gate_up_ref, padded), (down_ref, 0))
+    for i, (out_ref, base) in enumerate(places):
+        for k in range(far):
+            for r in range(2):
+                columns = slab_of(where_ref, 2 * k + r, slab)
+                out_ref[base : base + half, columns] = refs[k][r, i]
+                out_ref[base + half : base + hidden, columns] = refs[far + k][r, i]
+        if padded > hidden:
+            out_ref[base + hidden : base + padded, :] = jnp.zeros(
+                (padded - hidden, out_ref.shape[1]), out_ref.dtype
+            )
+
+
+def feed_kernel(where_ref, normed_ref, rows_ref, grad_act_ref, grads_ref, act_ref):
+    padded = act_ref.shape[1]
+    for t in range(0, normed_ref.shape[0], 256):
+        lin = dot_nt(normed_ref[t : t + 256, :], rows_ref[...])
+        gate, up, grad_act = lin[:, :padded], lin[:, padded:], grad_act_ref[t : t + 256, :]
+        below = 1.0 + jnp.exp(-gate)
+        sigmoid, silu = 1.0 / below, gate / below
+        act_ref[t : t + 256, :] = (silu * up).astype(BF16)
+        grad_gate = grad_act * up * sigmoid * (1.0 + gate * (1.0 - sigmoid))
+        grads_ref[t : t + 256, :padded] = grad_gate.astype(BF16)
+        grads_ref[t : t + 256, padded:] = (grad_act * silu).astype(BF16)
 
 
 def outer_kernel(half, where_ref, mine_ref, other_ref, *refs):
@@ -259,10 +428,6 @@
     key_columns = key_weight.shape[1]
     hidden = gate_weight.shape[1] // nf
     half_hidden = hidden // 2
-    local_groups = key_columns // HEAD_DIM
-    group_size = HEADS // KV_HEADS
-    group_width = group_size * HEAD_DIM
-    score_scale = HEAD_DIM ** (-0.5)
 
     def my_half(array):
         return lax.dynamic_slice_in_dim(array, core * half_rows, half_rows, 0)
@@ -276,22 +441,23 @@
 
     def plane_rows(array):
         mine = jnp.concatenate(plane.gather(my_half(array)), axis=0)
-        return jnp.concatenate([mine, plane.swap_tp(mine)], axis=0)
+        return mine, plane.swap_tp(mine)
 
     def columns_near(array):
-        mine = my_half(array)
+        mine, parity = lax.optimization_barrier((my_half(array), low))
         blocks = [mine[:, i * slab : (i + 1) * slab] for i in range(nf)]
-        return plane.exchange_near(blocks, low)
+        return plane.exchange_near(blocks, parity)
 
     fences = Fences(doc_positions[0])
 
-    gain_rows = jnp.zeros((8, query_columns + 2 * key_columns), BF16)
+    gain_rows = jnp.zeros((16, query_columns + 2 * key_columns), BF16)
     gain_rows = gain_rows.at[0, :slab].set(attn_gain).at[1, :slab].set(mlp_gain)
     qkv_shard = jnp.concatenate(
         [jnp.concatenate([query_weight, key_weight, value_weight], axis=1), gain_rows], axis=0
     )
-    qkv_blocks = plane.gather(qkv_shard)
-    output_blocks = plane.gather(output_weight)
+    shared_rows = slab * 5 // 16 // 16 * 16
+    qkv_own, qkv_blocks, qkv_groups, qkv_others = plane.gather_shared(qkv_shard, ctx, shared_rows)
+    wo_own, wo_blocks, wo_groups, wo_others = plane.gather_shared(output_weight, ctx, shared_rows)
     cot_all = plane_rows(cotangent)
 
     mlp_shard = jnp.stack([gate_weight.T, up_weight.T, down_weight.T])
@@ -304,33 +470,31 @@
     fences.cut()
     fences.cut()
     fences.cut()
+    fences.cut()
     tokens = tokens_in.astype(F32)
     rms_one = lax.rsqrt(jnp.mean(tokens * tokens, axis=-1, keepdims=True) + EPSILON)
     scaled_one = tokens * rms_one
-    where = jnp.stack([me, core]).astype(jnp.int32)
-    qkv_lin, normed_one, gains = local_kernel(
-        functools.partial(project_in_kernel, slab),
+    where = jnp.stack([me, core, ctx]).astype(jnp.int32)
+    cosine, sine = pair_tables(doc_positions)
+    queries, kv_mine, normed_one, gains, qkv_whole = local_kernel(
+        functools.partial(project_in_kernel, slab, qkv_others),
         [
-            jax.ShapeDtypeStruct((rows, query_columns + 2 * key_columns), F32),
+            jax.ShapeDtypeStruct((rows, query_columns), BF16),
+            jax.ShapeDtypeStruct((rows, 2 * key_columns), BF16),
             jax.ShapeDtypeStruct((rows, width), BF16),
-            jax.ShapeDtypeStruct((8, width), F32),
+            jax.ShapeDtypeStruct((16, width), F32),
+            jax.ShapeDtypeStruct((nf,) + qkv_shard.shape, BF16),
         ],
         [],
         where,
         tokens_in,
+        cosine,
+        sine,
+        qkv_own,
         *qkv_blocks,
+        *qkv_groups,
     )
     gain_one, gain_two = gains[0:1], gains[1:2]
-
-    def project_out(left, blocks):
-        return local_kernel(
-            functools.partial(project_out_kernel, slab),
-            [jax.ShapeDtypeStruct((rows, width), F32)],
-            [],
-            where,
-            left,
-            *blocks,
-        )[0]
 
     def outer(got, blocks):
         mine = jnp.concatenate(got)
@@ -344,61 +508,37 @@
             *blocks,
         )[0]
 
-    query_lin = qkv_lin[:, :query_columns]
-    key_lin = qkv_lin[:, query_columns : query_columns + key_columns]
-    value_lin = qkv_lin[:, query_columns + key_columns :]
-    cosine_table, sine_table = rotary_tables(doc_positions)
-    queries = (
-        apply_rotary(query_lin.reshape(rows, -1, HEAD_DIM), cosine_table, sine_table)
-        .astype(BF16)
-        .reshape(rows, query_columns)
-    )
-    keys_low = (
-        apply_rotary(key_lin.reshape(rows, -1, HEAD_DIM), cosine_table, sine_table)
-        .astype(BF16)
-        .reshape(rows, key_columns)
-    )
-    values_low = value_lin.astype(BF16)
-    kv_mine = jnp.concatenate([keys_low, values_low], axis=1)
+    kv_other = plane.swap_ctx(kv_mine)
     kv_mine, queries = fences.cut(kv_mine, queries)
-    kv_all = jnp.concatenate([kv_mine, plane.swap_ctx(kv_mine)], axis=0)
-    key_all, value_all = kv_all[:, :key_columns], kv_all[:, key_columns:]
-    places = jnp.arange(rows, dtype=jnp.int32)
-    query_places = ctx * rows + places
-    key_places = jnp.concatenate([ctx * rows + places, (1 - ctx) * rows + places])
-    allowed = (key_places[None, :] <= query_places[:, None]) & (
-        key_places[None, :] >= (query_places - doc_positions)[:, None]
-    )
-
-    def head_scores(query_group, key_head):
-        raw_scores = (
-            jnp.einsum("ngd,kd->gnk", query_group, key_head, preferred_element_type=F32)
-            * score_scale
-        )
-        return jnp.where(allowed[None], raw_scores, NEG_FILL)
-
-    attended_parts = []
-    lse_parts = []
-    for group_index in range(local_groups):
-        query_group = queries[
-            :, group_index * group_width : (group_index + 1) * group_width
-        ].reshape(rows, group_size, HEAD_DIM)
-        key_head = key_all[:, group_index * HEAD_DIM : (group_index + 1) * HEAD_DIM]
-        value_head = value_all[:, group_index * HEAD_DIM : (group_index + 1) * HEAD_DIM]
-        scores = head_scores(query_group, key_head)
-        largest = jnp.max(scores, axis=-1, keepdims=True)
-        exponent = jnp.exp(scores - largest)
-        totals = jnp.sum(exponent, axis=-1, keepdims=True)
-        probs_low = (exponent / totals).astype(BF16)
-        attended_parts.append(
-            jnp.einsum("gnk,kd->ngd", probs_low, value_head, preferred_element_type=F32).reshape(
-                rows, group_width
-            )
-        )
-        lse_parts.append(largest + jnp.log(totals))
-    attended_low = jnp.concatenate(attended_parts, axis=1).astype(BF16)
+    kv_all = jnp.concatenate([kv_mine, kv_other], axis=0)
+    positions = doc_positions[None, :]
+    attended_low, lse = local_kernel(
+        attend_kernel,
+        [
+            jax.ShapeDtypeStruct((rows, query_columns), BF16),
+            jax.ShapeDtypeStruct((query_columns // 128, 2, rows), F32),
+        ],
+        [],
+        where,
+        positions,
+        queries,
+        kv_all,
+    )
     attended_low = fences.cut(attended_low)
-    residual = tokens + tp_sum(project_out(attended_low, output_blocks))
+    branch, wo_whole = local_kernel(
+        functools.partial(project_gathered_kernel, slab, wo_others),
+        [
+            jax.ShapeDtypeStruct((rows, width), F32),
+            jax.ShapeDtypeStruct((nf,) + output_weight.shape, BF16),
+        ],
+        [],
+        where,
+        attended_low,
+        wo_own,
+        *wo_blocks,
+        *wo_groups,
+    )
+    residual = tokens + tp_sum(branch)
     rms_two = lax.rsqrt(jnp.mean(residual * residual, axis=-1, keepdims=True) + EPSILON)
     scaled_two = residual * rms_two
     normed_two = (scaled_two * gain_two).astype(BF16)
@@ -408,24 +548,42 @@
     fences.cut()
     fences.cut()
     fences.cut()
-    mlp_mine = place([b[r] for b in mlp_blocks for r in range(2)], me, nf, 2)
-    mlp_all = jnp.concatenate([mlp_mine, plane.swap_ctx(mlp_mine)], axis=1)
-    gate_t, up_t, down_t = mlp_all[0], mlp_all[1], mlp_all[2]
-    attended_far = plane.gather_far(attended_low)
-    normed_near = columns_near(normed_one)
+    padded = -(-hidden // 128) * 128
+    gate_up_t, down_t = local_kernel(
+        functools.partial(hidden_kernel, hidden, slab),
+        [
+            jax.ShapeDtypeStruct((2 * padded, width), BF16),
+            jax.ShapeDtypeStruct((padded, width), BF16),
+        ],
+        [],
+        where,
+        *mlp_blocks,
+        *(plane.swap_ctx(b) for b in mlp_blocks),
+    )
+    attended_all = plane.gather(attended_low)
+    normed_near = columns_near(fences.after(normed_one))
     normed_got = plane.exchange_far(*normed_near, high)
-    gate_lin = dot_nt(normed_all, gate_t)
-    up_lin = dot_nt(normed_all, up_t)
-    grad_act = dot_nt(cot_all, down_t)
-    sigmoid = 1.0 / (1.0 + jnp.exp(-gate_lin))
-    silu_value = gate_lin / (1.0 + jnp.exp(-gate_lin))
-    act_low = (silu_value * up_lin).astype(BF16)
-    grad_gate_lin = (grad_act * up_lin * sigmoid * (1.0 + gate_lin * (1.0 - sigmoid))).astype(BF16)
-    grad_up_lin = (grad_act * silu_value).astype(BF16)
-
-    def ctx_half(left, right):
-        whole = dot_tn(left, right)
-        return whole[:half_hidden], plane.swap_ctx(whole[half_hidden:])
+    grads, acts = [], []
+    for h in range(2):
+        grad_h, act_h = local_kernel(
+            feed_kernel,
+            [
+                jax.ShapeDtypeStruct((nf * half_rows, 2 * padded), BF16),
+                jax.ShapeDtypeStruct((nf * half_rows, padded), BF16),
+            ],
+            [],
+            where,
+            normed_all[h],
+            gate_up_t,
+            dot_nt(cot_all[h], down_t),
+        )
+        grads.append(grad_h)
+        acts.append(act_h)
+
+    def ctx_half(whole, first):
+        middle, last = first + half_hidden, first + hidden
+        got = plane.swap_ctx(fences.after(whole[middle:last]))
+        return sum(lax.optimization_barrier((whole[first:middle], got)))
 
     def owners_near(halves):
         blocks = [
@@ -438,14 +596,10 @@
         where = jnp.stack([high, low, ctx]).astype(jnp.int32)
         return owned(got, other, where)
 
-    def tp_part(terms, wire, columns):
-        half = nf * half_rows
-        mine, other = [
-            sum(dot_nn(left[h * half : (h + 1) * half], right[:, columns]) for left, right in terms)
-            for h in range(2)
-        ]
-        other = plane.swap_tp(other.astype(wire)).astype(F32)
-        return plane.reduce_near((mine + other).reshape(nf, half_rows, -1), wire)
+    def tp_part(lefts, right, wire):
+        other = plane.swap_tp(dot_nn(lefts[1], right).astype(wire)).astype(F32)
+        mine = dot_nn(lefts[0], right) + other
+        return plane.reduce_near(mine.reshape(nf, half_rows, -1), wire)
 
     def whole_rows(mine):
         one, two = tp_order(mine, plane.swap_tp(mine))
@@ -457,32 +611,28 @@
     reduced = []
 
     def piece(i):
-        near.append(
-            tp_part(
-                ((fences.after(grad_gate_lin), gate_t), (fences.after(grad_up_lin), up_t)),
-                F32,
-                slice(i * step, (i + 1) * step),
-            )
-        )
+        lefts = [fences.after(g) for g in grads]
+        near.append(tp_part(lefts, gate_up_t[:, i * step : (i + 1) * step], F32))
 
     def piece_far(i):
         reduced.append(plane.reduce_far(near[i][0] + near[i][1]))
 
-    grad_gate_lin, grad_up_lin, act_low = fences.cut(grad_gate_lin, grad_up_lin, act_low)
+    grads[0], grads[1], acts[0], acts[1] = fences.cut(*grads, *acts)
     piece(0)
     piece(1)
-    half_down = sum(ctx_half(fences.after(act_low), cot_all))
+    half_down = ctx_half(sum(dot_tn(fences.after(a), c) for a, c in zip(acts, cot_all)), 0)
     fences.cut()
     piece_far(0)
     piece(2)
-    half_gate = sum(ctx_half(fences.after(grad_gate_lin), normed_all))
+    gate_up_grad = sum(dot_tn(fences.after(g), n) for g, n in zip(grads, normed_all))
+    half_gate = ctx_half(gate_up_grad, 0)
     fences.cut()
     piece_far(1)
     piece(3)
-    half_up = sum(ctx_half(fences.after(grad_up_lin), normed_all))
+    half_up = ctx_half(gate_up_grad, padded)
     fences.cut()
     piece_far(2)
-    mlp_kept, mlp_odd = tp_part(((fences.after(act_low), down_t),), BF16, slice(None))
+    mlp_kept, mlp_odd = tp_part([fences.after(a) for a in acts], down_t, BF16)
     down_near = owners_near([half_down])
     fences.cut()
     piece_far(3)
@@ -508,62 +658,53 @@
         [],
         where,
         grad_attn_low,
-        *output_blocks,
+        wo_whole,
     )[0]
-    grad_attn_near = columns_near(grad_attn_low)
+    grad_attn_near = columns_near(fences.after(grad_attn_low))
     grad_attended = fences.cut(grad_attended)
-    query_grads = []
-    key_grads = []
-    value_grads = []
-    for group_index in range(local_groups):
-        query_group = queries[
-            :, group_index * group_width : (group_index + 1) * group_width
-        ].reshape(rows, group_size, HEAD_DIM)
-        key_head = key_all[:, group_index * HEAD_DIM : (group_index + 1) * HEAD_DIM]
-        value_head = value_all[:, group_index * HEAD_DIM : (group_index + 1) * HEAD_DIM]
-        probabilities = jnp.exp(head_scores(query_group, key_head) - lse_parts[group_index])
-        probs_low = probabilities.astype(BF16)
-        grad_group = grad_attended[
-            :, group_index * group_width : (group_index + 1) * group_width
-        ].reshape(rows, group_size, HEAD_DIM)
-        grad_probs = jnp.einsum("ngd,kd->gnk", grad_group, value_head, preferred_element_type=F32)
-        row_dot = jnp.sum(probabilities * grad_probs, axis=-1, keepdims=True)
-        grad_scores = (probabilities * (grad_probs - row_dot)).astype(BF16)
-        query_grads.append(
-            jnp.einsum("gnk,kd->ngd", grad_scores, key_head, preferred_element_type=F32)
-            * score_scale
-        )
-        key_grads.append(
-            jnp.einsum("gnk,ngd->kd", grad_scores, query_group, preferred_element_type=F32)
-            * score_scale
-        )
-        value_grads.append(
-            jnp.einsum("gnk,ngd->kd", probs_low, grad_group, preferred_element_type=F32)
-        )
-    kv_grads = jnp.concatenate(key_grads + value_grads, axis=1)
-    kv_grads, *query_grads = fences.cut(kv_grads, *query_grads)
+    grad_query, kv_grads = local_kernel(
+        attend_back_kernel,
+        [
+            jax.ShapeDtypeStruct((rows, query_columns), BF16),
+            jax.ShapeDtypeStruct((2 * rows, 2 * key_columns), F32),
+        ],
+        [],
+        where,
+        positions,
+        queries,
+        kv_all,
+        lse,
+        grad_attended,
+        cosine,
+        sine,
+    )
+    kv_grads, grad_query = fences.cut(kv_grads, grad_query)
     mlp_mine = plane.reduce_far(mlp_kept + mlp_odd.astype(F32), BF16)
     grad_attn_got = plane.exchange_far(*grad_attn_near, high)
-    kv_grad_local = kv_grads[:rows] + plane.swap_ctx(kv_grads[rows:])
-    key_grad_local, value_grad_local = kv_grad_local[:, :key_columns], kv_grad_local[:, key_columns:]
-    grad_q_lin = (
-        undo_rotary(jnp.concatenate(query_grads, axis=1), cosine_table, sine_table)
-        .astype(BF16)
-        .reshape(rows, query_columns)
-    )
-    grad_k_lin = (
-        undo_rotary(key_grad_local.reshape(rows, -1, HEAD_DIM), cosine_table, sine_table)
-        .astype(BF16)
-        .reshape(rows, key_columns)
-    )
-    grad_qkv_lin = jnp.concatenate(
-        [grad_q_lin, grad_k_lin, value_grad_local.astype(BF16)], axis=1
+    (grad_qkv_lin,) = local_kernel(
+        finish_kv_kernel,
+        [jax.ShapeDtypeStruct((rows, query_columns + 2 * key_columns), BF16)],
+        [],
+        where,
+        grad_query,
+        kv_grads[:rows],
+        plane.swap_ctx(kv_grads[rows:]),
+        cosine,
+        sine,
     )
     grad_qkv_all = plane.gather(grad_qkv_lin)
     fences.cut()
     gate_up_got = plane.exchange_far(*gate_up_near, high)
-    attended_all = plane.gather_near(attended_far)
-    grad_normed_one = tp_sum(project_out(fences.after(grad_qkv_lin), qkv_blocks))
+    grad_normed_one = tp_sum(
+        local_kernel(
+            functools.partial(project_out_kernel, slab),
+            [jax.ShapeDtypeStruct((rows, width), F32)],
+            [],
+            where,
+            fences.after(grad_qkv_lin),
+            qkv_whole,
+        )[0],
+    )
     fences.cut()
     gain_sums = plane.sum_all(
         jnp.stack(
@@ -612,6 +753,29 @@
         gate_grad,
         up_grad,
         down_grad,
+    )
+
+
+def rotary_tables(positions):
+    half_dim = HEAD_DIM // 2
+    inverse = 1.0 / 10000.0 ** (jnp.arange(half_dim, dtype=F32) * (2.0 / HEAD_DIM))
+    angles = positions.astype(F32)[:, None] * inverse[None, :]
+    cosine_table = jnp.concatenate([jnp.cos(angles), jnp.cos(angles)], axis=-1)[:, None, :]
+    sine_table = jnp.concatenate([jnp.sin(angles), jnp.sin(angles)], axis=-1)[:, None, :]
+    return (cosine_table, sine_table)
+
+
+def apply_rotary(values, cosine_table, sine_table):
+    half_dim = values.shape[-1] // 2
+    turned = jnp.concatenate([-values[..., half_dim:], values[..., :half_dim]], axis=-1)
+    return values * cosine_table + turned * sine_table
+
+
+def undo_rotary(gradient, cosine_table, sine_table):
+    half_dim = gradient.shape[-1] // 2
+    sined = gradient * sine_table
+    return gradient * cosine_table + jnp.concatenate(
+        [sined[..., half_dim:], -sined[..., :half_dim]], axis=-1
     )
 
 

time: 1100 us -> 1170 us (1.064)
  waiting for transfers between devices: 560 us -> 609 us
  Pallas kernels: 34.1 us -> 73.7 us
  matrix products: 86.4 us -> 65.7 us
    ppermute x116 -> x125, waiting for transfers between devices: 560 us -> 609 us  [send(): return lax.ppermute(array, axis, pairs)]
    pallas_call x8 -> x14, Pallas kernels: 34.1 us -> 73.7 us  [local_kernel(): pl.pallas_call(kernel, out_shape=outs, in_specs=[SCALARS] + [WHOLE] * (le...]
    dot_general x12 -> x0, matrix products: 17.8 us -> none  [the longest x2 6.09 us: layer(): jnp.einsum('gnk,ngd->kd', probs_low, grad_group, preferred_element_type=F32)]
    concatenate x7 -> x2, local copies, waits for them, and re-layouts: 13.4 us -> 0.87 us  [the longest x1 0.86 us: layer(): jnp.concatenate([query_weight, key_weight, value_weight], axis=1)]
    unnamed x212 -> x201, local copies, waits for them, and re-layouts: 55.1 us -> 65.4 us
    ppermute x116 -> x125, starting transfers between devices: 230 us -> 237 us  [send(): return lax.ppermute(array, axis, pairs)]
    dot_general x18 -> x10, matrix products: 36.3 us -> 34.9 us  [dot_nn(): return jnp.dot(left, right, preferred_element_type=F32)]
  transfers between devices with their start and end apart: 116 -> 125, of which waited for: 43 -> 53; matrix products, arithmetic and copies ran while one was open for 19% -> 15% of each run, Pallas kernels for 3% -> 6%
where the time goes in v1:
time: 1170 us; the launch traced here: 1160 us
  waiting for transfers between devices  609 us (52%)
  starting transfers between devices  237 us (20%)
  local copies, waits for them, and re-layouts  99.5 us (9%)
  Pallas kernels  73.7 us (6%)
  other arithmetic  67 us (6%)
  matrix products  65.7 us (6%)
    ppermute x125, waiting for transfers between devices, send(): return lax.ppermute(array, axis, pairs)  609 us
    ppermute x125, starting transfers between devices, send(): return lax.ppermute(array, axis, pairs)  237 us
    pallas_call x14, Pallas kernels, local_kernel(): pl.pallas_call(kernel, out_shape=outs, in_specs=[SCALARS] + [WHOLE] * (le...  73.7 us
    unnamed x201, local copies, waits for them, and re-layouts  65.4 us
    dot_general x10, matrix products, dot_nn(): return jnp.dot(left, right, preferred_element_type=F32)  34.9 us
  transfers between devices with their start and end apart: 125, of which 53 were waited for; matrix products, arithmetic and copies ran while one was open for 15% of the time, Pallas kernels for 6%

profile of v1, /device:TPU:0, one launch (start us, length us, event | category | flops | bytes accessed | tf_op | source)
XLA Modules:
  0.0 1155.6 jit_solution(6874129536591281502)
XLA Ops:
  26.1 26.6 %collective-permute-done.16.refs_6_ = bf16[176,1024]{1,0:T(8,128)(2,1)S(1)} collective-permute-done((bf16[176,1024]{1,0:T(8,128)(2,1)}, bf16[176,1024]{1,0:T(8,128)(2,1)S(1)}, u32[]{:S(2)}, u32[]{:S(2)}) %collective-permute-start.16) | collective-permute-done | bytes 360480 | tf_op jit(solution)/shard_map/ppermute | solution.py:65
  52.8 26.6 %collective-permute-start.12 = (bf16[176,1024]{1,0:T(8,128)(2,1)}, bf16[176,1024]{1,0:T(8,128)(2,1)S(1)}, u32[]{:S(2)}, u32[]{:S(2)}) collective-permute-start(bf16[176,1024]{1,0:T(8,128)(2,1)} %pad_maximum_fusion.23), channel_id=1, source_target_pairs={{0,8},{4,12},{8,0},{12,4},{16,24},{20,28},{24,16},{28,20},{1,9},{5... | collective-permute-start | bytes 1081352 | tf_op jit(solution)/shard_map/ppermute | solution.py:65
  79.4 6.1 collective-permute-done.14.refs_4_
  87.0 5.8 collective-permute-done.12.refs_2_
  101.9 5.3 collective-permute-done.refs_1_
  108.7 25.1 %collective-permute-done.17.refs_7_ = bf16[176,1024]{1,0:T(8,128)(2,1)S(1)} collective-permute-done((bf16[176,1024]{1,0:T(8,128)(2,1)S(1)}, bf16[176,1024]{1,0:T(8,128)(2,1)S(1)}, u32[]{:S(2)}, u32[]{:S(2)}) %collective-permute-start.17) | collective-permute-done | bytes 360480 | tf_op jit(solution)/shard_map/ppermute | solution.py:65
  135.3 6.2 collective-permute-done.15.refs_5_
  143.1 9.0 collective-permute-done.2.refs_3_
  153.7 8.9 collective-permute-done.6.refs_7_
  164.1 7.8 collective-permute-done.4.refs_5_
  177.3 10.0 collective-permute-done.9.refs_10_
  198.2 14.0 %collective-permute-done.10 = bf16[256,256]{1,0:T(8,128)(2,1)S(1)} collective-permute-done((bf16[256,256]{1,0:T(8,128)(2,1)S(1)}, bf16[256,256]{1,0:T(8,128)(2,1)S(1)}, u32[]{:S(2)}, u32[]{:S(2)}) %collective-permute-start.10) | collective-permute-done | bytes 131104 | tf_op jit(solution)/shard_map/ppermute | solution.py:65
  212.3 11.5 shard_map.204
  234.1 4.5 shard_map.205
  247.7 12.6 %collective-permute-done.40 = bf16[128,2048]{1,0:T(8,128)(2,1)} collective-permute-done((bf16[128,2048]{1,0:T(8,128)(2,1)}, bf16[128,2048]{1,0:T(8,128)(2,1)}, u32[]{:S(2)}, u32[]{:S(2)}) %collective-permute-start.40) | collective-permute-done | bytes 524320 | tf_op jit(solution)/shard_map/ppermute | solution.py:65
  274.1 10.0 collective-permute-start.23
  286.5 7.5 collective-permute-done.41
  296.8 8.4 collective-permute-done.43
  309.4 7.1 collective-permute-done.22
  316.4 13.4 %collective-permute-done.25 = bf16[128,2048]{1,0:T(8,128)(2,1)S(1)} collective-permute-done((bf16[128,2048]{1,0:T(8,128)(2,1)S(1)}, bf16[128,2048]{1,0:T(8,128)(2,1)S(1)}, u32[]{:S(2)}, u32[]{:S(2)}) %collective-permute-start.25) | collective-permute-done | bytes 524320 | tf_op jit(solution)/shard_map/ppermute | solution.py:65
  335.2 8.8 collective-permute-done.26
  362.0 9.3 collective-permute-done.32.refs_3_
  374.7 29.0 %collective-permute-done.31.refs_2_ = bf16[2,3,176,256]{3,2,1,0:T(8,128)(2,1)S(1)} collective-permute-done((bf16[2,3,176,256]{3,2,1,0:T(8,128)(2,1)}, bf16[2,3,176,256]{3,2,1,0:T(8,128)(2,1)S(1)}, u32[]{:S(2)}, u32[]{:S(2)}) %collective-permute-start.31) | collective-permute-done | bytes 540704 | tf_op jit(solution)/shard_map/ppermute | solution.py:65
  421.2 11.6 %collective-permute-done.35.refs_6_ = bf16[2,3,176,256]{3,2,1,0:T(8,128)(2,1)S(1)} collective-permute-done((bf16[2,3,176,256]{3,2,1,0:T(8,128)(2,1)S(1)}, bf16[2,3,176,256]{3,2,1,0:T(8,128)(2,1)S(1)}, u32[]{:S(2)}, u32[]{:S(2)}) %collective-permute-start.35) | collective-permute-done | bytes 540704 | tf_op jit(solution)/shard_map/ppermute | solution.py:65
  432.8 10.0 collective-permute-done.34.refs_5_
  444.6 6.2 fusion.68.grad_act_ref
  450.9 6.5 shard_map.207
  457.5 4.8 fusion.69.grad_act_ref
  462.3 6.2 shard_map.208
  482.2 5.8 fusion.71
  488.0 5.5 convolution_add_fusion
  515.3 31.1 %collective-permute-done.106 = f32[176,2048]{1,0:T(8,128)} collective-permute-done((f32[176,2048]{1,0:T(8,128)}, f32[176,2048]{1,0:T(8,128)}, u32[]{:S(2)}, u32[]{:S(2)}) %collective-permute-start.106) | collective-permute-done | bytes 1441824 | tf_op jit(solution)/shard_map/ppermute | solution.py:65
  546.4 28.4 %collective-permute-done.107 = f32[176,2048]{1,0:T(8,128)} collective-permute-done((f32[176,2048]{1,0:T(8,128)}, f32[176,2048]{1,0:T(8,128)}, u32[]{:S(2)}, u32[]{:S(2)}) %collective-permute-start.107) | collective-permute-done | bytes 1441824 | tf_op jit(solution)/shard_map/ppermute | solution.py:65
  614.3 28.2 %collective-permute-done.108 = f32[4,2,176,256]{3,2,1,0:T(8,128)S(1)} collective-permute-done((f32[4,2,176,256]{3,2,1,0:T(8,128)S(1)}, f32[4,2,176,256]{3,2,1,0:T(8,128)S(1)}, u32[]{:S(2)}, u32[]{:S(2)}) %collective-permute-start.108) | collective-permute-done | bytes 1441824 | tf_op jit(solution)/shard_map/ppermute | solution.py:65
  643.0 22.0 %collective-permute-done.47 = f32[4,128,512]{2,1,0:T(8,128)S(1)} collective-permute-done((f32[4,128,512]{2,1,0:T(8,128)S(1)}, f32[4,128,512]{2,1,0:T(8,128)S(1)}, u32[]{:S(2)}, u32[]{:S(2)}) %collective-permute-start.47) | collective-permute-done | bytes 1048608 | tf_op jit(solution)/shard_map/ppermute | solution.py:65
  665.3 22.1 %collective-permute-done.52 = f32[4,128,512]{2,1,0:T(8,128)S(1)} collective-permute-done((f32[4,128,512]{2,1,0:T(8,128)S(1)}, f32[4,128,512]{2,1,0:T(8,128)S(1)}, u32[]{:S(2)}, u32[]{:S(2)}) %collective-permute-start.52) | collective-permute-done | bytes 1048608 | tf_op jit(solution)/shard_map/ppermute | solution.py:65
  687.7 22.2 %collective-permute-done.57 = f32[4,128,512]{2,1,0:T(8,128)S(1)} collective-permute-done((f32[4,128,512]{2,1,0:T(8,128)S(1)}, f32[4,128,512]{2,1,0:T(8,128)S(1)}, u32[]{:S(2)}, u32[]{:S(2)}) %collective-permute-start.57) | collective-permute-done | bytes 1048608 | tf_op jit(solution)/shard_map/ppermute | solution.py:65
  711.9 20.0 %collective-permute-done.62 = f32[4,128,512]{2,1,0:T(8,128)S(1)} collective-permute-done((f32[4,128,512]{2,1,0:T(8,128)S(1)}, f32[4,128,512]{2,1,0:T(8,128)S(1)}, u32[]{:S(2)}, u32[]{:S(2)}) %collective-permute-start.62) | collective-permute-done | bytes 1048608 | tf_op jit(solution)/shard_map/ppermute | solution.py:65
  736.7 9.7 collective-permute-done.53
  746.8 6.8 collective-permute-done.54
  755.4 15.6 %collective-permute-start.63 = (f32[128,512]{1,0:T(8,128)S(1)}, f32[128,512]{1,0:T(8,128)S(1)}, u32[]{:S(2)}, u32[]{:S(2)}) collective-permute-start(f32[128,512]{1,0:T(8,128)S(1)} %get-tuple-element.380), channel_id=1, source_target_pairs={{0,8},{4,12},{8,0},{12,4},{16,24},{20,28},{24,16},{28,20},{1,9},{5... | collective-permute-start | bytes 786440 | tf_op jit(solution)/shard_map/ppermute | solution.py:65
  771.3 13.2 %collective-permute-done.59 = f32[128,512]{1,0:T(8,128)S(1)} collective-permute-done((f32[128,512]{1,0:T(8,128)S(1)}, f32[128,512]{1,0:T(8,128)S(1)}, u32[]{:S(2)}, u32[]{:S(2)}) %collective-permute-start.59) | collective-permute-done | bytes 262176 | tf_op jit(solution)/shard_map/ppermute | solution.py:65
  786.4 5.5 collective-permute-start.79
  792.5 6.0 collective-permute-done.64
  803.4 18.8 %collective-permute-start.96 = (bf16[2,128,256]{2,1,0:T(8,128)(2,1)S(1)}, bf16[2,128,256]{2,1,0:T(8,128)(2,1)S(1)}, u32[]{:S(2)}, u32[]{:S(2)}) collective-permute-start(bf16[2,128,256]{2,1,0:T(8,128)(2,1)S(1)} %copy-done.79), channel_id=1, source_target_pairs={{0,16},{4,20},{8,24},{12,28},{16,0},{20,4},{24,8},{28,12},{1,17},{... | collective-permute-start | bytes 393224 | tf_op jit(solution)/shard_map/ppermute | solution.py:65
  822.2 7.8 convert_add_fusion
  844.7 9.0 collective-permute-done.75.refs_6_
  855.2 20.1 %collective-permute-start.119 = (f32[2,1,176,256]{3,2,1,0:T(8,128)}, f32[2,1,176,256]{3,2,1,0:T(8,128)}, u32[]{:S(2)}, u32[]{:S(2)}) collective-permute-start(f32[2,1,176,256]{3,2,1,0:T(8,128)} %pad_maximum_fusion.34), channel_id=1, source_target_pairs={{0,16},{4,20},{8,24},{12,28},{16,0},{20,4},{24,8},{28,12},{1,17},{... | collective-permute-start | bytes 1081352 | tf_op jit(solution)/shard_map/ppermute | solution.py:65
  881.6 8.5 collective-permute-done.119.refs_2_
  910.8 11.9 %shard_map.210 = (bf16[256,1024]{1,0:T(8,128)(2,1)S(1)}, f32[512,256]{1,0:T(8,128)S(1)}) custom-call(s32[3]{0:T(128)S(1)} %add_add_fusion.where_ref, s32[1,256]{1,0:T(1,128)S(1)} %bitcast.297, bf16[256,1024]{1,0:T(8,128)(2,1)S(1)} %copy-done.17, bf16[512,256]{1,0:T(8,128)(2,1)S(1)} %constant_dynamic-update-slice_fusion.3.kv_ref, ...), custom_call_target="tpu_custom_call" | custom-call | bytes 2638860 | tf_op jit(solution)/shard_map/pallas_call | solution.py:171
  926.5 7.7 collective-permute-done.122.refs_5_
  936.1 23.4 %collective-permute-done.110.refs_2_ = f32[2,2,176,256]{3,2,1,0:T(8,128)} collective-permute-done((f32[2,2,176,256]{3,2,1,0:T(8,128)}, f32[2,2,176,256]{3,2,1,0:T(8,128)}, u32[]{:S(2)}, u32[]{:S(2)}) %collective-permute-start.110) | collective-permute-done | bytes 720928 | tf_op jit(solution)/shard_map/ppermute | solution.py:65
  970.4 15.3 %collective-permute-done.67.other_ref = f32[256,256]{1,0:T(8,128)S(1)} collective-permute-done((f32[256,256]{1,0:T(8,128)S(1)}, f32[256,256]{1,0:T(8,128)S(1)}, u32[]{:S(2)}, u32[]{:S(2)}) %collective-permute-start.67) | collective-permute-done | bytes 262176 | tf_op jit(solution)/shard_map/ppermute | solution.py:65
  997.8 18.4 %collective-permute-done.72.refs_2_ = bf16[256,1280]{1,0:T(8,128)(2,1)} collective-permute-done((bf16[256,1280]{1,0:T(8,128)(2,1)}, bf16[256,1280]{1,0:T(8,128)(2,1)}, u32[]{:S(2)}, u32[]{:S(2)}) %collective-permute-start.72) | collective-permute-done | bytes 655392 | tf_op jit(solution)/shard_map/ppermute | solution.py:65
  1022.0 6.3 collective-permute-done.74.refs_1_
  1029.0 12.2 %collective-permute-done.70.refs_4_ = bf16[256,1280]{1,0:T(8,128)(2,1)} collective-permute-done((bf16[256,1280]{1,0:T(8,128)(2,1)}, bf16[256,1280]{1,0:T(8,128)(2,1)}, u32[]{:S(2)}, u32[]{:S(2)}) %collective-permute-start.70) | collective-permute-done | bytes 655392 | tf_op jit(solution)/shard_map/ppermute | solution.py:65
  1044.7 4.4 shard_map.216
  1049.1 5.4 shard_map.215
  1061.8 4.7 shard_map.214
  1068.2 6.8 shard_map.213
  1079.1 9.5 collective-permute-start.84
  1100.8 10.8 collective-permute-done.84
  1111.5 14.5 %collective-permute-done.85 = bf16[128,2048]{1,0:T(8,128)(2,1)S(1)} collective-permute-done((bf16[128,2048]{1,0:T(8,128)(2,1)S(1)}, bf16[128,2048]{1,0:T(8,128)(2,1)S(1)}, u32[]{:S(2)}, u32[]{:S(2)}) %collective-permute-start.85) | collective-permute-done | bytes 524320 | tf_op jit(solution)/shard_map/ppermute | solution.py:65
  1130.2 11.4 collective-permute-start.91
  (567 shorter events, 364.7 us)
Async XLA Ops:
  6.1 95.2 %collective-permute-start.1 = (bf16[192,1280]{1,0:T(8,128)(2,1)}, bf16[192,1280]{1,0:T(8,128)(2,1)S(1)}, u32[]{:S(2)}, u32[]{:S(2)}) collective-permute-start(bf16[192,1280]{1,0:T(8,128)(2,1)} %pad_maximum_fusion.19), channel_id=1, source_target_pairs={{0,8},{4,12},{8,0},{12,4},{16,24},{20,28},{24,16},{28,20},{1,9},{5... | collective-permute-start | bytes 1474568 | tf_op jit(solution)/shard_map/ppermute | solution.py:65
  9.1 88.1 %collective-permute-start.5 = (bf16[192,1280]{1,0:T(8,128)(2,1)}, bf16[192,1280]{1,0:T(8,128)(2,1)}, u32[]{:S(2)}, u32[]{:S(2)}) collective-permute-start(bf16[192,1280]{1,0:T(8,128)(2,1)} %pad_maximum_fusion.19), channel_id=1, source_target_pairs={{0,24},{4,28},{8,16},{12,20},{16,8},{20,12},{24,0},{28,4},{1,25},{... | collective-permute-start | bytes 1474568 | tf_op jit(solution)/shard_map/ppermute | solution.py:65
  11.6 87.1 %collective-permute-start.3 = (bf16[192,1280]{1,0:T(8,128)(2,1)}, bf16[192,1280]{1,0:T(8,128)(2,1)}, u32[]{:S(2)}, u32[]{:S(2)}) collective-permute-start(bf16[192,1280]{1,0:T(8,128)(2,1)} %pad_maximum_fusion.19), channel_id=1, source_target_pairs={{0,16},{4,20},{8,24},{12,28},{16,0},{20,4},{24,8},{28,12},{1,17},{... | collective-permute-start | bytes 1474568 | tf_op jit(solution)/shard_map/ppermute | solution.py:65
  12.5 40.2 %collective-permute-start.16 = (bf16[176,1024]{1,0:T(8,128)(2,1)}, bf16[176,1024]{1,0:T(8,128)(2,1)S(1)}, u32[]{:S(2)}, u32[]{:S(2)}) collective-permute-start(bf16[176,1024]{1,0:T(8,128)(2,1)} %pad_maximum_fusion.23), channel_id=1, source_target_pairs={{0,24},{4,28},{8,16},{12,20},{16,8},{20,12},{24,0},{28,4},{1,25},{... | collective-permute-start | bytes 1081352 | tf_op jit(solution)/shard_map/ppermute | solution.py:65
  15.4 70.0 %collective-permute-start.14 = (bf16[176,1024]{1,0:T(8,128)(2,1)}, bf16[176,1024]{1,0:T(8,128)(2,1)S(1)}, u32[]{:S(2)}, u32[]{:S(2)}) collective-permute-start(bf16[176,1024]{1,0:T(8,128)(2,1)} %pad_maximum_fusion.23), channel_id=1, source_target_pairs={{0,16},{4,20},{8,24},{12,28},{16,0},{20,4},{24,8},{28,12},{1,17},{... | collective-permute-start | bytes 1081352 | tf_op jit(solution)/shard_map/ppermute | solution.py:65
  52.8 40.1 %collective-permute-start.12 = (bf16[176,1024]{1,0:T(8,128)(2,1)}, bf16[176,1024]{1,0:T(8,128)(2,1)S(1)}, u32[]{:S(2)}, u32[]{:S(2)}) collective-permute-start(bf16[176,1024]{1,0:T(8,128)(2,1)} %pad_maximum_fusion.23), channel_id=1, source_target_pairs={{0,8},{4,12},{8,0},{12,4},{16,24},{20,28},{24,16},{28,20},{1,9},{5... | collective-permute-start | bytes 1081352 | tf_op jit(solution)/shard_map/ppermute | solution.py:65
  94.9 152.2 %collective-permute-start.37 = (bf16[128,2048]{1,0:T(8,128)(2,1)}, bf16[128,2048]{1,0:T(8,128)(2,1)}, u32[]{:S(2)}, u32[]{:S(2)}) collective-permute-start(bf16[128,2048]{1,0:T(8,128)(2,1)} %get-tuple-element.300), channel_id=1, source_target_pairs={{0,4},{4,0},{8,12},{12,8},{16,20},{20,16},{24,28},{28,24},{1,5},{5... | collective-permute-start | bytes 1572872 | tf_op jit(solution)/shard_map/ppermute | solution.py:65
  97.2 77.1 %collective-permute-start.13 = (bf16[176,1024]{1,0:T(8,128)(2,1)S(1)}, bf16[176,1024]{1,0:T(8,128)(2,1)S(1)}, u32[]{:S(2)}, u32[]{:S(2)}) collective-permute-start(bf16[176,1024]{1,0:T(8,128)(2,1)S(1)} %collective-permute-done.12.refs_2_), channel_id=1, source_target_pairs={{0,4},{4,0},{8,12},{12,8},{16,20},{20,16},{24,28},{28,24},{1,5},{5... | collective-permute-start | bytes 1081352 | tf_op jit(solution)/shard_map/ppermute | solution.py:65
  98.7 35.1 %collective-permute-start.17 = (bf16[176,1024]{1,0:T(8,128)(2,1)S(1)}, bf16[176,1024]{1,0:T(8,128)(2,1)S(1)}, u32[]{:S(2)}, u32[]{:S(2)}) collective-permute-start(bf16[176,1024]{1,0:T(8,128)(2,1)S(1)} %collective-permute-done.16.refs_6_), channel_id=1, source_target_pairs={{0,4},{4,0},{8,12},{12,8},{16,20},{20,16},{24,28},{28,24},{1,5},{5... | collective-permute-start | bytes 1081352 | tf_op jit(solution)/shard_map/ppermute | solution.py:65
  101.3 40.3 %collective-permute-start.15 = (bf16[176,1024]{1,0:T(8,128)(2,1)S(1)}, bf16[176,1024]{1,0:T(8,128)(2,1)S(1)}, u32[]{:S(2)}, u32[]{:S(2)}) collective-permute-start(bf16[176,1024]{1,0:T(8,128)(2,1)S(1)} %collective-permute-done.14.refs_4_), channel_id=1, source_target_pairs={{0,4},{4,0},{8,12},{12,8},{16,20},{20,16},{24,28},{28,24},{1,5},{5... | collective-permute-start | bytes 1081352 | tf_op jit(solution)/shard_map/ppermute | solution.py:65
  107.1 44.9 %collective-permute-start.2 = (bf16[192,1280]{1,0:T(8,128)(2,1)S(1)}, bf16[192,1280]{1,0:T(8,128)(2,1)S(1)}, u32[]{:S(2)}, u32[]{:S(2)}) collective-permute-start(bf16[192,1280]{1,0:T(8,128)(2,1)S(1)} %collective-permute-done.1.refs_2_), channel_id=1, source_target_pairs={{0,4},{4,0},{8,12},{12,8},{16,20},{20,16},{24,28},{28,24},{1,5},{5... | collective-permute-start | bytes 1474568 | tf_op jit(solution)/shard_map/ppermute | solution.py:65
  133.8 41.9 %collective-permute-start.7 = (bf16[2,80,1280]{2,1,0:T(8,128)(2,1)S(1)}, bf16[2,80,1280]{2,1,0:T(8,128)(2,1)S(1)}, u32[]{:S(2)}, u32[]{:S(2)}) collective-permute-start(bf16[2,80,1280]{2,1,0:T(8,128)(2,1)S(1)} %pad_maximum_fusion.21), channel_id=1, source_target_pairs={{0,2},{2,0},{1,3},{3,1},{4,6},{6,4},{5,7},{7,5},{8,10},{10,8},{9,1... | collective-permute-start | bytes 1228808 | tf_op jit(solution)/shard_map/ppermute | solution.py:65
  174.3 49.5 %collective-permute-start.18 = (bf16[2,80,1024]{2,1,0:T(8,128)(2,1)}, bf16[2,80,1024]{2,1,0:T(8,128)(2,1)}, u32[]{:S(2)}, u32[]{:S(2)}) collective-permute-start(bf16[2,80,1024]{2,1,0:T(8,128)(2,1)} %pad_maximum_fusion.36), channel_id=1, source_target_pairs={{0,2},{2,0},{1,3},{3,1},{4,6},{6,4},{5,7},{7,5},{8,10},{10,8},{9,1... | collective-permute-start | bytes 983048 | tf_op jit(solution)/shard_map/ppermute | solution.py:65
  175.8 52.4 %collective-permute-start.19 = (bf16[3,80,1024]{2,1,0:T(8,128)(2,1)}, bf16[3,80,1024]{2,1,0:T(8,128)(2,1)}, u32[]{:S(2)}, u32[]{:S(2)}) collective-permute-start(bf16[3,80,1024]{2,1,0:T(8,128)(2,1)} %pad_maximum_fusion.20), channel_id=1, source_target_pairs={{0,2},{2,0},{1,3},{3,1},{4,6},{6,4},{5,7},{7,5},{8,10},{10,8},{9,1... | collective-permute-start | bytes 1474568 | tf_op jit(solution)/shard_map/ppermute | solution.py:65
  187.3 38.8 %collective-permute-start.20 = (bf16[2,80,1024]{2,1,0:T(8,128)(2,1)}, bf16[2,80,1024]{2,1,0:T(8,128)(2,1)}, u32[]{:S(2)}, u32[]{:S(2)}) collective-permute-start(bf16[2,80,1024]{2,1,0:T(8,128)(2,1)} %pad_maximum_fusion.37), channel_id=1, source_target_pairs={{0,2},{2,0},{1,3},{3,1},{4,6},{6,4},{5,7},{7,5},{8,10},{10,8},{9,1... | collective-permute-start | bytes 983048 | tf_op jit(solution)/shard_map/ppermute | solution.py:65
  223.8 36.5 %collective-permute-start.40 = (bf16[128,2048]{1,0:T(8,128)(2,1)}, bf16[128,2048]{1,0:T(8,128)(2,1)}, u32[]{:S(2)}, u32[]{:S(2)}) collective-permute-start(bf16[128,2048]{1,0:T(8,128)(2,1)} %get-tuple-element.300), channel_id=1, source_target_pairs={{0,16},{4,20},{8,24},{12,28},{16,0},{20,4},{24,8},{28,12},{1,17},{... | collective-permute-start | bytes 1572872 | tf_op jit(solution)/shard_map/ppermute | solution.py:65
  226.1 35.7 %collective-permute-start.42 = (bf16[128,2048]{1,0:T(8,128)(2,1)}, bf16[128,2048]{1,0:T(8,128)(2,1)}, u32[]{:S(2)}, u32[]{:S(2)}) collective-permute-start(bf16[128,2048]{1,0:T(8,128)(2,1)} %get-tuple-element.300), channel_id=1, source_target_pairs={{0,24},{4,28},{8,16},{12,20},{16,8},{20,12},{24,0},{28,4},{1,25},{... | collective-permute-start | bytes 1572872 | tf_op jit(solution)/shard_map/ppermute | solution.py:65
  247.2 104.7 %collective-permute-start.29 = (bf16[4,3,176,256]{3,2,1,0:T(8,128)(2,1)}, bf16[4,3,176,256]{3,2,1,0:T(8,128)(2,1)}, u32[]{:S(2)}, u32[]{:S(2)}) collective-permute-start(bf16[4,3,176,256]{3,2,1,0:T(8,128)(2,1)} %pad_maximum_fusion.5), channel_id=1, source_target_pairs={{0,4},{4,0},{8,12},{12,8},{16,20},{20,16},{24,28},{28,24},{1,5},{5... | collective-permute-start | bytes 3244040 | tf_op jit(solution)/shard_map/ppermute | solution.py:65
  260.3 33.7 %collective-permute-start.41 = (bf16[128,2048]{1,0:T(8,128)(2,1)}, bf16[128,2048]{1,0:T(8,128)(2,1)S(1)}, u32[]{:S(2)}, u32[]{:S(2)}) collective-permute-start(bf16[128,2048]{1,0:T(8,128)(2,1)} %collective-permute-done.40), channel_id=1, source_target_pairs={{0,4},{4,0},{8,12},{12,8},{16,20},{20,16},{24,28},{28,24},{1,5},{5... | collective-permute-start | bytes 1572872 | tf_op jit(solution)/shard_map/ppermute | solution.py:65
  261.8 43.4 %collective-permute-start.43 = (bf16[128,2048]{1,0:T(8,128)(2,1)}, bf16[128,2048]{1,0:T(8,128)(2,1)S(1)}, u32[]{:S(2)}, u32[]{:S(2)}) collective-permute-start(bf16[128,2048]{1,0:T(8,128)(2,1)} %collective-permute-done.42), channel_id=1, source_target_pairs={{0,4},{4,0},{8,12},{12,8},{16,20},{20,16},{24,28},{28,24},{1,5},{5... | collective-permute-start | bytes 1572872 | tf_op jit(solution)/shard_map/ppermute | solution.py:65
  294.0 35.9 %collective-permute-start.25 = (bf16[128,2048]{1,0:T(8,128)(2,1)S(1)}, bf16[128,2048]{1,0:T(8,128)(2,1)S(1)}, u32[]{:S(2)}, u32[]{:S(2)}) collective-permute-start(bf16[128,2048]{1,0:T(8,128)(2,1)S(1)} %get-tuple-element.302), channel_id=1, source_target_pairs={{0,16},{4,20},{8,24},{12,28},{16,0},{20,4},{24,8},{28,12},{1,17},{... | collective-permute-start | bytes 1572872 | tf_op jit(solution)/shard_map/ppermute | solution.py:65
  316.4 141.0 %collective-permute-start.45 = (bf16[1024,2048]{1,0:T(8,128)(2,1)}, bf16[1024,2048]{1,0:T(8,128)(2,1)}, u32[]{:S(2)}, u32[]{:S(2)}) collective-permute-start(bf16[1024,2048]{1,0:T(8,128)(2,1)} %constant_dynamic-update-slice_fusion.13), channel_id=1, source_target_pairs={{0,1},{1,0},{2,3},{3,2},{4,5},{5,4},{6,7},{7,6},{8,9},{9,8},{10,11... | collective-permute-start | bytes 12582920 | tf_op jit(solution)/shard_map/ppermute | solution.py:65
  350.5 111.8 %collective-permute-start.44 = (bf16[1024,2048]{1,0:T(8,128)(2,1)}, bf16[1024,2048]{1,0:T(8,128)(2,1)}, u32[]{:S(2)}, u32[]{:S(2)}) collective-permute-start(bf16[1024,2048]{1,0:T(8,128)(2,1)} %constant_dynamic-update-slice_fusion.5.normed_ref), channel_id=1, source_target_pairs={{0,1},{1,0},{2,3},{3,2},{4,5},{5,4},{6,7},{7,6},{8,9},{9,8},{10,11... | collective-permute-start | bytes 12582920 | tf_op jit(solution)/shard_map/ppermute | solution.py:65
  356.5 47.1 %collective-permute-start.31 = (bf16[2,3,176,256]{3,2,1,0:T(8,128)(2,1)}, bf16[2,3,176,256]{3,2,1,0:T(8,128)(2,1)S(1)}, u32[]{:S(2)}, u32[]{:S(2)}) collective-permute-start(bf16[2,3,176,256]{3,2,1,0:T(8,128)(2,1)} %pad_maximum_fusion.17), channel_id=1, source_target_pairs={{0,16},{4,20},{8,24},{12,28},{16,0},{20,4},{24,8},{28,12},{1,17},{... | collective-permute-start | bytes 1622024 | tf_op jit(solution)/shard_map/ppermute | solution.py:65
  357.7 48.4 %collective-permute-start.30 = (bf16[2,3,176,256]{3,2,1,0:T(8,128)(2,1)}, bf16[2,3,176,256]{3,2,1,0:T(8,128)(2,1)}, u32[]{:S(2)}, u32[]{:S(2)}) collective-permute-start(bf16[2,3,176,256]{3,2,1,0:T(8,128)(2,1)} %pad_maximum_fusion.16), channel_id=1, source_target_pairs={{0,8},{4,12},{8,0},{12,4},{16,24},{20,28},{24,16},{28,20},{1,9},{5... | collective-permute-start | bytes 1622024 | tf_op jit(solution)/shard_map/ppermute | solution.py:65
  371.3 36.3 %collective-permute-start.33 = (bf16[2,3,176,256]{3,2,1,0:T(8,128)(2,1)S(1)}, bf16[2,3,176,256]{3,2,1,0:T(8,128)(2,1)}, u32[]{:S(2)}, u32[]{:S(2)}) collective-permute-start(bf16[2,3,176,256]{3,2,1,0:T(8,128)(2,1)S(1)} %pad_maximum_fusion.15.refs_0_), channel_id=1, source_target_pairs={{0,2},{2,0},{1,3},{3,1},{4,6},{6,4},{5,7},{7,5},{8,10},{10,8},{9,1... | collective-permute-start | bytes 1622024 | tf_op jit(solution)/shard_map/ppermute | solution.py:65
  480.7 98.2 %collective-permute-start.116 = (f32[176,2048]{1,0:T(8,128)}, f32[176,2048]{1,0:T(8,128)}, u32[]{:S(2)}, u32[]{:S(2)}) collective-permute-start(f32[176,2048]{1,0:T(8,128)} %get-tuple-element.286), channel_id=1, source_target_pairs={{0,2},{2,0},{1,3},{3,1},{4,6},{6,4},{5,7},{7,5},{8,10},{10,8},{9,1... | collective-permute-start | bytes 4325384 | tf_op jit(solution)/shard_map/ppermute | solution.py:65
  496.1 50.3 %collective-permute-start.106 = (f32[176,2048]{1,0:T(8,128)}, f32[176,2048]{1,0:T(8,128)}, u32[]{:S(2)}, u32[]{:S(2)}) collective-permute-start(f32[176,2048]{1,0:T(8,128)} %get-tuple-element.276), channel_id=1, source_target_pairs={{0,2},{2,0},{1,3},{3,1},{4,6},{6,4},{5,7},{7,5},{8,10},{10,8},{9,1... | collective-permute-start | bytes 4325384 | tf_op jit(solution)/shard_map/ppermute | solution.py:65
  496.6 78.2 %collective-permute-start.107 = (f32[176,2048]{1,0:T(8,128)}, f32[176,2048]{1,0:T(8,128)}, u32[]{:S(2)}, u32[]{:S(2)}) collective-permute-start(f32[176,2048]{1,0:T(8,128)} %get-tuple-element.279), channel_id=1, source_target_pairs={{0,2},{2,0},{1,3},{3,1},{4,6},{6,4},{5,7},{7,5},{8,10},{10,8},{9,1... | collective-permute-start | bytes 4325384 | tf_op jit(solution)/shard_map/ppermute | solution.py:65
  502.0 90.5 %collective-permute-start.46 = (f32[1024,512]{1,0:T(8,128)}, f32[1024,512]{1,0:T(8,128)}, u32[]{:S(2)}, u32[]{:S(2)}) collective-permute-start(f32[1024,512]{1,0:T(8,128)} %fusion.27), channel_id=1, source_target_pairs={{0,1},{1,0},{2,3},{3,2},{4,5},{5,4},{6,7},{7,6},{8,9},{9,8},{10,11... | collective-permute-start | bytes 6291464 | tf_op jit(solution)/shard_map/ppermute | solution.py:65
  506.1 89.8 %collective-permute-start.51 = (f32[1024,512]{1,0:T(8,128)}, f32[1024,512]{1,0:T(8,128)}, u32[]{:S(2)}, u32[]{:S(2)}) collective-permute-start(f32[1024,512]{1,0:T(8,128)} %fusion.24), channel_id=1, source_target_pairs={{0,1},{1,0},{2,3},{3,2},{4,5},{5,4},{6,7},{7,6},{8,9},{9,8},{10,11... | collective-permute-start | bytes 6291464 | tf_op jit(solution)/shard_map/ppermute | solution.py:65
  546.4 53.6 %collective-permute-start.56 = (f32[1024,512]{1,0:T(8,128)}, f32[1024,512]{1,0:T(8,128)}, u32[]{:S(2)}, u32[]{:S(2)}) collective-permute-start(f32[1024,512]{1,0:T(8,128)} %fusion.21), channel_id=1, source_target_pairs={{0,1},{1,0},{2,3},{3,2},{4,5},{5,4},{6,7},{7,6},{8,9},{9,8},{10,11... | collective-permute-start | bytes 6291464 | tf_op jit(solution)/shard_map/ppermute | solution.py:65
  578.9 224.4 %collective-permute-start.82 = (bf16[1024,2048]{1,0:T(8,128)(2,1)}, bf16[1024,2048]{1,0:T(8,128)(2,1)}, u32[]{:S(2)}, u32[]{:S(2)}) collective-permute-start(bf16[1024,2048]{1,0:T(8,128)(2,1)} %convolution_convert_fusion), channel_id=1, source_target_pairs={{0,1},{1,0},{2,3},{3,2},{4,5},{5,4},{6,7},{7,6},{8,9},{9,8},{10,11... | collective-permute-start | bytes 12582920 | tf_op jit(solution)/shard_map/ppermute | solution.py:65
  595.9 46.6 %collective-permute-start.108 = (f32[4,2,176,256]{3,2,1,0:T(8,128)S(1)}, f32[4,2,176,256]{3,2,1,0:T(8,128)S(1)}, u32[]{:S(2)}, u32[]{:S(2)}) collective-permute-start(f32[4,2,176,256]{3,2,1,0:T(8,128)S(1)} %pad_maximum_fusion.3), channel_id=1, source_target_pairs={{0,4},{4,0},{8,12},{12,8},{16,20},{20,16},{24,28},{28,24},{1,5},{5... | collective-permute-start | bytes 4325384 | tf_op jit(solution)/shard_map/ppermute | solution.py:65
  600.0 64.9 %collective-permute-start.47 = (f32[4,128,512]{2,1,0:T(8,128)S(1)}, f32[4,128,512]{2,1,0:T(8,128)S(1)}, u32[]{:S(2)}, u32[]{:S(2)}) collective-permute-start(f32[4,128,512]{2,1,0:T(8,128)S(1)} %slice_bitcast_fusion.7), channel_id=1, source_target_pairs={{0,4},{4,0},{8,12},{12,8},{16,20},{20,16},{24,28},{28,24},{1,5},{5... | collective-permute-start | bytes 3145736 | tf_op jit(solution)/shard_map/ppermute | solution.py:65
  603.3 84.1 %collective-permute-start.52 = (f32[4,128,512]{2,1,0:T(8,128)S(1)}, f32[4,128,512]{2,1,0:T(8,128)S(1)}, u32[]{:S(2)}, u32[]{:S(2)}) collective-permute-start(f32[4,128,512]{2,1,0:T(8,128)S(1)} %slice_bitcast_fusion.5), channel_id=1, source_target_pairs={{0,4},{4,0},{8,12},{12,8},{16,20},{20,16},{24,28},{28,24},{1,5},{5... | collective-permute-start | bytes 3145736 | tf_op jit(solution)/shard_map/ppermute | solution.py:65
  611.6 98.3 %collective-permute-start.57 = (f32[4,128,512]{2,1,0:T(8,128)S(1)}, f32[4,128,512]{2,1,0:T(8,128)S(1)}, u32[]{:S(2)}, u32[]{:S(2)}) collective-permute-start(f32[4,128,512]{2,1,0:T(8,128)S(1)} %slice_bitcast_fusion.3), channel_id=1, source_target_pairs={{0,4},{4,0},{8,12},{12,8},{16,20},{20,16},{24,28},{28,24},{1,5},{5... | collective-permute-start | bytes 3145736 | tf_op jit(solution)/shard_map/ppermute | solution.py:65
  642.5 89.4 %collective-permute-start.62 = (f32[4,128,512]{2,1,0:T(8,128)S(1)}, f32[4,128,512]{2,1,0:T(8,128)S(1)}, u32[]{:S(2)}, u32[]{:S(2)}) collective-permute-start(f32[4,128,512]{2,1,0:T(8,128)S(1)} %slice_bitcast_fusion.1), channel_id=1, source_target_pairs={{0,4},{4,0},{8,12},{12,8},{16,20},{20,16},{24,28},{28,24},{1,5},{5... | collective-permute-start | bytes 3145736 | tf_op jit(solution)/shard_map/ppermute | solution.py:65
  665.2 66.9 %collective-permute-start.48 = (f32[128,512]{1,0:T(8,128)S(1)}, f32[128,512]{1,0:T(8,128)S(1)}, u32[]{:S(2)}, u32[]{:S(2)}) collective-permute-start(f32[128,512]{1,0:T(8,128)S(1)} %get-tuple-element.371), channel_id=1, source_target_pairs={{0,8},{4,12},{8,0},{12,4},{16,24},{20,28},{24,16},{28,20},{1,9},{5... | collective-permute-start | bytes 786440 | tf_op jit(solution)/shard_map/ppermute | solution.py:65
  687.4 47.2 %collective-permute-start.49 = (f32[128,512]{1,0:T(8,128)S(1)}, f32[128,512]{1,0:T(8,128)S(1)}, u32[]{:S(2)}, u32[]{:S(2)}) collective-permute-start(f32[128,512]{1,0:T(8,128)S(1)} %get-tuple-element.373), channel_id=1, source_target_pairs={{0,16},{4,20},{8,24},{12,28},{16,0},{20,4},{24,8},{28,12},{1,17},{... | collective-permute-start | bytes 786440 | tf_op jit(solution)/shard_map/ppermute | solution.py:65
  736.7 34.2 %collective-permute-start.58 = (f32[128,512]{1,0:T(8,128)S(1)}, f32[128,512]{1,0:T(8,128)S(1)}, u32[]{:S(2)}, u32[]{:S(2)}) collective-permute-start(f32[128,512]{1,0:T(8,128)S(1)} %get-tuple-element.377), channel_id=1, source_target_pairs={{0,8},{4,12},{8,0},{12,4},{16,24},{20,28},{24,16},{28,20},{1,9},{5... | collective-permute-start | bytes 786440 | tf_op jit(solution)/shard_map/ppermute | solution.py:65
  746.5 38.0 %collective-permute-start.59 = (f32[128,512]{1,0:T(8,128)S(1)}, f32[128,512]{1,0:T(8,128)S(1)}, u32[]{:S(2)}, u32[]{:S(2)}) collective-permute-start(f32[128,512]{1,0:T(8,128)S(1)} %get-tuple-element.379), channel_id=1, source_target_pairs={{0,16},{4,20},{8,24},{12,28},{16,0},{20,4},{24,8},{28,12},{1,17},{... | collective-permute-start | bytes 786440 | tf_op jit(solution)/shard_map/ppermute | solution.py:65
  755.4 36.5 %collective-permute-start.63 = (f32[128,512]{1,0:T(8,128)S(1)}, f32[128,512]{1,0:T(8,128)S(1)}, u32[]{:S(2)}, u32[]{:S(2)}) collective-permute-start(f32[128,512]{1,0:T(8,128)S(1)} %get-tuple-element.380), channel_id=1, source_target_pairs={{0,8},{4,12},{8,0},{12,4},{16,24},{20,28},{24,16},{28,20},{1,9},{5... | collective-permute-start | bytes 786440 | tf_op jit(solution)/shard_map/ppermute | solution.py:65
  786.4 52.1 %collective-permute-start.79 = (bf16[256,1024]{1,0:T(8,128)(2,1)}, bf16[256,1024]{1,0:T(8,128)(2,1)S(1)}, u32[]{:S(2)}, u32[]{:S(2)}) collective-permute-start(bf16[256,1024]{1,0:T(8,128)(2,1)} %get-tuple-element.268.left_ref.refs_0_), channel_id=1, source_target_pairs={{0,8},{4,12},{8,0},{12,4},{16,24},{20,28},{24,16},{28,20},{1,9},{5... | collective-permute-start | bytes 1572872 | tf_op jit(solution)/shard_map/ppermute | solution.py:65
  792.0 46.9 %collective-permute-start.77 = (bf16[256,1024]{1,0:T(8,128)(2,1)}, bf16[256,1024]{1,0:T(8,128)(2,1)S(1)}, u32[]{:S(2)}, u32[]{:S(2)}) collective-permute-start(bf16[256,1024]{1,0:T(8,128)(2,1)} %get-tuple-element.268.left_ref.refs_0_), channel_id=1, source_target_pairs={{0,16},{4,20},{8,24},{12,28},{16,0},{20,4},{24,8},{28,12},{1,17},{... | collective-permute-start | bytes 1572872 | tf_op jit(solution)/shard_map/ppermute | solution.py:65
  798.6 33.7 %collective-permute-start.97 = (bf16[2,128,256]{2,1,0:T(8,128)(2,1)S(1)}, bf16[2,128,256]{2,1,0:T(8,128)(2,1)S(1)}, u32[]{:S(2)}, u32[]{:S(2)}) collective-permute-start(bf16[2,128,256]{2,1,0:T(8,128)(2,1)S(1)} %copy-done.80), channel_id=1, source_target_pairs={{0,24},{4,28},{8,16},{12,20},{16,8},{20,12},{24,0},{28,4},{1,25},{... | collective-permute-start | bytes 393224 | tf_op jit(solution)/shard_map/ppermute | solution.py:65
  803.4 33.3 %collective-permute-start.96 = (bf16[2,128,256]{2,1,0:T(8,128)(2,1)S(1)}, bf16[2,128,256]{2,1,0:T(8,128)(2,1)S(1)}, u32[]{:S(2)}, u32[]{:S(2)}) collective-permute-start(bf16[2,128,256]{2,1,0:T(8,128)(2,1)S(1)} %copy-done.79), channel_id=1, source_target_pairs={{0,16},{4,20},{8,24},{12,28},{16,0},{20,4},{24,8},{28,12},{1,17},{... | collective-permute-start | bytes 393224 | tf_op jit(solution)/shard_map/ppermute | solution.py:65
  838.5 36.8 %collective-permute-start.80 = (bf16[256,1024]{1,0:T(8,128)(2,1)S(1)}, bf16[256,1024]{1,0:T(8,128)(2,1)S(1)}, u32[]{:S(2)}, u32[]{:S(2)}) collective-permute-start(bf16[256,1024]{1,0:T(8,128)(2,1)S(1)} %collective-permute-done.79.refs_2_), channel_id=1, source_target_pairs={{0,4},{4,0},{8,12},{12,8},{16,20},{20,16},{24,28},{28,24},{1,5},{5... | collective-permute-start | bytes 1572872 | tf_op jit(solution)/shard_map/ppermute | solution.py:65
  838.9 37.2 %collective-permute-start.78 = (bf16[256,1024]{1,0:T(8,128)(2,1)S(1)}, bf16[256,1024]{1,0:T(8,128)(2,1)S(1)}, u32[]{:S(2)}, u32[]{:S(2)}) collective-permute-start(bf16[256,1024]{1,0:T(8,128)(2,1)S(1)} %collective-permute-done.77.refs_4_), channel_id=1, source_target_pairs={{0,4},{4,0},{8,12},{12,8},{16,20},{20,16},{24,28},{28,24},{1,5},{5... | collective-permute-start | bytes 1572872 | tf_op jit(solution)/shard_map/ppermute | solution.py:65
  840.6 37.8 %collective-permute-start.120 = (f32[2,1,176,256]{3,2,1,0:T(8,128)S(1)}, f32[2,1,176,256]{3,2,1,0:T(8,128)}, u32[]{:S(2)}, u32[]{:S(2)}) collective-permute-start(f32[2,1,176,256]{3,2,1,0:T(8,128)S(1)} %pad_maximum_fusion.35), channel_id=1, source_target_pairs={{0,24},{4,28},{8,16},{12,20},{16,8},{20,12},{24,0},{28,4},{1,25},{... | collective-permute-start | bytes 1081352 | tf_op jit(solution)/shard_map/ppermute | solution.py:65
  853.7 38.4 %collective-permute-start.76 = (bf16[256,1024]{1,0:T(8,128)(2,1)}, bf16[256,1024]{1,0:T(8,128)(2,1)}, u32[]{:S(2)}, u32[]{:S(2)}) collective-permute-start(bf16[256,1024]{1,0:T(8,128)(2,1)} %collective-permute-done.75.refs_6_), channel_id=1, source_target_pairs={{0,4},{4,0},{8,12},{12,8},{16,20},{20,16},{24,28},{28,24},{1,5},{5... | collective-permute-start | bytes 1572872 | tf_op jit(solution)/shard_map/ppermute | solution.py:65
  855.2 35.0 %collective-permute-start.119 = (f32[2,1,176,256]{3,2,1,0:T(8,128)}, f32[2,1,176,256]{3,2,1,0:T(8,128)}, u32[]{:S(2)}, u32[]{:S(2)}) collective-permute-start(f32[2,1,176,256]{3,2,1,0:T(8,128)} %pad_maximum_fusion.34), channel_id=1, source_target_pairs={{0,16},{4,20},{8,24},{12,28},{16,0},{20,4},{24,8},{28,12},{1,17},{... | collective-permute-start | bytes 1081352 | tf_op jit(solution)/shard_map/ppermute | solution.py:65
  892.1 34.3 %collective-permute-start.111 = (f32[2,2,176,256]{3,2,1,0:T(8,128)}, f32[2,2,176,256]{3,2,1,0:T(8,128)}, u32[]{:S(2)}, u32[]{:S(2)}) collective-permute-start(f32[2,2,176,256]{3,2,1,0:T(8,128)} %pad_maximum_fusion.11), channel_id=1, source_target_pairs={{0,24},{4,28},{8,16},{12,20},{16,8},{20,12},{24,0},{28,4},{1,25},{... | collective-permute-start | bytes 2162696 | tf_op jit(solution)/shard_map/ppermute | solution.py:65
  895.0 64.4 %collective-permute-start.110 = (f32[2,2,176,256]{3,2,1,0:T(8,128)}, f32[2,2,176,256]{3,2,1,0:T(8,128)}, u32[]{:S(2)}, u32[]{:S(2)}) collective-permute-start(f32[2,2,176,256]{3,2,1,0:T(8,128)} %pad_maximum_fusion.10), channel_id=1, source_target_pairs={{0,16},{4,20},{8,24},{12,28},{16,0},{20,4},{24,8},{28,12},{1,17},{... | collective-permute-start | bytes 2162696 | tf_op jit(solution)/shard_map/ppermute | solution.py:65
  895.1 64.4 %collective-permute-start.109 = (f32[2,2,176,256]{3,2,1,0:T(8,128)}, f32[2,2,176,256]{3,2,1,0:T(8,128)}, u32[]{:S(2)}, u32[]{:S(2)}) collective-permute-start(f32[2,2,176,256]{3,2,1,0:T(8,128)} %pad_maximum_fusion.9), channel_id=1, source_target_pairs={{0,8},{4,12},{8,0},{12,4},{16,24},{20,28},{24,16},{28,20},{1,9},{5... | collective-permute-start | bytes 2162696 | tf_op jit(solution)/shard_map/ppermute | solution.py:65
  902.2 59.5 %collective-permute-start.112 = (f32[2,2,176,256]{3,2,1,0:T(8,128)S(1)}, f32[2,2,176,256]{3,2,1,0:T(8,128)}, u32[]{:S(2)}, u32[]{:S(2)}) collective-permute-start(f32[2,2,176,256]{3,2,1,0:T(8,128)S(1)} %pad_maximum_fusion.8.refs_0_), channel_id=1, source_target_pairs={{0,2},{2,0},{1,3},{3,1},{4,6},{6,4},{5,7},{7,5},{8,10},{10,8},{9,1... | collective-permute-start | bytes 2162696 | tf_op jit(solution)/shard_map/ppermute | solution.py:65
  926.4 60.9 %collective-permute-start.115 = (f32[2,2,176,256]{3,2,1,0:T(8,128)}, f32[2,2,176,256]{3,2,1,0:T(8,128)S(1)}, u32[]{:S(2)}, u32[]{:S(2)}) collective-permute-start(f32[2,2,176,256]{3,2,1,0:T(8,128)} %collective-permute-done.111.refs_3_), channel_id=1, source_target_pairs={{0,2},{2,0},{1,3},{3,1},{4,6},{6,4},{5,7},{7,5},{8,10},{10,8},{9,1... | collective-permute-start | bytes 2162696 | tf_op jit(solution)/shard_map/ppermute | solution.py:65
  968.7 106.6 %collective-permute-start.83 = (bf16[4,128,2048]{2,1,0:T(8,128)(2,1)}, bf16[4,128,2048]{2,1,0:T(8,128)(2,1)}, u32[]{:S(2)}, u32[]{:S(2)}) collective-permute-start(bf16[4,128,2048]{2,1,0:T(8,128)(2,1)} %fusion.8), channel_id=1, source_target_pairs={{0,4},{4,0},{8,12},{12,8},{16,20},{20,16},{24,28},{28,24},{1,5},{5... | collective-permute-start | bytes 6291464 | tf_op jit(solution)/shard_map/ppermute | solution.py:65
  989.2 39.1 %collective-permute-start.74 = (bf16[256,1280]{1,0:T(8,128)(2,1)}, bf16[256,1280]{1,0:T(8,128)(2,1)}, u32[]{:S(2)}, u32[]{:S(2)}) collective-permute-start(bf16[256,1280]{1,0:T(8,128)(2,1)} %shard_map.211.left_ref.refs_0_), channel_id=1, source_target_pairs={{0,4},{4,0},{8,12},{12,8},{16,20},{20,16},{24,28},{28,24},{1,5},{5... | collective-permute-start | bytes 1966088 | tf_op jit(solution)/shard_map/ppermute | solution.py:65
  994.3 46.9 %collective-permute-start.70 = (bf16[256,1280]{1,0:T(8,128)(2,1)}, bf16[256,1280]{1,0:T(8,128)(2,1)}, u32[]{:S(2)}, u32[]{:S(2)}) collective-permute-start(bf16[256,1280]{1,0:T(8,128)(2,1)} %shard_map.211.left_ref.refs_0_), channel_id=1, source_target_pairs={{0,16},{4,20},{8,24},{12,28},{16,0},{20,4},{24,8},{28,12},{1,17},{... | collective-permute-start | bytes 1966088 | tf_op jit(solution)/shard_map/ppermute | solution.py:65
  996.3 45.5 %collective-permute-start.68 = (bf16[256,1280]{1,0:T(8,128)(2,1)}, bf16[256,1280]{1,0:T(8,128)(2,1)}, u32[]{:S(2)}, u32[]{:S(2)}) collective-permute-start(bf16[256,1280]{1,0:T(8,128)(2,1)} %shard_map.211.left_ref.refs_0_), channel_id=1, source_target_pairs={{0,24},{4,28},{8,16},{12,20},{16,8},{20,12},{24,0},{28,4},{1,25},{... | collective-permute-start | bytes 1966088 | tf_op jit(solution)/shard_map/ppermute | solution.py:65
  1028.4 69.5 %collective-permute-start.88 = (f32[256,2048]{1,0:T(8,128)S(1)}, f32[256,2048]{1,0:T(8,128)}, u32[]{:S(2)}, u32[]{:S(2)}) collective-permute-start(f32[256,2048]{1,0:T(8,128)S(1)} %shard_map.212), channel_id=1, source_target_pairs={{0,1},{1,0},{2,3},{3,2},{4,5},{5,4},{6,7},{7,6},{8,9},{9,8},{10,11... | collective-permute-start | bytes 6291464 | tf_op jit(solution)/shard_map/ppermute | solution.py:65
  1075.0 73.6 %collective-permute-start.99 = (f32[256,1280]{1,0:T(8,128)}, f32[256,1280]{1,0:T(8,128)}, u32[]{:S(2)}, u32[]{:S(2)}) collective-permute-start(f32[256,1280]{1,0:T(8,128)} %shard_map.213), channel_id=1, source_target_pairs={{0,2},{2,0},{1,3},{3,1},{4,6},{6,4},{5,7},{7,5},{8,10},{10,8},{9,1... | collective-permute-start | bytes 3932168 | tf_op jit(solution)/shard_map/ppermute | solution.py:65
  1088.6 37.4 %collective-permute-start.85 = (bf16[128,2048]{1,0:T(8,128)(2,1)S(1)}, bf16[128,2048]{1,0:T(8,128)(2,1)S(1)}, u32[]{:S(2)}, u32[]{:S(2)}) collective-permute-start(bf16[128,2048]{1,0:T(8,128)(2,1)S(1)} %get-tuple-element.325), channel_id=1, source_target_pairs={{0,16},{4,20},{8,24},{12,28},{16,0},{20,4},{24,8},{28,12},{1,17},{... | collective-permute-start | bytes 1572872 | tf_op jit(solution)/shard_map/ppermute | solution.py:65
  (151 other events, 2357.8 us)

commit v2 on v1

--- a/solution.py
+++ b/solution.py
@@ -149,11 +149,11 @@
 def owned_kernel(far, count, half_hidden, place_ref, *refs):
     got, other = refs[:far], refs[far : 2 * far]
     outs, rows = refs[2 * far : 2 * far + count], refs[-1]
-    high, low, ctx = place_ref[0], place_ref[1], place_ref[2]
+    me, ctx = place_ref[0], place_ref[2]
     for i in range(count):
         for k in range(far):
             for r in range(2):
-                owner = (high ^ k) * 2 + (low ^ r)
+                owner = me ^ (2 * k + r)
                 first = pl.multiple_of((owner * 2 + ctx) * half_hidden, 8)
                 second = pl.multiple_of((owner * 2 + 1 - ctx) * half_hidden, 8)
                 rows[pl.ds(first, half_hidden), :] = got[k][r, i]
@@ -257,33 +257,34 @@
     return (key <= query) & (key >= query - positions)
 
 
-def attend_kernel(where_ref, positions_ref, query_ref, kv_ref, out_ref, lse_ref):
-    keys = kv_ref.shape[1] // 2
-    groups = keys // HEAD_DIM
+def attend_kernel(where_ref, positions_ref, query_ref, kv_ref, out_ref, lse_ref, key_ref, value_ref):
+    groups = key_ref.shape[0]
+    keys = groups * HEAD_DIM
     pairs = query_ref.shape[1] // 128 // groups
     allowed = allowed_pairs(where_ref[2], positions_ref[...])
     for g in range(groups):
-        key = kv_ref[:, g * HEAD_DIM : (g + 1) * HEAD_DIM]
-        value_t = kv_ref[:, keys + g * HEAD_DIM : keys + (g + 1) * HEAD_DIM].T
-
-        def step(i, carry, g=g, key=key, value_t=value_t):
-            at = g * pairs + i
-            columns = pl.ds(pl.multiple_of(at * 128, 128), 128)
-            query = query_ref[:, columns]
-            attended, sums = [], []
-            for h in range(2):
-                scores = dot_nt(key, query[:, h * HEAD_DIM : (h + 1) * HEAD_DIM])
-                scores = jnp.where(allowed, scores * HEAD_DIM ** (-0.5), NEG_FILL)
-                largest = jnp.max(scores, axis=0, keepdims=True)
-                exponent = jnp.exp(scores - largest)
-                totals = jnp.sum(exponent, axis=0, keepdims=True)
-                attended.append(dot_nn(value_t, (exponent / totals).astype(BF16)))
-                sums.append(largest + jnp.log(totals))
-            out_ref[:, columns] = jnp.concatenate(attended, axis=0).T.astype(BF16)
-            lse_ref[at] = jnp.concatenate(sums, axis=0)
-            return carry
-
-        lax.fori_loop(0, pairs, step, 0)
+        key_ref[g] = kv_ref[:, g * HEAD_DIM : (g + 1) * HEAD_DIM]
+        value_ref[g] = kv_ref[:, keys + g * HEAD_DIM : keys + (g + 1) * HEAD_DIM].T
+
+    def step(at, carry):
+        g = lax.div(at, pairs)
+        key, value_t = key_ref[g], value_ref[g]
+        columns = pl.ds(pl.multiple_of(at * 128, 128), 128)
+        query = query_ref[:, columns]
+        attended, sums = [], []
+        for h in range(2):
+            scores = dot_nt(key, query[:, h * HEAD_DIM : (h + 1) * HEAD_DIM])
+            scores = jnp.where(allowed, scores * HEAD_DIM ** (-0.5), NEG_FILL)
+            largest = jnp.max(scores, axis=0, keepdims=True)
+            exponent = jnp.exp(scores - largest)
+            totals = jnp.sum(exponent, axis=0, keepdims=True)
+            attended.append(dot_nn(value_t, (exponent / totals).astype(BF16)))
+            sums.append(largest + jnp.log(totals))
+        out_ref[:, columns] = jnp.concatenate(attended, axis=0).T.astype(BF16)
+        lse_ref[at] = jnp.concatenate(sums, axis=0)
+        return carry
+
+    lax.fori_loop(0, groups * pairs, step, 0)
 
 
 def attend_back_kernel(
@@ -518,13 +519,17 @@
             jax.ShapeDtypeStruct((rows, query_columns), BF16),
             jax.ShapeDtypeStruct((query_columns // 128, 2, rows), F32),
         ],
-        [],
+        [
+            pltpu.VMEM((key_columns // HEAD_DIM, 2 * rows, HEAD_DIM), BF16),
+            pltpu.VMEM((key_columns // HEAD_DIM, HEAD_DIM, 2 * rows), BF16),
+        ],
         where,
         positions,
         queries,
         kv_all,
     )
     attended_low = fences.cut(attended_low)
+    fences.cut()
     branch, wo_whole = local_kernel(
         functools.partial(project_gathered_kernel, slab, wo_others),
         [
@@ -591,9 +596,8 @@
         ]
         return plane.exchange_near(blocks, low)
 
-    def from_owners(got):
+    def from_owners(got, where):
         other = [plane.swap_ctx(g) for g in got]
-        where = jnp.stack([high, low, ctx]).astype(jnp.int32)
         return owned(got, other, where)
 
     def tp_part(lefts, right, wire):
@@ -719,8 +723,6 @@
     fences.cut()
     grad_qkv = outer(normed_got, [fences.after(b) for b in grad_qkv_all])
     fences.cut()
-    fences.cut()
-    fences.cut()
     scaled_grad_one = grad_normed_one * gain_one
     grad_tokens = (
         grad_residual
@@ -729,15 +731,17 @@
         * (rms_one * rms_one * rms_one)
         * jnp.mean(scaled_grad_one * tokens, axis=-1, keepdims=True)
     )
-
     output_grad = grad_wo + plane.swap_ctx(grad_wo)
+    (down_grad,) = from_owners(down_got, where)
+    grad_tokens, output_grad, down_grad = fences.cut(grad_tokens, output_grad, down_grad)
+    fences.cut()
     block_out = (fences.after(residual) + whole_rows(mlp_mine)).astype(BF16)
     grad_qkv = grad_qkv + plane.swap_ctx(grad_qkv)
+    block_out, grad_qkv, last = lax.optimization_barrier((block_out, grad_qkv, where))
     query_grad = grad_qkv[:, :query_columns]
     key_grad = grad_qkv[:, query_columns : query_columns + key_columns]
     value_grad = grad_qkv[:, query_columns + key_columns :]
-    (down_grad,) = from_owners(down_got)
-    gate_grad, up_grad = from_owners(gate_up_got)
+    gate_grad, up_grad = from_owners(gate_up_got, last)
 
     gain_sums = lax.dynamic_slice_in_dim(gain_sums, me * slab, slab, 1)
     gain_sums = jnp.where(fences.value > 0, gain_sums, 0.0)

time: 1170 us -> 1270 us (1.085)
  waiting for transfers between devices: 609 us -> 661 us
  starting transfers between devices: 237 us -> 277 us
    ppermute x125, waiting for transfers between devices: 609 us -> 661 us  [send(): return lax.ppermute(array, axis, pairs)]
    ppermute x125, starting transfers between devices: 237 us -> 277 us  [send(): return lax.ppermute(array, axis, pairs)]
    unnamed x201 -> x231, local copies, waits for them, and re-layouts: 65.4 us -> 73.4 us
  transfers between devices with their start and end apart: 125 -> 125, of which waited for: 53 -> 55; matrix products, arithmetic and copies ran while one was open for 15% -> 14% of each run, Pallas kernels for 6% -> 5%
where the time goes in v2:
time: 1270 us; the launch traced here: 1260 us
  waiting for transfers between devices  661 us (52%)
  starting transfers between devices  277 us (22%)
  local copies, waits for them, and re-layouts  108 us (9%)
  other arithmetic  73.5 us (6%)
  Pallas kernels  70 us (6%)
  matrix products  66.3 us (5%)
    ppermute x125, waiting for transfers between devices, send(): return lax.ppermute(array, axis, pairs)  661 us
    ppermute x125, starting transfers between devices, send(): return lax.ppermute(array, axis, pairs)  277 us
    unnamed x231, local copies, waits for them, and re-layouts  73.4 us
    pallas_call x14, Pallas kernels, local_kernel(): pl.pallas_call(kernel, out_shape=outs, in_specs=[SCALARS] + [WHOLE] * (le...  70 us
    dot_general x10, matrix products, dot_nn(): return jnp.dot(left, right, preferred_element_type=F32)  35.6 us
  transfers between devices with their start and end apart: 125, of which 55 were waited for; matrix products, arithmetic and copies ran while one was open for 14% of the time, Pallas kernels for 5%

profile of v2, /device:TPU:0, one launch (start us, length us, event | category | flops | bytes accessed | tf_op | source)
XLA Modules:
  0.0 1258.3 jit_solution(9512416252103722574)
XLA Ops:
  27.2 25.6 %collective-permute-done.16.refs_6_ = bf16[176,1024]{1,0:T(8,128)(2,1)S(1)} collective-permute-done((bf16[176,1024]{1,0:T(8,128)(2,1)}, bf16[176,1024]{1,0:T(8,128)(2,1)S(1)}, u32[]{:S(2)}, u32[]{:S(2)}) %collective-permute-start.16) | collective-permute-done | bytes 360480 | tf_op jit(solution)/shard_map/ppermute | solution.py:65
  52.8 26.6 %collective-permute-start.12 = (bf16[176,1024]{1,0:T(8,128)(2,1)}, bf16[176,1024]{1,0:T(8,128)(2,1)S(1)}, u32[]{:S(2)}, u32[]{:S(2)}) collective-permute-start(bf16[176,1024]{1,0:T(8,128)(2,1)} %pad_maximum_fusion.23), channel_id=1, source_target_pairs={{0,8},{4,12},{8,0},{12,4},{16,24},{20,28},{24,16},{28,20},{1,9},{5... | collective-permute-start | bytes 1081352 | tf_op jit(solution)/shard_map/ppermute | solution.py:65
  79.4 6.1 collective-permute-done.14.refs_4_
  87.0 5.8 collective-permute-done.12.refs_2_
  101.8 5.3 collective-permute-done.refs_1_
  108.8 25.1 %collective-permute-done.17.refs_7_ = bf16[176,1024]{1,0:T(8,128)(2,1)S(1)} collective-permute-done((bf16[176,1024]{1,0:T(8,128)(2,1)S(1)}, bf16[176,1024]{1,0:T(8,128)(2,1)S(1)}, u32[]{:S(2)}, u32[]{:S(2)}) %collective-permute-start.17) | collective-permute-done | bytes 360480 | tf_op jit(solution)/shard_map/ppermute | solution.py:65
  135.4 6.2 collective-permute-done.15.refs_5_
  143.1 9.0 collective-permute-done.2.refs_3_
  153.7 8.9 collective-permute-done.6.refs_7_
  164.1 7.8 collective-permute-done.4.refs_5_
  177.4 10.0 collective-permute-done.9.refs_10_
  198.4 13.8 %collective-permute-done.10 = bf16[256,256]{1,0:T(8,128)(2,1)S(1)} collective-permute-done((bf16[256,256]{1,0:T(8,128)(2,1)S(1)}, bf16[256,256]{1,0:T(8,128)(2,1)S(1)}, u32[]{:S(2)}, u32[]{:S(2)}) %collective-permute-start.10) | collective-permute-done | bytes 131104 | tf_op jit(solution)/shard_map/ppermute | solution.py:65
  213.4 10.8 shard_map.204
  248.1 12.7 %collective-permute-done.40 = bf16[128,2048]{1,0:T(8,128)(2,1)} collective-permute-done((bf16[128,2048]{1,0:T(8,128)(2,1)}, bf16[128,2048]{1,0:T(8,128)(2,1)}, u32[]{:S(2)}, u32[]{:S(2)}) %collective-permute-start.40) | collective-permute-done | bytes 524320 | tf_op jit(solution)/shard_map/ppermute | solution.py:65
  273.4 10.0 collective-permute-start.23
  285.8 8.6 collective-permute-done.41
  297.2 8.4 collective-permute-done.43
  309.7 7.1 collective-permute-done.22
  316.8 12.5 collective-permute-done.25
  334.7 9.4 collective-permute-done.26
  364.9 7.8 collective-permute-done.32.refs_3_
  372.7 21.8 %collective-permute-start.30 = (bf16[2,3,176,256]{3,2,1,0:T(8,128)(2,1)}, bf16[2,3,176,256]{3,2,1,0:T(8,128)(2,1)}, u32[]{:S(2)}, u32[]{:S(2)}) collective-permute-start(bf16[2,3,176,256]{3,2,1,0:T(8,128)(2,1)} %pad_maximum_fusion.16), channel_id=1, source_target_pairs={{0,8},{4,12},{8,0},{12,4},{16,24},{20,28},{24,16},{28,20},{1,9},{5... | collective-permute-start | bytes 1622024 | tf_op jit(solution)/shard_map/ppermute | solution.py:65
  398.3 7.0 collective-permute-done.31.refs_2_
  407.1 12.5 collective-permute-done.30.refs_1_
  432.4 5.6 collective-permute-done.36.refs_7_
  438.0 11.6 collective-permute-done.35.refs_6_
  449.6 10.1 collective-permute-done.34.refs_5_
  463.0 6.2 fusion.68.grad_act_ref
  469.8 6.5 shard_map.207
  481.2 6.1 shard_map.208
  499.5 5.8 fusion.71
  505.3 5.5 convolution_add_fusion
  524.8 6.0 convolution_convert_fusion
  538.2 10.0 collective-permute-done.115
  548.2 30.9 %collective-permute-done.116 = f32[176,2048]{1,0:T(8,128)} collective-permute-done((f32[176,2048]{1,0:T(8,128)}, f32[176,2048]{1,0:T(8,128)}, u32[]{:S(2)}, u32[]{:S(2)}) %collective-permute-start.116) | collective-permute-done | bytes 1441824 | tf_op jit(solution)/shard_map/ppermute | solution.py:65
  586.0 21.6 %collective-permute-done.89 = f32[176,2048]{1,0:T(8,128)} collective-permute-done((f32[176,2048]{1,0:T(8,128)}, f32[176,2048]{1,0:T(8,128)}, u32[]{:S(2)}, u32[]{:S(2)}) %collective-permute-start.89) | collective-permute-done | bytes 1441824 | tf_op jit(solution)/shard_map/ppermute | solution.py:65
  638.0 19.9 %collective-permute-done.47 = f32[4,128,512]{2,1,0:T(8,128)S(1)} collective-permute-done((f32[4,128,512]{2,1,0:T(8,128)S(1)}, f32[4,128,512]{2,1,0:T(8,128)S(1)}, u32[]{:S(2)}, u32[]{:S(2)}) %collective-permute-start.47) | collective-permute-done | bytes 1048608 | tf_op jit(solution)/shard_map/ppermute | solution.py:65
  658.7 21.6 %collective-permute-done.52 = f32[4,128,512]{2,1,0:T(8,128)S(1)} collective-permute-done((f32[4,128,512]{2,1,0:T(8,128)S(1)}, f32[4,128,512]{2,1,0:T(8,128)S(1)}, u32[]{:S(2)}, u32[]{:S(2)}) %collective-permute-start.52) | collective-permute-done | bytes 1048608 | tf_op jit(solution)/shard_map/ppermute | solution.py:65
  681.7 21.0 %collective-permute-done.57 = f32[4,128,512]{2,1,0:T(8,128)S(1)} collective-permute-done((f32[4,128,512]{2,1,0:T(8,128)S(1)}, f32[4,128,512]{2,1,0:T(8,128)S(1)}, u32[]{:S(2)}, u32[]{:S(2)}) %collective-permute-start.57) | collective-permute-done | bytes 1048608 | tf_op jit(solution)/shard_map/ppermute | solution.py:65
  705.0 19.7 %collective-permute-done.62 = f32[4,128,512]{2,1,0:T(8,128)S(1)} collective-permute-done((f32[4,128,512]{2,1,0:T(8,128)S(1)}, f32[4,128,512]{2,1,0:T(8,128)S(1)}, u32[]{:S(2)}, u32[]{:S(2)}) %collective-permute-start.62) | collective-permute-done | bytes 1048608 | tf_op jit(solution)/shard_map/ppermute | solution.py:65
  729.6 9.5 collective-permute-done.53
  739.2 7.8 collective-permute-done.54
  749.2 15.3 %collective-permute-start.63 = (f32[128,512]{1,0:T(8,128)S(1)}, f32[128,512]{1,0:T(8,128)S(1)}, u32[]{:S(2)}, u32[]{:S(2)}) collective-permute-start(f32[128,512]{1,0:T(8,128)S(1)} %get-tuple-element.394), channel_id=1, source_target_pairs={{0,8},{4,12},{8,0},{12,4},{16,24},{20,28},{24,16},{28,20},{1,9},{5... | collective-permute-start | bytes 786440 | tf_op jit(solution)/shard_map/ppermute | solution.py:65
  765.0 12.9 %collective-permute-done.59 = f32[128,512]{1,0:T(8,128)S(1)} collective-permute-done((f32[128,512]{1,0:T(8,128)S(1)}, f32[128,512]{1,0:T(8,128)S(1)}, u32[]{:S(2)}, u32[]{:S(2)}) %collective-permute-start.59) | collective-permute-done | bytes 262176 | tf_op jit(solution)/shard_map/ppermute | solution.py:65
  814.2 11.9 shard_map.210
  835.3 33.6 %collective-permute-done.83 = bf16[4,128,256]{2,1,0:T(8,128)(2,1)} collective-permute-done((bf16[4,128,256]{2,1,0:T(8,128)(2,1)}, bf16[4,128,256]{2,1,0:T(8,128)(2,1)}, u32[]{:S(2)}, u32[]{:S(2)}) %collective-permute-start.83) | collective-permute-done | bytes 262176 | tf_op jit(solution)/shard_map/ppermute | solution.py:65
  880.1 27.9 %collective-permute-start.85 = (bf16[2,128,256]{2,1,0:T(8,128)(2,1)}, bf16[2,128,256]{2,1,0:T(8,128)(2,1)}, u32[]{:S(2)}, u32[]{:S(2)}) collective-permute-start(bf16[2,128,256]{2,1,0:T(8,128)(2,1)} %pad_maximum_fusion.43), channel_id=1, source_target_pairs={{0,16},{4,20},{8,24},{12,28},{16,0},{20,4},{24,8},{28,12},{1,17},{... | collective-permute-start | bytes 393224 | tf_op jit(solution)/shard_map/ppermute | solution.py:65
  921.4 13.8 %collective-permute-done.76.refs_7_ = bf16[256,1024]{1,0:T(8,128)(2,1)} collective-permute-done((bf16[256,1024]{1,0:T(8,128)(2,1)}, bf16[256,1024]{1,0:T(8,128)(2,1)}, u32[]{:S(2)}, u32[]{:S(2)}) %collective-permute-start.76) | collective-permute-done | bytes 524320 | tf_op jit(solution)/shard_map/ppermute | solution.py:65
  935.2 28.0 %collective-permute-start.92 = (f32[2,1,176,256]{3,2,1,0:T(8,128)S(1)}, f32[2,1,176,256]{3,2,1,0:T(8,128)}, u32[]{:S(2)}, u32[]{:S(2)}) collective-permute-start(f32[2,1,176,256]{3,2,1,0:T(8,128)S(1)} %pad_maximum_fusion.26), channel_id=1, source_target_pairs={{0,16},{4,20},{8,24},{12,28},{16,0},{20,4},{24,8},{28,12},{1,17},{... | collective-permute-start | bytes 1081352 | tf_op jit(solution)/shard_map/ppermute | solution.py:65
  966.4 13.8 %collective-permute-done.92.refs_2_ = f32[2,1,176,256]{3,2,1,0:T(8,128)} collective-permute-done((f32[2,1,176,256]{3,2,1,0:T(8,128)S(1)}, f32[2,1,176,256]{3,2,1,0:T(8,128)}, u32[]{:S(2)}, u32[]{:S(2)}) %collective-permute-start.92) | collective-permute-done | bytes 360480 | tf_op jit(solution)/shard_map/ppermute | solution.py:65
  991.4 5.2 shard_map.213
  999.3 7.7 collective-permute-done.96.refs_6_
  1009.1 5.9 fusion.57
  1021.2 32.4 %collective-permute-done.70.refs_4_ = bf16[256,1280]{1,0:T(8,128)(2,1)S(1)} collective-permute-done((bf16[256,1280]{1,0:T(8,128)(2,1)S(1)}, bf16[256,1280]{1,0:T(8,128)(2,1)S(1)}, u32[]{:S(2)}, u32[]{:S(2)}) %collective-permute-start.70) | collective-permute-done | bytes 655392 | tf_op jit(solution)/shard_map/ppermute | solution.py:65
  1063.0 10.1 collective-permute-start.100
  1074.5 10.7 collective-permute-done.71.refs_5_
  1108.9 5.2 shard_map.215
  1121.9 16.6 %collective-permute-done.111 = f32[2,2048]{1,0:T(2,128)S(1)} collective-permute-done((f32[2,2048]{1,0:T(2,128)S(1)}, f32[2,2048]{1,0:T(2,128)S(1)}, u32[]{:S(2)}, u32[]{:S(2)}) %collective-permute-start.111) | collective-permute-done | bytes 16416 | tf_op jit(solution)/shard_map/ppermute | solution.py:65
  1146.7 21.4 %collective-permute-done.113 = f32[2,2048]{1,0:T(2,128)S(1)} collective-permute-done((f32[2,2048]{1,0:T(2,128)S(1)}, f32[2,2048]{1,0:T(2,128)S(1)}, u32[]{:S(2)}, u32[]{:S(2)}) %collective-permute-start.113) | collective-permute-done | bytes 16416 | tf_op jit(solution)/shard_map/ppermute | solution.py:65
  1177.0 28.3 %collective-permute-done.119.refs_2_ = f32[2,2,176,256]{3,2,1,0:T(8,128)} collective-permute-done((f32[2,2,176,256]{3,2,1,0:T(8,128)}, f32[2,2,176,256]{3,2,1,0:T(8,128)}, u32[]{:S(2)}, u32[]{:S(2)}) %collective-permute-start.119) | collective-permute-done | bytes 720928 | tf_op jit(solution)/shard_map/ppermute | solution.py:65
  1216.0 8.5 collective-permute-done.124.refs_7_
  1224.5 15.4 %collective-permute-done.123.refs_6_ = f32[2,2,176,256]{3,2,1,0:T(8,128)S(1)} collective-permute-done((f32[2,2,176,256]{3,2,1,0:T(8,128)}, f32[2,2,176,256]{3,2,1,0:T(8,128)S(1)}, u32[]{:S(2)}, u32[]{:S(2)}) %collective-permute-start.123) | collective-permute-done | bytes 720928 | tf_op jit(solution)/shard_map/ppermute | solution.py:65
  1239.9 12.7 %collective-permute-done.122.refs_5_ = f32[2,2,176,256]{3,2,1,0:T(8,128)S(1)} collective-permute-done((f32[2,2,176,256]{3,2,1,0:T(8,128)}, f32[2,2,176,256]{3,2,1,0:T(8,128)S(1)}, u32[]{:S(2)}, u32[]{:S(2)}) %collective-permute-start.122) | collective-permute-done | bytes 720928 | tf_op jit(solution)/shard_map/ppermute | solution.py:65
  1252.6 5.2 shard_map.216
  (596 shorter events, 408.3 us)
Async XLA Ops:
  6.1 95.2 %collective-permute-start.1 = (bf16[192,1280]{1,0:T(8,128)(2,1)}, bf16[192,1280]{1,0:T(8,128)(2,1)S(1)}, u32[]{:S(2)}, u32[]{:S(2)}) collective-permute-start(bf16[192,1280]{1,0:T(8,128)(2,1)} %pad_maximum_fusion.19), channel_id=1, source_target_pairs={{0,8},{4,12},{8,0},{12,4},{16,24},{20,28},{24,16},{28,20},{1,9},{5... | collective-permute-start | bytes 1474568 | tf_op jit(solution)/shard_map/ppermute | solution.py:65
  9.1 88.1 %collective-permute-start.5 = (bf16[192,1280]{1,0:T(8,128)(2,1)}, bf16[192,1280]{1,0:T(8,128)(2,1)}, u32[]{:S(2)}, u32[]{:S(2)}) collective-permute-start(bf16[192,1280]{1,0:T(8,128)(2,1)} %pad_maximum_fusion.19), channel_id=1, source_target_pairs={{0,24},{4,28},{8,16},{12,20},{16,8},{20,12},{24,0},{28,4},{1,25},{... | collective-permute-start | bytes 1474568 | tf_op jit(solution)/shard_map/ppermute | solution.py:65
  11.6 87.1 %collective-permute-start.3 = (bf16[192,1280]{1,0:T(8,128)(2,1)}, bf16[192,1280]{1,0:T(8,128)(2,1)}, u32[]{:S(2)}, u32[]{:S(2)}) collective-permute-start(bf16[192,1280]{1,0:T(8,128)(2,1)} %pad_maximum_fusion.19), channel_id=1, source_target_pairs={{0,16},{4,20},{8,24},{12,28},{16,0},{20,4},{24,8},{28,12},{1,17},{... | collective-permute-start | bytes 1474568 | tf_op jit(solution)/shard_map/ppermute | solution.py:65
  12.5 40.2 %collective-permute-start.16 = (bf16[176,1024]{1,0:T(8,128)(2,1)}, bf16[176,1024]{1,0:T(8,128)(2,1)S(1)}, u32[]{:S(2)}, u32[]{:S(2)}) collective-permute-start(bf16[176,1024]{1,0:T(8,128)(2,1)} %pad_maximum_fusion.23), channel_id=1, source_target_pairs={{0,24},{4,28},{8,16},{12,20},{16,8},{20,12},{24,0},{28,4},{1,25},{... | collective-permute-start | bytes 1081352 | tf_op jit(solution)/shard_map/ppermute | solution.py:65
  15.4 70.0 %collective-permute-start.14 = (bf16[176,1024]{1,0:T(8,128)(2,1)}, bf16[176,1024]{1,0:T(8,128)(2,1)S(1)}, u32[]{:S(2)}, u32[]{:S(2)}) collective-permute-start(bf16[176,1024]{1,0:T(8,128)(2,1)} %pad_maximum_fusion.23), channel_id=1, source_target_pairs={{0,16},{4,20},{8,24},{12,28},{16,0},{20,4},{24,8},{28,12},{1,17},{... | collective-permute-start | bytes 1081352 | tf_op jit(solution)/shard_map/ppermute | solution.py:65
  52.8 40.1 %collective-permute-start.12 = (bf16[176,1024]{1,0:T(8,128)(2,1)}, bf16[176,1024]{1,0:T(8,128)(2,1)S(1)}, u32[]{:S(2)}, u32[]{:S(2)}) collective-permute-start(bf16[176,1024]{1,0:T(8,128)(2,1)} %pad_maximum_fusion.23), channel_id=1, source_target_pairs={{0,8},{4,12},{8,0},{12,4},{16,24},{20,28},{24,16},{28,20},{1,9},{5... | collective-permute-start | bytes 1081352 | tf_op jit(solution)/shard_map/ppermute | solution.py:65
  94.9 152.6 %collective-permute-start.37 = (bf16[128,2048]{1,0:T(8,128)(2,1)}, bf16[128,2048]{1,0:T(8,128)(2,1)}, u32[]{:S(2)}, u32[]{:S(2)}) collective-permute-start(bf16[128,2048]{1,0:T(8,128)(2,1)} %get-tuple-element.314), channel_id=1, source_target_pairs={{0,4},{4,0},{8,12},{12,8},{16,20},{20,16},{24,28},{28,24},{1,5},{5... | collective-permute-start | bytes 1572872 | tf_op jit(solution)/shard_map/ppermute | solution.py:65
  97.2 77.1 %collective-permute-start.13 = (bf16[176,1024]{1,0:T(8,128)(2,1)S(1)}, bf16[176,1024]{1,0:T(8,128)(2,1)S(1)}, u32[]{:S(2)}, u32[]{:S(2)}) collective-permute-start(bf16[176,1024]{1,0:T(8,128)(2,1)S(1)} %collective-permute-done.12.refs_2_), channel_id=1, source_target_pairs={{0,4},{4,0},{8,12},{12,8},{16,20},{20,16},{24,28},{28,24},{1,5},{5... | collective-permute-start | bytes 1081352 | tf_op jit(solution)/shard_map/ppermute | solution.py:65
  101.2 40.3 %collective-permute-start.15 = (bf16[176,1024]{1,0:T(8,128)(2,1)S(1)}, bf16[176,1024]{1,0:T(8,128)(2,1)S(1)}, u32[]{:S(2)}, u32[]{:S(2)}) collective-permute-start(bf16[176,1024]{1,0:T(8,128)(2,1)S(1)} %collective-permute-done.14.refs_4_), channel_id=1, source_target_pairs={{0,4},{4,0},{8,12},{12,8},{16,20},{20,16},{24,28},{28,24},{1,5},{5... | collective-permute-start | bytes 1081352 | tf_op jit(solution)/shard_map/ppermute | solution.py:65
  107.2 44.9 %collective-permute-start.2 = (bf16[192,1280]{1,0:T(8,128)(2,1)S(1)}, bf16[192,1280]{1,0:T(8,128)(2,1)S(1)}, u32[]{:S(2)}, u32[]{:S(2)}) collective-permute-start(bf16[192,1280]{1,0:T(8,128)(2,1)S(1)} %collective-permute-done.1.refs_2_), channel_id=1, source_target_pairs={{0,4},{4,0},{8,12},{12,8},{16,20},{20,16},{24,28},{28,24},{1,5},{5... | collective-permute-start | bytes 1474568 | tf_op jit(solution)/shard_map/ppermute | solution.py:65
  133.8 42.0 %collective-permute-start.7 = (bf16[2,80,1280]{2,1,0:T(8,128)(2,1)S(1)}, bf16[2,80,1280]{2,1,0:T(8,128)(2,1)S(1)}, u32[]{:S(2)}, u32[]{:S(2)}) collective-permute-start(bf16[2,80,1280]{2,1,0:T(8,128)(2,1)S(1)} %pad_maximum_fusion.21), channel_id=1, source_target_pairs={{0,2},{2,0},{1,3},{3,1},{4,6},{6,4},{5,7},{7,5},{8,10},{10,8},{9,1... | collective-permute-start | bytes 1228808 | tf_op jit(solution)/shard_map/ppermute | solution.py:65
  174.4 49.8 %collective-permute-start.18 = (bf16[2,80,1024]{2,1,0:T(8,128)(2,1)}, bf16[2,80,1024]{2,1,0:T(8,128)(2,1)}, u32[]{:S(2)}, u32[]{:S(2)}) collective-permute-start(bf16[2,80,1024]{2,1,0:T(8,128)(2,1)} %pad_maximum_fusion.36), channel_id=1, source_target_pairs={{0,2},{2,0},{1,3},{3,1},{4,6},{6,4},{5,7},{7,5},{8,10},{10,8},{9,1... | collective-permute-start | bytes 983048 | tf_op jit(solution)/shard_map/ppermute | solution.py:65
  175.8 52.8 %collective-permute-start.19 = (bf16[3,80,1024]{2,1,0:T(8,128)(2,1)}, bf16[3,80,1024]{2,1,0:T(8,128)(2,1)}, u32[]{:S(2)}, u32[]{:S(2)}) collective-permute-start(bf16[3,80,1024]{2,1,0:T(8,128)(2,1)} %pad_maximum_fusion.20), channel_id=1, source_target_pairs={{0,2},{2,0},{1,3},{3,1},{4,6},{6,4},{5,7},{7,5},{8,10},{10,8},{9,1... | collective-permute-start | bytes 1474568 | tf_op jit(solution)/shard_map/ppermute | solution.py:65
  187.3 39.2 %collective-permute-start.20 = (bf16[2,80,1024]{2,1,0:T(8,128)(2,1)}, bf16[2,80,1024]{2,1,0:T(8,128)(2,1)}, u32[]{:S(2)}, u32[]{:S(2)}) collective-permute-start(bf16[2,80,1024]{2,1,0:T(8,128)(2,1)} %pad_maximum_fusion.37), channel_id=1, source_target_pairs={{0,2},{2,0},{1,3},{3,1},{4,6},{6,4},{5,7},{7,5},{8,10},{10,8},{9,1... | collective-permute-start | bytes 983048 | tf_op jit(solution)/shard_map/ppermute | solution.py:65
  224.2 36.6 %collective-permute-start.40 = (bf16[128,2048]{1,0:T(8,128)(2,1)}, bf16[128,2048]{1,0:T(8,128)(2,1)}, u32[]{:S(2)}, u32[]{:S(2)}) collective-permute-start(bf16[128,2048]{1,0:T(8,128)(2,1)} %get-tuple-element.314), channel_id=1, source_target_pairs={{0,16},{4,20},{8,24},{12,28},{16,0},{20,4},{24,8},{28,12},{1,17},{... | collective-permute-start | bytes 1572872 | tf_op jit(solution)/shard_map/ppermute | solution.py:65
  226.6 35.7 %collective-permute-start.42 = (bf16[128,2048]{1,0:T(8,128)(2,1)}, bf16[128,2048]{1,0:T(8,128)(2,1)}, u32[]{:S(2)}, u32[]{:S(2)}) collective-permute-start(bf16[128,2048]{1,0:T(8,128)(2,1)} %get-tuple-element.314), channel_id=1, source_target_pairs={{0,24},{4,28},{8,16},{12,20},{16,8},{20,12},{24,0},{28,4},{1,25},{... | collective-permute-start | bytes 1572872 | tf_op jit(solution)/shard_map/ppermute | solution.py:65
  247.6 105.0 %collective-permute-start.29 = (bf16[4,3,176,256]{3,2,1,0:T(8,128)(2,1)}, bf16[4,3,176,256]{3,2,1,0:T(8,128)(2,1)}, u32[]{:S(2)}, u32[]{:S(2)}) collective-permute-start(bf16[4,3,176,256]{3,2,1,0:T(8,128)(2,1)} %pad_maximum_fusion.5), channel_id=1, source_target_pairs={{0,4},{4,0},{8,12},{12,8},{16,20},{20,16},{24,28},{28,24},{1,5},{5... | collective-permute-start | bytes 3244040 | tf_op jit(solution)/shard_map/ppermute | solution.py:65
  262.3 43.3 %collective-permute-start.43 = (bf16[128,2048]{1,0:T(8,128)(2,1)}, bf16[128,2048]{1,0:T(8,128)(2,1)S(1)}, u32[]{:S(2)}, u32[]{:S(2)}) collective-permute-start(bf16[128,2048]{1,0:T(8,128)(2,1)} %collective-permute-done.42), channel_id=1, source_target_pairs={{0,4},{4,0},{8,12},{12,8},{16,20},{20,16},{24,28},{28,24},{1,5},{5... | collective-permute-start | bytes 1572872 | tf_op jit(solution)/shard_map/ppermute | solution.py:65
  316.8 159.5 %collective-permute-start.45 = (bf16[1024,2048]{1,0:T(8,128)(2,1)}, bf16[1024,2048]{1,0:T(8,128)(2,1)}, u32[]{:S(2)}, u32[]{:S(2)}) collective-permute-start(bf16[1024,2048]{1,0:T(8,128)(2,1)} %constant_dynamic-update-slice_fusion.13), channel_id=1, source_target_pairs={{0,1},{1,0},{2,3},{3,2},{4,5},{5,4},{6,7},{7,6},{8,9},{9,8},{10,11... | collective-permute-start | bytes 12582920 | tf_op jit(solution)/shard_map/ppermute | solution.py:65
  351.5 129.7 %collective-permute-start.44 = (bf16[1024,2048]{1,0:T(8,128)(2,1)}, bf16[1024,2048]{1,0:T(8,128)(2,1)}, u32[]{:S(2)}, u32[]{:S(2)}) collective-permute-start(bf16[1024,2048]{1,0:T(8,128)(2,1)} %constant_dynamic-update-slice_fusion.5.normed_ref), channel_id=1, source_target_pairs={{0,1},{1,0},{2,3},{3,2},{4,5},{5,4},{6,7},{7,6},{8,9},{9,8},{10,11... | collective-permute-start | bytes 12582920 | tf_op jit(solution)/shard_map/ppermute | solution.py:65
  358.1 47.2 %collective-permute-start.31 = (bf16[2,3,176,256]{3,2,1,0:T(8,128)(2,1)}, bf16[2,3,176,256]{3,2,1,0:T(8,128)(2,1)}, u32[]{:S(2)}, u32[]{:S(2)}) collective-permute-start(bf16[2,3,176,256]{3,2,1,0:T(8,128)(2,1)} %pad_maximum_fusion.17), channel_id=1, source_target_pairs={{0,16},{4,20},{8,24},{12,28},{16,0},{20,4},{24,8},{28,12},{1,17},{... | collective-permute-start | bytes 1622024 | tf_op jit(solution)/shard_map/ppermute | solution.py:65
  372.7 46.9 %collective-permute-start.30 = (bf16[2,3,176,256]{3,2,1,0:T(8,128)(2,1)}, bf16[2,3,176,256]{3,2,1,0:T(8,128)(2,1)}, u32[]{:S(2)}, u32[]{:S(2)}) collective-permute-start(bf16[2,3,176,256]{3,2,1,0:T(8,128)(2,1)} %pad_maximum_fusion.16), channel_id=1, source_target_pairs={{0,8},{4,12},{8,0},{12,4},{16,24},{20,28},{24,16},{28,20},{1,9},{5... | collective-permute-start | bytes 1622024 | tf_op jit(solution)/shard_map/ppermute | solution.py:65
  514.9 64.2 %collective-permute-start.116 = (f32[176,2048]{1,0:T(8,128)}, f32[176,2048]{1,0:T(8,128)}, u32[]{:S(2)}, u32[]{:S(2)}) collective-permute-start(f32[176,2048]{1,0:T(8,128)} %get-tuple-element.297), channel_id=1, source_target_pairs={{0,2},{2,0},{1,3},{3,1},{4,6},{6,4},{5,7},{7,5},{8,10},{10,8},{9,1... | collective-permute-start | bytes 4325384 | tf_op jit(solution)/shard_map/ppermute | solution.py:65
  519.3 97.0 %collective-permute-start.46 = (f32[1024,512]{1,0:T(8,128)}, f32[1024,512]{1,0:T(8,128)}, u32[]{:S(2)}, u32[]{:S(2)}) collective-permute-start(f32[1024,512]{1,0:T(8,128)} %fusion.27), channel_id=1, source_target_pairs={{0,1},{1,0},{2,3},{3,2},{4,5},{5,4},{6,7},{7,6},{8,9},{9,8},{10,11... | collective-permute-start | bytes 6291464 | tf_op jit(solution)/shard_map/ppermute | solution.py:65
  522.8 98.0 %collective-permute-start.51 = (f32[1024,512]{1,0:T(8,128)}, f32[1024,512]{1,0:T(8,128)}, u32[]{:S(2)}, u32[]{:S(2)}) collective-permute-start(f32[1024,512]{1,0:T(8,128)} %fusion.24), channel_id=1, source_target_pairs={{0,1},{1,0},{2,3},{3,2},{4,5},{5,4},{6,7},{7,6},{8,9},{9,8},{10,11... | collective-permute-start | bytes 6291464 | tf_op jit(solution)/shard_map/ppermute | solution.py:65
  523.3 84.4 %collective-permute-start.89 = (f32[176,2048]{1,0:T(8,128)}, f32[176,2048]{1,0:T(8,128)}, u32[]{:S(2)}, u32[]{:S(2)}) collective-permute-start(f32[176,2048]{1,0:T(8,128)} %get-tuple-element.266), channel_id=1, source_target_pairs={{0,2},{2,0},{1,3},{3,1},{4,6},{6,4},{5,7},{7,5},{8,10},{10,8},{9,1... | collective-permute-start | bytes 4325384 | tf_op jit(solution)/shard_map/ppermute | solution.py:65
  548.2 75.6 %collective-permute-start.56 = (f32[1024,512]{1,0:T(8,128)}, f32[1024,512]{1,0:T(8,128)}, u32[]{:S(2)}, u32[]{:S(2)}) collective-permute-start(f32[1024,512]{1,0:T(8,128)} %fusion.21), channel_id=1, source_target_pairs={{0,1},{1,0},{2,3},{3,2},{4,5},{5,4},{6,7},{7,6},{8,9},{9,8},{10,11... | collective-permute-start | bytes 6291464 | tf_op jit(solution)/shard_map/ppermute | solution.py:65
  579.1 49.1 %collective-permute-start.61 = (f32[1024,512]{1,0:T(8,128)}, f32[1024,512]{1,0:T(8,128)}, u32[]{:S(2)}, u32[]{:S(2)}) collective-permute-start(f32[1024,512]{1,0:T(8,128)} %fusion.18), channel_id=1, source_target_pairs={{0,1},{1,0},{2,3},{3,2},{4,5},{5,4},{6,7},{7,6},{8,9},{9,8},{10,11... | collective-permute-start | bytes 6291464 | tf_op jit(solution)/shard_map/ppermute | solution.py:65
  607.6 186.7 %collective-permute-start.98 = (bf16[1024,2048]{1,0:T(8,128)(2,1)}, bf16[1024,2048]{1,0:T(8,128)(2,1)}, u32[]{:S(2)}, u32[]{:S(2)}) collective-permute-start(bf16[1024,2048]{1,0:T(8,128)(2,1)} %convolution_convert_fusion), channel_id=1, source_target_pairs={{0,1},{1,0},{2,3},{3,2},{4,5},{5,4},{6,7},{7,6},{8,9},{9,8},{10,11... | collective-permute-start | bytes 12582920 | tf_op jit(solution)/shard_map/ppermute | solution.py:65
  620.7 37.1 %collective-permute-start.47 = (f32[4,128,512]{2,1,0:T(8,128)S(1)}, f32[4,128,512]{2,1,0:T(8,128)S(1)}, u32[]{:S(2)}, u32[]{:S(2)}) collective-permute-start(f32[4,128,512]{2,1,0:T(8,128)S(1)} %slice_bitcast_fusion.7), channel_id=1, source_target_pairs={{0,4},{4,0},{8,12},{12,8},{16,20},{20,16},{24,28},{28,24},{1,5},{5... | collective-permute-start | bytes 3145736 | tf_op jit(solution)/shard_map/ppermute | solution.py:65
  623.8 56.5 %collective-permute-start.52 = (f32[4,128,512]{2,1,0:T(8,128)S(1)}, f32[4,128,512]{2,1,0:T(8,128)S(1)}, u32[]{:S(2)}, u32[]{:S(2)}) collective-permute-start(f32[4,128,512]{2,1,0:T(8,128)S(1)} %slice_bitcast_fusion.5), channel_id=1, source_target_pairs={{0,4},{4,0},{8,12},{12,8},{16,20},{20,16},{24,28},{28,24},{1,5},{5... | collective-permute-start | bytes 3145736 | tf_op jit(solution)/shard_map/ppermute | solution.py:65
  628.2 74.5 %collective-permute-start.57 = (f32[4,128,512]{2,1,0:T(8,128)S(1)}, f32[4,128,512]{2,1,0:T(8,128)S(1)}, u32[]{:S(2)}, u32[]{:S(2)}) collective-permute-start(f32[4,128,512]{2,1,0:T(8,128)S(1)} %slice_bitcast_fusion.3), channel_id=1, source_target_pairs={{0,4},{4,0},{8,12},{12,8},{16,20},{20,16},{24,28},{28,24},{1,5},{5... | collective-permute-start | bytes 3145736 | tf_op jit(solution)/shard_map/ppermute | solution.py:65
  635.4 89.4 %collective-permute-start.62 = (f32[4,128,512]{2,1,0:T(8,128)S(1)}, f32[4,128,512]{2,1,0:T(8,128)S(1)}, u32[]{:S(2)}, u32[]{:S(2)}) collective-permute-start(f32[4,128,512]{2,1,0:T(8,128)S(1)} %slice_bitcast_fusion.1), channel_id=1, source_target_pairs={{0,4},{4,0},{8,12},{12,8},{16,20},{20,16},{24,28},{28,24},{1,5},{5... | collective-permute-start | bytes 3145736 | tf_op jit(solution)/shard_map/ppermute | solution.py:65
  658.1 67.5 %collective-permute-start.48 = (f32[128,512]{1,0:T(8,128)S(1)}, f32[128,512]{1,0:T(8,128)S(1)}, u32[]{:S(2)}, u32[]{:S(2)}) collective-permute-start(f32[128,512]{1,0:T(8,128)S(1)} %get-tuple-element.385), channel_id=1, source_target_pairs={{0,8},{4,12},{8,0},{12,4},{16,24},{20,28},{24,16},{28,20},{1,9},{5... | collective-permute-start | bytes 786440 | tf_op jit(solution)/shard_map/ppermute | solution.py:65
  680.3 47.4 %collective-permute-start.49 = (f32[128,512]{1,0:T(8,128)S(1)}, f32[128,512]{1,0:T(8,128)S(1)}, u32[]{:S(2)}, u32[]{:S(2)}) collective-permute-start(f32[128,512]{1,0:T(8,128)S(1)} %get-tuple-element.387), channel_id=1, source_target_pairs={{0,16},{4,20},{8,24},{12,28},{16,0},{20,4},{24,8},{28,12},{1,17},{... | collective-permute-start | bytes 786440 | tf_op jit(solution)/shard_map/ppermute | solution.py:65
  739.1 38.8 %collective-permute-start.59 = (f32[128,512]{1,0:T(8,128)S(1)}, f32[128,512]{1,0:T(8,128)S(1)}, u32[]{:S(2)}, u32[]{:S(2)}) collective-permute-start(f32[128,512]{1,0:T(8,128)S(1)} %get-tuple-element.393), channel_id=1, source_target_pairs={{0,16},{4,20},{8,24},{12,28},{16,0},{20,4},{24,8},{28,12},{1,17},{... | collective-permute-start | bytes 786440 | tf_op jit(solution)/shard_map/ppermute | solution.py:65
  780.1 48.4 %collective-permute-start.81 = (bf16[256,1024]{1,0:T(8,128)(2,1)S(1)}, bf16[256,1024]{1,0:T(8,128)(2,1)}, u32[]{:S(2)}, u32[]{:S(2)}) collective-permute-start(bf16[256,1024]{1,0:T(8,128)(2,1)S(1)} %get-tuple-element.258.left_ref.refs_0_), channel_id=1, source_target_pairs={{0,4},{4,0},{8,12},{12,8},{16,20},{20,16},{24,28},{28,24},{1,5},{5... | collective-permute-start | bytes 1572872 | tf_op jit(solution)/shard_map/ppermute | solution.py:65
  792.0 39.4 %collective-permute-start.77 = (bf16[256,1024]{1,0:T(8,128)(2,1)S(1)}, bf16[256,1024]{1,0:T(8,128)(2,1)}, u32[]{:S(2)}, u32[]{:S(2)}) collective-permute-start(bf16[256,1024]{1,0:T(8,128)(2,1)S(1)} %get-tuple-element.258.left_ref.refs_0_), channel_id=1, source_target_pairs={{0,16},{4,20},{8,24},{12,28},{16,0},{20,4},{24,8},{28,12},{1,17},{... | collective-permute-start | bytes 1572872 | tf_op jit(solution)/shard_map/ppermute | solution.py:65
  792.0 42.9 %collective-permute-start.75 = (bf16[256,1024]{1,0:T(8,128)(2,1)S(1)}, bf16[256,1024]{1,0:T(8,128)(2,1)}, u32[]{:S(2)}, u32[]{:S(2)}) collective-permute-start(bf16[256,1024]{1,0:T(8,128)(2,1)S(1)} %get-tuple-element.258.left_ref.refs_0_), channel_id=1, source_target_pairs={{0,24},{4,28},{8,16},{12,20},{16,8},{20,12},{24,0},{28,4},{1,25},{... | collective-permute-start | bytes 1572872 | tf_op jit(solution)/shard_map/ppermute | solution.py:65
  803.9 68.2 %collective-permute-start.108 = (bf16[8,128,256]{2,1,0:T(8,128)(2,1)}, bf16[8,128,256]{2,1,0:T(8,128)(2,1)}, u32[]{:S(2)}, u32[]{:S(2)}) collective-permute-start(bf16[8,128,256]{2,1,0:T(8,128)(2,1)} %constant_dynamic-update-slice_fusion.26.mine_ref), channel_id=1, source_target_pairs={{0,1},{1,0},{2,3},{3,2},{4,5},{5,4},{6,7},{7,6},{8,9},{9,8},{10,11... | collective-permute-start | bytes 1572872 | tf_op jit(solution)/shard_map/ppermute | solution.py:65
  804.4 69.2 %collective-permute-start.80 = (bf16[256,1024]{1,0:T(8,128)(2,1)}, bf16[256,1024]{1,0:T(8,128)(2,1)}, u32[]{:S(2)}, u32[]{:S(2)}) collective-permute-start(bf16[256,1024]{1,0:T(8,128)(2,1)} %collective-permute-done.79.refs_2_), channel_id=1, source_target_pairs={{0,4},{4,0},{8,12},{12,8},{16,20},{20,16},{24,28},{28,24},{1,5},{5... | collective-permute-start | bytes 1572872 | tf_op jit(solution)/shard_map/ppermute | solution.py:65
  828.5 134.7 %collective-permute-start.117 = (f32[4,2,176,256]{3,2,1,0:T(8,128)}, f32[4,2,176,256]{3,2,1,0:T(8,128)}, u32[]{:S(2)}, u32[]{:S(2)}) collective-permute-start(f32[4,2,176,256]{3,2,1,0:T(8,128)} %pad_maximum_fusion.3), channel_id=1, source_target_pairs={{0,4},{4,0},{8,12},{12,8},{16,20},{20,16},{24,28},{28,24},{1,5},{5... | collective-permute-start | bytes 4325384 | tf_op jit(solution)/shard_map/ppermute | solution.py:65
  831.5 37.5 %collective-permute-start.83 = (bf16[4,128,256]{2,1,0:T(8,128)(2,1)}, bf16[4,128,256]{2,1,0:T(8,128)(2,1)}, u32[]{:S(2)}, u32[]{:S(2)}) collective-permute-start(bf16[4,128,256]{2,1,0:T(8,128)(2,1)} %pad_maximum_fusion.39), channel_id=1, source_target_pairs={{0,4},{4,0},{8,12},{12,8},{16,20},{20,16},{24,28},{28,24},{1,5},{5... | collective-permute-start | bytes 786440 | tf_op jit(solution)/shard_map/ppermute | solution.py:65
  834.9 45.2 %collective-permute-start.78 = (bf16[256,1024]{1,0:T(8,128)(2,1)}, bf16[256,1024]{1,0:T(8,128)(2,1)S(1)}, u32[]{:S(2)}, u32[]{:S(2)}) collective-permute-start(bf16[256,1024]{1,0:T(8,128)(2,1)} %collective-permute-done.77.refs_4_), channel_id=1, source_target_pairs={{0,4},{4,0},{8,12},{12,8},{16,20},{20,16},{24,28},{28,24},{1,5},{5... | collective-permute-start | bytes 1572872 | tf_op jit(solution)/shard_map/ppermute | solution.py:65
  868.9 138.1 %collective-permute-start.99 = (bf16[4,128,2048]{2,1,0:T(8,128)(2,1)}, bf16[4,128,2048]{2,1,0:T(8,128)(2,1)}, u32[]{:S(2)}, u32[]{:S(2)}) collective-permute-start(bf16[4,128,2048]{2,1,0:T(8,128)(2,1)} %fusion.8), channel_id=1, source_target_pairs={{0,4},{4,0},{8,12},{12,8},{16,20},{20,16},{24,28},{28,24},{1,5},{5... | collective-permute-start | bytes 6291464 | tf_op jit(solution)/shard_map/ppermute | solution.py:65
  872.1 36.6 %collective-permute-start.67 = (f32[256,256]{1,0:T(8,128)}, f32[256,256]{1,0:T(8,128)S(1)}, u32[]{:S(2)}, u32[]{:S(2)}) collective-permute-start(f32[256,256]{1,0:T(8,128)} %get-tuple-element.429), channel_id=1, source_target_pairs={{0,2},{2,0},{1,3},{3,1},{4,6},{6,4},{5,7},{7,5},{8,10},{10,8},{9,1... | collective-permute-start | bytes 786440 | tf_op jit(solution)/shard_map/ppermute | solution.py:65
  873.6 36.0 %collective-permute-start.86 = (bf16[2,128,256]{2,1,0:T(8,128)(2,1)S(1)}, bf16[2,128,256]{2,1,0:T(8,128)(2,1)S(1)}, u32[]{:S(2)}, u32[]{:S(2)}) collective-permute-start(bf16[2,128,256]{2,1,0:T(8,128)(2,1)S(1)} %pad_maximum_fusion.44), channel_id=1, source_target_pairs={{0,24},{4,28},{8,16},{12,20},{16,8},{20,12},{24,0},{28,4},{1,25},{... | collective-permute-start | bytes 393224 | tf_op jit(solution)/shard_map/ppermute | solution.py:65
  880.1 37.1 %collective-permute-start.85 = (bf16[2,128,256]{2,1,0:T(8,128)(2,1)}, bf16[2,128,256]{2,1,0:T(8,128)(2,1)}, u32[]{:S(2)}, u32[]{:S(2)}) collective-permute-start(bf16[2,128,256]{2,1,0:T(8,128)(2,1)} %pad_maximum_fusion.43), channel_id=1, source_target_pairs={{0,16},{4,20},{8,24},{12,28},{16,0},{20,4},{24,8},{28,12},{1,17},{... | collective-permute-start | bytes 393224 | tf_op jit(solution)/shard_map/ppermute | solution.py:65
  917.2 138.5 %collective-permute-start.82 = (f32[256,2048]{1,0:T(8,128)S(1)}, f32[256,2048]{1,0:T(8,128)}, u32[]{:S(2)}, u32[]{:S(2)}) collective-permute-start(f32[256,2048]{1,0:T(8,128)S(1)} %shard_map.212), channel_id=1, source_target_pairs={{0,1},{1,0},{2,3},{3,2},{4,5},{5,4},{6,7},{7,6},{8,9},{9,8},{10,11... | collective-permute-start | bytes 6291464 | tf_op jit(solution)/shard_map/ppermute | solution.py:65
  935.2 47.0 %collective-permute-start.87 = (bf16[8,128,256]{2,1,0:T(8,128)(2,1)S(1)}, bf16[8,128,256]{2,1,0:T(8,128)(2,1)S(1)}, u32[]{:S(2)}, u32[]{:S(2)}) collective-permute-start(bf16[8,128,256]{2,1,0:T(8,128)(2,1)S(1)} %constant_dynamic-update-slice_fusion.21.mine_ref), channel_id=1, source_target_pairs={{0,1},{1,0},{2,3},{3,2},{4,5},{5,4},{6,7},{7,6},{8,9},{9,8},{10,11... | collective-permute-start | bytes 1572872 | tf_op jit(solution)/shard_map/ppermute | solution.py:65
  935.2 44.9 %collective-permute-start.92 = (f32[2,1,176,256]{3,2,1,0:T(8,128)S(1)}, f32[2,1,176,256]{3,2,1,0:T(8,128)}, u32[]{:S(2)}, u32[]{:S(2)}) collective-permute-start(f32[2,1,176,256]{3,2,1,0:T(8,128)S(1)} %pad_maximum_fusion.26), channel_id=1, source_target_pairs={{0,16},{4,20},{8,24},{12,28},{16,0},{20,4},{24,8},{28,12},{1,17},{... | collective-permute-start | bytes 1081352 | tf_op jit(solution)/shard_map/ppermute | solution.py:65
  1007.0 46.6 %collective-permute-start.70 = (bf16[256,1280]{1,0:T(8,128)(2,1)S(1)}, bf16[256,1280]{1,0:T(8,128)(2,1)S(1)}, u32[]{:S(2)}, u32[]{:S(2)}) collective-permute-start(bf16[256,1280]{1,0:T(8,128)(2,1)S(1)} %copy-done.7), channel_id=1, source_target_pairs={{0,16},{4,20},{8,24},{12,28},{16,0},{20,4},{24,8},{28,12},{1,17},{... | collective-permute-start | bytes 1966088 | tf_op jit(solution)/shard_map/ppermute | solution.py:65
  1007.0 48.2 %collective-permute-start.68 = (bf16[256,1280]{1,0:T(8,128)(2,1)S(1)}, bf16[256,1280]{1,0:T(8,128)(2,1)S(1)}, u32[]{:S(2)}, u32[]{:S(2)}) collective-permute-start(bf16[256,1280]{1,0:T(8,128)(2,1)S(1)} %copy-done.7), channel_id=1, source_target_pairs={{0,24},{4,28},{8,16},{12,20},{16,8},{20,12},{24,0},{28,4},{1,25},{... | collective-permute-start | bytes 1966088 | tf_op jit(solution)/shard_map/ppermute | solution.py:65
  1014.9 47.2 %collective-permute-start.74 = (bf16[256,1280]{1,0:T(8,128)(2,1)S(1)}, bf16[256,1280]{1,0:T(8,128)(2,1)S(1)}, u32[]{:S(2)}, u32[]{:S(2)}) collective-permute-start(bf16[256,1280]{1,0:T(8,128)(2,1)S(1)} %copy-done.7), channel_id=1, source_target_pairs={{0,4},{4,0},{8,12},{12,8},{16,20},{20,16},{24,28},{28,24},{1,5},{5... | collective-permute-start | bytes 1966088 | tf_op jit(solution)/shard_map/ppermute | solution.py:65
  1019.7 94.4 %collective-permute-start.88 = (f32[256,1024]{1,0:T(8,128)}, f32[256,1024]{1,0:T(8,128)}, u32[]{:S(2)}, u32[]{:S(2)}) collective-permute-start(f32[256,1024]{1,0:T(8,128)} %shard_map.213), channel_id=1, source_target_pairs={{0,2},{2,0},{1,3},{3,1},{4,6},{6,4},{5,7},{7,5},{8,10},{10,8},{9,1... | collective-permute-start | bytes 3145736 | tf_op jit(solution)/shard_map/ppermute | solution.py:65
  1055.6 37.2 %collective-permute-start.69 = (bf16[256,1280]{1,0:T(8,128)(2,1)S(1)}, bf16[256,1280]{1,0:T(8,128)(2,1)S(1)}, u32[]{:S(2)}, u32[]{:S(2)}) collective-permute-start(bf16[256,1280]{1,0:T(8,128)(2,1)S(1)} %collective-permute-done.68.refs_6_), channel_id=1, source_target_pairs={{0,4},{4,0},{8,12},{12,8},{16,20},{20,16},{24,28},{28,24},{1,5},{5... | collective-permute-start | bytes 1966088 | tf_op jit(solution)/shard_map/ppermute | solution.py:65
  1063.0 56.0 %collective-permute-start.100 = (bf16[128,2048]{1,0:T(8,128)(2,1)}, bf16[128,2048]{1,0:T(8,128)(2,1)}, u32[]{:S(2)}, u32[]{:S(2)}) collective-permute-start(bf16[128,2048]{1,0:T(8,128)(2,1)} %get-tuple-element.337), channel_id=1, source_target_pairs={{0,8},{4,12},{8,0},{12,4},{16,24},{20,28},{24,16},{28,20},{1,9},{5... | collective-permute-start | bytes 1572872 | tf_op jit(solution)/shard_map/ppermute | solution.py:65
  1073.9 45.0 %collective-permute-start.101 = (bf16[128,2048]{1,0:T(8,128)(2,1)}, bf16[128,2048]{1,0:T(8,128)(2,1)}, u32[]{:S(2)}, u32[]{:S(2)}) collective-permute-start(bf16[128,2048]{1,0:T(8,128)(2,1)} %get-tuple-element.339), channel_id=1, source_target_pairs={{0,16},{4,20},{8,24},{12,28},{16,0},{20,4},{24,8},{28,12},{1,17},{... | collective-permute-start | bytes 1572872 | tf_op jit(solution)/shard_map/ppermute | solution.py:65
  1114.1 93.2 %collective-permute-start.109 = (f32[256,1280]{1,0:T(8,128)}, f32[256,1280]{1,0:T(8,128)}, u32[]{:S(2)}, u32[]{:S(2)}) collective-permute-start(f32[256,1280]{1,0:T(8,128)} %shard_map.215), channel_id=1, source_target_pairs={{0,2},{2,0},{1,3},{3,1},{4,6},{6,4},{5,7},{7,5},{8,10},{10,8},{9,1... | collective-permute-start | bytes 3932168 | tf_op jit(solution)/shard_map/ppermute | solution.py:65
  1121.9 88.8 %collective-permute-start.103 = (f32[128,2048]{1,0:T(8,128)}, f32[128,2048]{1,0:T(8,128)}, u32[]{:S(2)}, u32[]{:S(2)}) collective-permute-start(f32[128,2048]{1,0:T(8,128)} %fusion.12), channel_id=1, source_target_pairs={{0,1},{1,0},{2,3},{3,2},{4,5},{5,4},{6,7},{7,6},{8,9},{9,8},{10,11... | collective-permute-start | bytes 3145736 | tf_op jit(solution)/shard_map/ppermute | solution.py:65
  1168.1 37.2 %collective-permute-start.119 = (f32[2,2,176,256]{3,2,1,0:T(8,128)}, f32[2,2,176,256]{3,2,1,0:T(8,128)}, u32[]{:S(2)}, u32[]{:S(2)}) collective-permute-start(f32[2,2,176,256]{3,2,1,0:T(8,128)} %pad_maximum_fusion.12), channel_id=1, source_target_pairs={{0,16},{4,20},{8,24},{12,28},{16,0},{20,4},{24,8},{28,12},{1,17},{... | collective-permute-start | bytes 2162696 | tf_op jit(solution)/shard_map/ppermute | solution.py:65
  1168.1 38.7 %collective-permute-start.118 = (f32[2,2,176,256]{3,2,1,0:T(8,128)}, f32[2,2,176,256]{3,2,1,0:T(8,128)}, u32[]{:S(2)}, u32[]{:S(2)}) collective-permute-start(f32[2,2,176,256]{3,2,1,0:T(8,128)} %pad_maximum_fusion.11), channel_id=1, source_target_pairs={{0,8},{4,12},{8,0},{12,4},{16,24},{20,28},{24,16},{28,20},{1,9},{5... | collective-permute-start | bytes 2162696 | tf_op jit(solution)/shard_map/ppermute | solution.py:65
  1175.4 40.6 %collective-permute-start.121 = (f32[2,2,176,256]{3,2,1,0:T(8,128)}, f32[2,2,176,256]{3,2,1,0:T(8,128)S(1)}, u32[]{:S(2)}, u32[]{:S(2)}) collective-permute-start(f32[2,2,176,256]{3,2,1,0:T(8,128)} %pad_maximum_fusion.10.refs_0_), channel_id=1, source_target_pairs={{0,2},{2,0},{1,3},{3,1},{4,6},{6,4},{5,7},{7,5},{8,10},{10,8},{9,1... | collective-permute-start | bytes 2162696 | tf_op jit(solution)/shard_map/ppermute | solution.py:65
  1207.3 45.3 %collective-permute-start.122 = (f32[2,2,176,256]{3,2,1,0:T(8,128)}, f32[2,2,176,256]{3,2,1,0:T(8,128)S(1)}, u32[]{:S(2)}, u32[]{:S(2)}) collective-permute-start(f32[2,2,176,256]{3,2,1,0:T(8,128)} %collective-permute-done.118.refs_1_), channel_id=1, source_target_pairs={{0,2},{2,0},{1,3},{3,1},{4,6},{6,4},{5,7},{7,5},{8,10},{10,8},{9,1... | collective-permute-start | bytes 2162696 | tf_op jit(solution)/shard_map/ppermute | solution.py:65
  (166 other events, 3358.6 us)
